TPU v7x, 32 devices: a whole 2x2x4 slice. The times are simulated.
32 devices in a mesh: row: 8 (over z, y), col: 4 (over x, core).
Axes of the slice: x: 2, y: 2, z: 4, core: 2. Of those that a mesh axis runs over, the one named last changes fastest.
Arguments:
- tokens: bfloat16 [4096, 2560], P('row', 'col'), may hold values from -6 to 6
- document_ids: int32 [4096], replicated, may hold values from 0 to 3, never falling along the last dimension, each value on 1 to 2000 neighbouring positions
- gain_first: float32 [2560], P('row'), may hold values from 0.5 to 1.5
- query_down: float32 [2560, 768], P('row'), may hold values from -0.125 to 0.125
- query_gain: float32 [768], P('row'), may hold values from 0.5 to 1.5
- latent_down: float32 [2560, 288], P('row'), may hold values from -0.125 to 0.125
- latent_gain: float32 [256], P('row'), may hold values from 0.5 to 1.5
- query_up: float32 [768, 3840], P('row', 'col'), may hold values from -0.21875 to 0.21875
- latent_up: float32 [256, 5120], P('row', 'col'), may hold values from -0.375 to 0.375
- output_weight: float32 [2560, 2560], P('col', 'row'), may hold values from -3 to 3
- gain_second: float32 [2560], P('row'), may hold values from 0.5 to 1.5
- gate_weight: float32 [2560, 6400], P('row', 'col'), may hold values from -0.125 to 0.125
- up_weight: float32 [2560, 6400], P('row', 'col'), may hold values from -0.125 to 0.125
- down_weight: float32 [6400, 2560], P('col', 'row'), may hold values from -1 to 1
- cotangent: float32 [4096, 2560], P('row', 'col'), may hold values from -6 to 6
Outputs:
- result: float32 [4096, 2560], P('row', 'col')
- back_tokens: float32 [4096, 2560], P('row', 'col')
- slope_gain_first: float32 [2560], P('row')
- slope_query_down: float32 [2560, 768], P('row')
- slope_query_gain: float32 [768], P('row')
- slope_latent_down: float32 [2560, 288], P('row')
- slope_latent_gain: float32 [256], P('row')
- slope_query_up: float32 [768, 3840], P('row', 'col')
- slope_latent_up: float32 [256, 5120], P('row', 'col')
- slope_output: float32 [2560, 2560], P('col', 'row')
- slope_gain_second: float32 [2560], P('row')
- slope_gate: float32 [2560, 6400], P('row', 'col')
- slope_up: float32 [2560, 6400], P('row', 'col')
- slope_down: float32 [6400, 2560], P('col', 'row')
Inputs may be any that keep to these rules, and one draw needn't show every extreme that they name: `document_ids`: never falls along the tokens; each document has 1 to 2000 tokens and one has exactly 2000.
All inputs are finite; a program needn't handle non-finite values.
Results may differ from a plain program's by a relative error of at most 0.018.
The roundings to bfloat16 on the way count: a program that leaves them out, or rounds other values in their place, can miss the bound.
Values may be sent and summed in bfloat16 or wider, within the bound.
A program may use at most 384 MiB of HBM per device.

v0:
```python
import math

import jax
import jax.numpy as jnp
from jax import lax
from jax.sharding import PartitionSpec as P

DN = 64
DR = 32
DV = 64
KR = 256
SEQ_LEN = 4096
REACH = 4


EPS = 1e-05
RES = 1.4 / math.sqrt(62.0)
THETA = 10000.0
NEG = -1e30


def from_behind(value, axis, steps):
    count = lax.axis_size(axis)
    initial, last = (max(0, -steps), min(count, count - steps))
    return lax.ppermute(value, axis, [(source, source + steps) for source in range(initial, last)])


def normalize(value, gain):
    inverse = lax.rsqrt(jnp.mean(value * value, axis=-1, keepdims=True) + EPS)
    return (value * inverse * gain, inverse)


def norm_back(value, inverse, gain, upstream):
    unit = value * inverse
    scaled = upstream * gain
    inward = inverse * (scaled - unit * jnp.mean(scaled * unit, axis=-1, keepdims=True))
    return (inward, jnp.sum(upstream * unit, axis=0))


def angles(start, count):
    place = ((start + jnp.arange(count, dtype=jnp.int32)) % SEQ_LEN).astype(jnp.float32)
    half = DR // 2
    freq = jnp.exp(jnp.arange(half, dtype=jnp.float32) * (-math.log(THETA) / half))
    turn = place[:, None] * freq[None, :]
    return (jnp.cos(turn), jnp.sin(turn))


def rotate(value, cosine, sine):
    half = value.shape[-1] // 2
    front, behind = (value[..., :half], value[..., half:])
    return jnp.concatenate(
        [front * cosine - behind * sine, behind * cosine + front * sine], axis=-1
    )


def multiply(left, right):
    return jnp.dot(left, right, preferred_element_type=jnp.float32)


def against(left, right):
    return lax.dot_general(
        left, right, (((1,), (1,)), ((), ())), preferred_element_type=jnp.float32
    )


def outer_sum(left, right):
    return lax.dot_general(
        left, right, (((0,), (0,)), ((), ())), preferred_element_type=jnp.float32
    )


def visible(start, key_start, count, document_ids):
    query_place = start + jnp.arange(count, dtype=jnp.int32)
    key_place = key_start + jnp.arange(count, dtype=jnp.int32)
    query_doc = lax.dynamic_slice_in_dim(document_ids, start, count)
    key_doc = lax.dynamic_slice_in_dim(document_ids, jnp.maximum(key_start, 0), count)
    same_doc = query_doc[:, None] == key_doc[None, :]
    causal = key_place[None, :] <= query_place[:, None]
    same_seq = (query_place // SEQ_LEN)[:, None] == (key_place // SEQ_LEN)[None, :]
    return same_doc & causal & same_seq


def shards(
    tokens,
    document_ids,
    gain_first,
    query_down,
    query_gain,
    latent_down,
    latent_gain,
    query_up,
    latent_up,
    output_weight,
    gain_second,
    gate_weight,
    up_weight,
    down_weight,
    cotangent,
):
    count = tokens.shape[0]
    own_width = tokens.shape[1]
    start = lax.axis_index("row") * count
    column = lax.axis_index("col")
    heads = query_up.shape[1] // (DN + DR)
    scale = (DN + DR) ** (-0.5)
    cosine, sine = angles(start, count)
    bf = jnp.bfloat16
    halves = (
        gain_first.astype(bf),
        query_down.astype(bf),
        query_gain.astype(bf),
        latent_down.astype(bf),
        latent_gain.astype(bf),
        query_up.astype(bf),
        latent_up.astype(bf),
        output_weight.astype(bf),
        gain_second.astype(bf),
        gate_weight.astype(bf),
        up_weight.astype(bf),
        down_weight.astype(bf),
    )
    (
        wide_gain_first,
        wide_query_down,
        wide_query_gain,
        wide_latent_down,
        wide_latent_gain,
        wide_query_up,
        wide_latent_up,
        wide_output,
        wide_gain_second,
        wide_gate,
        wide_up,
        wide_down,
    ) = (
        lax.all_gather(halves[0], "row", axis=0, tiled=True),
        lax.all_gather(halves[1], "row", axis=0, tiled=True),
        lax.all_gather(halves[2], "row", axis=0, tiled=True),
        lax.all_gather(halves[3], "row", axis=0, tiled=True),
        lax.all_gather(halves[4], "row", axis=0, tiled=True),
        lax.all_gather(halves[5], "row", axis=0, tiled=True),
        lax.all_gather(halves[6], "row", axis=0, tiled=True),
        lax.all_gather(halves[7], "row", axis=1, tiled=True),
        lax.all_gather(halves[8], "row", axis=0, tiled=True),
        lax.all_gather(halves[9], "row", axis=0, tiled=True),
        lax.all_gather(halves[10], "row", axis=0, tiled=True),
        lax.all_gather(halves[11], "row", axis=1, tiled=True),
    )
    features = lax.all_gather(tokens, "col", axis=1, tiled=True)
    residual = features.astype(jnp.float32)
    gain_one = wide_gain_first.astype(jnp.float32)
    query_scale = wide_query_gain.astype(jnp.float32)
    latent_scale = wide_latent_gain.astype(jnp.float32)
    gain_two = wide_gain_second.astype(jnp.float32)
    normed, inverse_first = normalize(residual, gain_one)
    first_in = normed.astype(bf)
    query_latent = multiply(first_in, wide_query_down)
    latent_all = multiply(first_in, wide_latent_down)
    query_normed, inverse_query = normalize(query_latent, query_scale)
    query_in = query_normed.astype(bf)
    latent_normed, inverse_latent = normalize(latent_all[:, :KR], latent_scale)
    latent_in = latent_normed.astype(bf)
    key_rot = rotate(latent_all[:, KR:], cosine, sine).astype(bf)
    raw_query = multiply(query_in, wide_query_up).reshape(count, heads, DN + DR)
    queries = jnp.concatenate(
        [raw_query[..., :DN], rotate(raw_query[..., DN:], cosine[:, None, :], sine[:, None, :])],
        axis=-1,
    ).astype(bf)

    def expand(latent_part, rot_part, up_matrix):
        packed = multiply(latent_part, up_matrix).astype(bf).reshape(count, heads, DN + DV)
        keys = jnp.concatenate(
            [packed[..., :DN], jnp.broadcast_to(rot_part[:, None, :], (count, heads, DR))], axis=-1
        )
        return (keys, packed[..., DN:])

    local_keys, local_values = expand(latent_in, key_rot, wide_latent_up)
    sources = [(local_keys, local_values, start)]
    for step in range(1, REACH + 1):
        far_latent, far_rot = from_behind((latent_in, key_rot), "row", step)
        far_keys, far_values = expand(far_latent, far_rot, wide_latent_up)
        sources.append((far_keys, far_values, start - step * count))
    masks = [visible(start, entry[2], count, document_ids) for entry in sources]

    def scores_of(keys, mask):
        raw = jnp.einsum("qhd,khd->hqk", queries, keys, preferred_element_type=jnp.float32) * scale
        return jnp.where(mask[None], raw, NEG)

    top = jnp.full((heads, count), NEG, jnp.float32)
    total = jnp.zeros((heads, count), jnp.float32)
    for entry, mask in zip(sources, masks):
        scores = scores_of(entry[0], mask)
        new_top = jnp.maximum(top, jnp.max(scores, axis=-1))
        total = total * jnp.exp(top - new_top) + jnp.sum(
            jnp.exp(scores - new_top[..., None]), axis=-1
        )
        top = new_top
    logsum = top + jnp.log(total)
    attended = jnp.zeros((count, heads, DV), jnp.float32)
    for entry, mask in zip(sources, masks):
        chance = jnp.exp(scores_of(entry[0], mask) - logsum[..., None]).astype(bf)
        attended = attended + jnp.einsum(
            "hqk,khd->qhd", chance, entry[1], preferred_element_type=jnp.float32
        )
    attended_low = attended.astype(bf).reshape(count, heads * DV)
    branch = lax.psum(multiply(attended_low, wide_output), "col")
    middle = residual + RES * branch
    second_normed, inverse_second = normalize(middle, gain_two)
    second_in = second_normed.astype(bf)
    gate = multiply(second_in, wide_gate)
    upward = multiply(second_in, wide_up)
    sigma = jax.nn.sigmoid(gate)
    hidden = (gate * sigma * upward).astype(bf)
    down_sum = lax.psum_scatter(multiply(hidden, wide_down), "col", scatter_dimension=1, tiled=True)
    middle_own = lax.dynamic_slice_in_dim(middle, column * own_width, own_width, 1)
    result = middle_own + RES * down_sum
    (
        wide_gain_first,
        wide_query_down,
        wide_query_gain,
        wide_latent_down,
        wide_latent_gain,
        wide_query_up,
        wide_latent_up,
        wide_output,
        wide_gain_second,
        wide_gate,
        wide_up,
        wide_down,
    ) = (
        lax.all_gather(halves[0], "row", axis=0, tiled=True),
        lax.all_gather(halves[1], "row", axis=0, tiled=True),
        lax.all_gather(halves[2], "row", axis=0, tiled=True),
        lax.all_gather(halves[3], "row", axis=0, tiled=True),
        lax.all_gather(halves[4], "row", axis=0, tiled=True),
        lax.all_gather(halves[5], "row", axis=0, tiled=True),
        lax.all_gather(halves[6], "row", axis=0, tiled=True),
        lax.all_gather(halves[7], "row", axis=1, tiled=True),
        lax.all_gather(halves[8], "row", axis=0, tiled=True),
        lax.all_gather(halves[9], "row", axis=0, tiled=True),
        lax.all_gather(halves[10], "row", axis=0, tiled=True),
        lax.all_gather(halves[11], "row", axis=1, tiled=True),
    )
    gain_one = wide_gain_first.astype(jnp.float32)
    query_scale = wide_query_gain.astype(jnp.float32)
    latent_scale = wide_latent_gain.astype(jnp.float32)
    gain_two = wide_gain_second.astype(jnp.float32)
    upstream = lax.all_gather(cotangent, "col", axis=1, tiled=True)
    back_down = (RES * upstream).astype(bf)
    back_hidden = against(back_down, wide_down)
    back_gate = (back_hidden * upward * sigma * (1.0 + gate * (1.0 - sigma))).astype(bf)
    back_upward = (back_hidden * gate * sigma).astype(bf)
    back_second = lax.psum(against(back_gate, wide_gate) + against(back_upward, wide_up), "col")
    back_middle_norm, slope_gain_second = norm_back(middle, inverse_second, gain_two, back_second)
    back_middle = upstream + back_middle_norm
    back_branch = (RES * back_middle).astype(bf)
    slope_output = outer_sum(attended_low, back_branch)
    back_attended = against(back_branch, wide_output).astype(bf).reshape(count, heads, DV)
    delta = jnp.zeros((heads, count), jnp.float32)
    for entry, mask in zip(sources, masks):
        chance = jnp.exp(scores_of(entry[0], mask) - logsum[..., None])
        back_chance = jnp.einsum(
            "qhd,khd->hqk", back_attended, entry[1], preferred_element_type=jnp.float32
        )
        delta = delta + jnp.sum(chance * back_chance, axis=-1)
    back_queries = jnp.zeros((count, heads, DN + DR), jnp.float32)
    back_pair = jnp.zeros((count, heads, DN + DV), jnp.float32)
    back_rot = jnp.zeros((count, DR), jnp.float32)
    for index in range(len(sources)):
        keys, values, key_start = sources[index]
        chance = jnp.exp(scores_of(keys, masks[index]) - logsum[..., None])
        back_chance = jnp.einsum(
            "qhd,khd->hqk", back_attended, values, preferred_element_type=jnp.float32
        )
        back_scores = (chance * (back_chance - delta[..., None])).astype(bf)
        back_queries = back_queries + scale * jnp.einsum(
            "hqk,khd->qhd", back_scores, keys, preferred_element_type=jnp.float32
        )
        back_keys = scale * jnp.einsum(
            "hqk,qhd->khd", back_scores, queries, preferred_element_type=jnp.float32
        )
        back_values = jnp.einsum(
            "hqk,qhd->khd", chance.astype(bf), back_attended, preferred_element_type=jnp.float32
        )
        pair_part = jnp.concatenate([back_keys[..., :DN], back_values], axis=-1)
        rot_part = jnp.sum(back_keys[..., DN:], axis=1)
        if index > 0:
            pair_part, rot_part = from_behind((pair_part, rot_part), "row", -index)
        back_pair = back_pair + pair_part
        back_rot = back_rot + rot_part
    back_packed = back_pair.reshape(count, heads * (DN + DV)).astype(bf)
    latent_part = against(back_packed, wide_latent_up)
    slope_latent_up = outer_sum(latent_in, back_packed)
    back_raw = jnp.concatenate(
        [
            back_queries[..., :DN],
            rotate(back_queries[..., DN:], cosine[:, None, :], -sine[:, None, :]),
        ],
        axis=-1,
    )
    back_raw = back_raw.reshape(count, heads * (DN + DR)).astype(bf)
    query_part = against(back_raw, wide_query_up)
    slope_query_up = outer_sum(query_in, back_raw)
    back_query_in, back_latent_in, back_rot_total = lax.psum(
        (query_part, latent_part, back_rot), "col"
    )
    back_query_latent, slope_query_gain = norm_back(
        query_latent, inverse_query, query_scale, back_query_in
    )
    back_query_low = back_query_latent.astype(bf)
    back_latent_c, slope_latent_gain = norm_back(
        latent_all[:, :KR], inverse_latent, latent_scale, back_latent_in
    )
    back_latent_low = jnp.concatenate(
        [back_latent_c, rotate(back_rot_total, cosine, -sine)], axis=-1
    ).astype(bf)
    slope_query_down = outer_sum(first_in, back_query_low)
    slope_latent_down = outer_sum(first_in, back_latent_low)
    back_first = against(back_query_low, wide_query_down) + against(
        back_latent_low, wide_latent_down
    )
    back_norm_first, slope_gain_first = norm_back(residual, inverse_first, gain_one, back_first)
    back_tokens = lax.dynamic_slice_in_dim(
        back_middle + back_norm_first, column * own_width, own_width, 1
    )
    slope_gate_local = outer_sum(second_in, back_gate)
    slope_up_local = outer_sum(second_in, back_upward)
    slope_down_local = outer_sum(hidden, back_down)
    slopes = (
        lax.psum_scatter(slope_gain_first, "row", scatter_dimension=0, tiled=True),
        lax.psum_scatter(slope_query_down, "row", scatter_dimension=0, tiled=True),
        lax.psum_scatter(slope_query_gain, "row", scatter_dimension=0, tiled=True),
        lax.psum_scatter(slope_latent_down, "row", scatter_dimension=0, tiled=True),
        lax.psum_scatter(slope_latent_gain, "row", scatter_dimension=0, tiled=True),
        lax.psum_scatter(slope_query_up, "row", scatter_dimension=0, tiled=True),
        lax.psum_scatter(slope_latent_up, "row", scatter_dimension=0, tiled=True),
        lax.psum_scatter(slope_output, "row", scatter_dimension=1, tiled=True),
        lax.psum_scatter(slope_gain_second, "row", scatter_dimension=0, tiled=True),
        lax.psum_scatter(slope_gate_local, "row", scatter_dimension=0, tiled=True),
        lax.psum_scatter(slope_up_local, "row", scatter_dimension=0, tiled=True),
        lax.psum_scatter(slope_down_local, "row", scatter_dimension=1, tiled=True),
    )
    ffn_slopes = (slopes[9], slopes[10], slopes[11])
    return (
        result,
        back_tokens,
        slopes[0],
        slopes[1],
        slopes[2],
        slopes[3],
        slopes[4],
        slopes[5],
        slopes[6],
        slopes[7],
        slopes[8],
        ffn_slopes[0],
        ffn_slopes[1],
        ffn_slopes[2],
    )


def solution(mesh):
    placed = (
        P("row", "col"),
        P(),
        P("row"),
        P("row", None),
        P("row"),
        P("row", None),
        P("row"),
        P("row", "col"),
        P("row", "col"),
        P("col", "row"),
        P("row"),
        P("row", "col"),
        P("row", "col"),
        P("col", "row"),
        P("row", "col"),
    )
    return jax.shard_map(
        shards,
        mesh=mesh,
        in_specs=placed,
        out_specs=(
            P("row", "col"),
            P("row", "col"),
            P("row"),
            P("row", None),
            P("row"),
            P("row", None),
            P("row"),
            P("row", "col"),
            P("row", "col"),
            P("col", "row"),
            P("row"),
            P("row", "col"),
            P("row", "col"),
            P("col", "row"),
        ),
        check_vma=False,
    )
```

profile of v0, /device:TPU:0, one launch (start us, length us, event | category | flops | bytes accessed | tf_op | source)
XLA Modules:
  0.0 3003.7 jit_solution(7822894912674559678)
XLA Ops:
  17.5 39.5 %all-reduce.10 = (bf16[2560]{0:T(1024)(128)(2,1)S(1)}, bf16[256]{0:T(256)(128)(2,1)S(1)}, bf16[768]{0:T(1024)(128)(2,1)S(1)}, bf16[2560]{0:T(1024)(128)(2,1)}) all-reduce(bf16[2560]{0:T(1024)(128)(2,1)S(1)} %dynamic-update-slice, bf16[256]{0:T(256)(128)(2,1)S(1)} %dynamic-update-slice.1, ...), channel_id=1, replica_groups=mesh['row'=8,'col'=4] {'row'}, use_global_device_ids=true, to_apply=%add | all-reduce | flops 6144 | bytes 24576
  57.0 31.5 %all_gather.58 = bf16[256,1280]{1,0:T(8,128)(2,1)S(1)} all-gather(bf16[32,1280]{1,0:T(8,128)(2,1)S(1)} %convert_element_type.171), channel_id=1, replica_groups=mesh['row'=8,'col'=4] {'row'}, dimensions={0}, use_global_device_ids=true | all-gather | bytes 737280 | tf_op jit(solution)/shard_map/all_gather | solution.py:142
  189.1 43.3 %all-gather.15.cloned.1.call-done = bf16[768,960]{1,0:T(8,128)(2,1)} async-done(((bf16[96,960]{1,0:T(8,128)(2,1)}), bf16[768,960]{1,0:T(8,128)(2,1)}) %all-gather.15.cloned.1.call-update) | async-done | bytes 1474576 | tf_op jit(solution)/shard_map/all_gather | solution.py:141
  325.8 92.7 %all-reduce.15.cloned.1.call-done = f32[512,2560]{1,0:T(8,128)} async-done(((f32[512,2560]{1,0:T(8,128)}), f32[512,2560]{1,0:T(8,128)}) %all-reduce.15.cloned.1.call-update) | async-done | bytes 5242896 | tf_op jit(solution)/shard_map/psum | solution.py:206
  424.8 122.8 %all-gather.19.cloned.1.call-done = bf16[2560,1600]{1,0:T(8,128)(2,1)} async-done(((bf16[320,1600]{1,0:T(8,128)(2,1)}), bf16[2560,1600]{1,0:T(8,128)(2,1)}) %all-gather.19.cloned.1.call-update) | async-done | bytes 8192016 | tf_op jit(solution)/shard_map/all_gather | solution.py:145
  556.6 118.0 %all-gather.21.cloned.1.call-done = bf16[2560,1600]{1,0:T(8,128)(2,1)} async-done(((bf16[320,1600]{1,0:T(8,128)(2,1)}), bf16[2560,1600]{1,0:T(8,128)(2,1)}) %all-gather.21.cloned.1.call-update) | async-done | bytes 8192016 | tf_op jit(solution)/shard_map/all_gather | solution.py:146
  683.2 31.6 %all-gather.25.cloned.1.call-done = f32[512,2560]{1,0:T(8,128)} async-done(((f32[512,640]{1,0:T(8,128)}), f32[512,2560]{1,0:T(8,128)}) %all-gather.25.cloned.1.call-update) | async-done | bytes 5242896 | tf_op jit(solution)/shard_map/all_gather | solution.py:248
  714.8 128.7 %all-gather.23.cloned.1.call-done = bf16[1600,2560]{0,1:T(8,128)(2,1)} async-done(((bf16[1600,320]{0,1:T(8,128)(2,1)}), bf16[1600,2560]{0,1:T(8,128)(2,1)}) %all-gather.23.cloned.1.call-update) | async-done | bytes 8192016 | tf_op jit(solution)/shard_map/all_gather | solution.py:147
  876.6 100.8 %all-reduce.17.cloned.1.call-done = f32[512,2560]{1,0:T(8,128)} async-done(((f32[512,2560]{1,0:T(8,128)}), f32[512,2560]{1,0:T(8,128)}) %all-reduce.17.cloned.1.call-update) | async-done | bytes 5242896 | tf_op jit(solution)/shard_map/psum | solution.py:253
  1017.8 37.1 %multiply_reduce_fusion.3 = (f32[10,512]{1,0:T(8,128)S(1)}, f32[10,512]{1,0:T(8,128)S(1)}, f32[10,512]{1,0:T(8,128)S(1)}, f32[10,512]{1,0:T(8,128)S(1)}, f32[10,512]{1,0:T(8,128)S(1)}, /*index=5*/f32[10,512,512]{1,2,0:T(8,128)}) fusion(f32[10,512,512]{1,2,0:T(8,128)} %get-tuple-element.90, f32[10,512]{1,0:T(8,128)S(1)} %log_add_fusion, ...), kind=kOutput, calls=%fused_computation.8 | convolution fusion | flops 401054720 | bytes 107614208 | tf_op jit(solution)/shard_map/qhd,khd->hqk/dot_general | solution.py:262
  1054.9 44.0 %multiply_convert_fusion = (bf16[10,512,512]{1,2,0:T(8,128)(2,1)}, bf16[10,512,512]{1,2,0:T(8,128)(2,1)}, bf16[10,512,512]{1,2,0:T(8,128)(2,1)}, bf16[10,512,512]{1,2,0:T(8,128)(2,1)}, bf16[10,512,512]{1,2,0:T(8,128)(2,1)}) fusion(f32[10,512,512]{1,2,0:T(8,128)} %fusion.30, f32[10,512,512]{1,2,0:T(8,128)} %copy-done.2, f32[10,512]{1,0:T(8,128)S(1)} %add_add_fusion.1, ...), kind=kLoop, calls=%fused_computation | loop fusion | flops 78643200 | bytes 132423680 | tf_op jit(solution)/shard_map/convert_element_type | solution.py:275
  1169.1 157.0 %collective-permute-done.14 = f32[512,32]{0,1:T(8,128)S(1)} collective-permute-done((f32[512,32]{0,1:T(8,128)S(1)}, f32[512,32]{0,1:T(8,128)S(1)}, u32[]{:S(2)}, u32[]{:S(2)}) %collective-permute-start.14) | collective-permute-done | bytes 65568 | tf_op jit(solution)/shard_map/ppermute | solution.py:25
  1327.4 58.4 %collective-permute-done.13 = f32[512,32]{0,1:T(8,128)S(1)} collective-permute-done((f32[512,32]{0,1:T(8,128)S(1)}, f32[512,32]{0,1:T(8,128)S(1)}, u32[]{:S(2)}, u32[]{:S(2)}) %collective-permute-start.13) | collective-permute-done | bytes 65568 | tf_op jit(solution)/shard_map/ppermute | solution.py:25
  1387.5 118.2 %collective-permute-done.12 = f32[512,32]{0,1:T(8,128)S(1)} collective-permute-done((f32[512,32]{0,1:T(8,128)S(1)}, f32[512,32]{0,1:T(8,128)S(1)}, u32[]{:S(2)}, u32[]{:S(2)}) %collective-permute-start.12) | collective-permute-done | bytes 65568 | tf_op jit(solution)/shard_map/ppermute | solution.py:25
  1523.2 41.5 %all-reduce.19.cloned.1.call-done = (f32[512,768]{1,0:T(8,128)}, f32[512,32]{0,1:T(8,128)}, f32[512,256]{0,1:T(8,128)}) async-done(((f32[512,768]{1,0:T(8,128)}, f32[512,32]{0,1:T(8,128)}, f32[512,256]{0,1:T(8,128)}), (f32[512,768]{1,0:T(8,128)}, f32[512,32]{0,1:T(8,128)}, f32[512,256]{0,1:T(8,128)})) %all-reduce.19.cloned.1.call-update) | async-done | bytes 2162704 | tf_op jit(solution)/shard_map/psum | solution.py:304
  1644.4 37.8 %all-reduce.8 = (f32[2560]{0:T(1024)S(1)}, f32[768]{0:T(1024)S(1)}, f32[256]{0:T(256)S(1)}, f32[2560]{0:T(1024)S(1)}) all-reduce(f32[2560]{0:T(1024)S(1)} %get-tuple-element.18, f32[768]{0:T(1024)S(1)} %get-tuple-element.16, f32[256]{0:T(256)S(1)} %get-tuple-element.20, ...), channel_id=3, replica_groups=mesh['row'=8,'col'=4] {'row'}, use_global_device_ids=true, to_apply=%region_35.36.clone | all-reduce | flops 6144 | bytes 49152
  1691.2 16.7 reduce-scatter.28.cloned.1.call-done
  1709.9 66.2 %reduce-scatter.18.cloned.1.call-done = f32[32,1280]{1,0:T(8,128)} async-done(((f32[256,1280]{1,0:T(8,128)}), f32[32,1280]{1,0:T(8,128)}) %reduce-scatter.18.cloned.1.call-update) | async-done | bytes 163856 | tf_op jit(solution)/shard_map/reduce_scatter | solution.py:336
  1776.1 77.6 %reduce-scatter.16.cloned.1.call-done = f32[96,960]{1,0:T(8,128)} async-done(((f32[768,960]{1,0:T(8,128)}), f32[96,960]{1,0:T(8,128)}) %reduce-scatter.16.cloned.1.call-update) | async-done | bytes 368656 | tf_op jit(solution)/shard_map/reduce_scatter | solution.py:335
  1853.8 125.3 %reduce-scatter.20.cloned.1.call-done = f32[640,320]{0,1:T(8,128)} async-done(((f32[640,2560]{0,1:T(8,128)}), f32[640,320]{0,1:T(8,128)}) %reduce-scatter.20.cloned.1.call-update) | async-done | bytes 819216 | tf_op jit(solution)/shard_map/reduce_scatter | solution.py:337
  1979.1 143.2 %reduce-scatter.14.cloned.1.call-done = f32[320,768]{1,0:T(8,128)} async-done(((f32[2560,768]{1,0:T(8,128)}), f32[320,768]{1,0:T(8,128)}) %reduce-scatter.14.cloned.1.call-update) | async-done | bytes 983056 | tf_op jit(solution)/shard_map/reduce_scatter | solution.py:331
  2122.3 291.3 %reduce-scatter.22.cloned.1.call-done = f32[320,1600]{1,0:T(8,128)} async-done(((f32[2560,1600]{1,0:T(8,128)}), f32[320,1600]{1,0:T(8,128)}) %reduce-scatter.22.cloned.1.call-update) | async-done | bytes 2048016 | tf_op jit(solution)/shard_map/reduce_scatter | solution.py:339
  2413.6 291.7 %reduce-scatter.24.cloned.1.call-done = f32[320,1600]{1,0:T(8,128)} async-done(((f32[2560,1600]{1,0:T(8,128)}), f32[320,1600]{1,0:T(8,128)}) %reduce-scatter.24.cloned.1.call-update) | async-done | bytes 2048016 | tf_op jit(solution)/shard_map/reduce_scatter | solution.py:340
  2705.3 291.3 %reduce-scatter.26.cloned.1.call-done = f32[1600,320]{0,1:T(8,128)} async-done(((f32[1600,2560]{0,1:T(8,128)}), f32[1600,320]{0,1:T(8,128)}) %reduce-scatter.26.cloned.1.call-update) | async-done | bytes 2048016 | tf_op jit(solution)/shard_map/reduce_scatter | solution.py:341
  (570 shorter events, 476.4 us)
Async XLA Ops:
  9.9 174.0 %all-gather.13.cloned.1.call-start = ((), (), s32[]{:S(2)}) async-start(), calls=%async_computation.10 | async-start | bytes 4423680 | tf_op jit(solution)/shard_map/all_gather | solution.py:137
  12.0 220.4 %all-gather.15.cloned.1.call-start = ((), (), s32[]{:S(2)}) async-start(), calls=%async_computation.11 | async-start | bytes 1769472 | tf_op jit(solution)/shard_map/all_gather | solution.py:141
  12.8 297.1 %all-gather.17.cloned.1.call-start = ((), (), s32[]{:S(2)}) async-start(), calls=%async_computation.12 | async-start | bytes 3686400 | tf_op jit(solution)/shard_map/all_gather | solution.py:143
  13.7 404.9 %all-reduce.15.cloned.1.call-start = ((), (), s32[]{:S(2)}) async-start(), calls=%async_computation.13 | async-start | bytes 10485760 | tf_op jit(solution)/shard_map/psum | solution.py:206
  316.6 230.9 %all-gather.19.cloned.1.call-start = ((), (), s32[]{:S(2)}) async-start(), calls=%async_computation.14 | async-start | bytes 9584640 | tf_op jit(solution)/shard_map/all_gather | solution.py:145
  319.4 355.2 %all-gather.21.cloned.1.call-start = ((), (), s32[]{:S(2)}) async-start(), calls=%async_computation.15 | async-start | bytes 9584640 | tf_op jit(solution)/shard_map/all_gather | solution.py:146
  322.1 392.7 %all-gather.25.cloned.1.call-start = ((), (), s32[]{:S(2)}) async-start(), calls=%async_computation.18 | async-start | bytes 6553600 | tf_op jit(solution)/shard_map/all_gather | solution.py:248
  322.9 520.6 %all-gather.23.cloned.1.call-start = ((), (), s32[]{:S(2)}) async-start(), calls=%async_computation.16 | async-start | bytes 9584640 | tf_op jit(solution)/shard_map/all_gather | solution.py:147
  325.8 651.7 %all-reduce.17.cloned.1.call-start = ((), (), s32[]{:S(2)}) async-start(), calls=%async_computation.19 | async-start | bytes 10485760 | tf_op jit(solution)/shard_map/psum | solution.py:253
  876.6 688.1 %all-reduce.19.cloned.1.call-start = ((), (), s32[]{:S(2)}) async-start(), calls=%async_computation.29 | async-start | bytes 4325376 | tf_op jit(solution)/shard_map/psum | solution.py:304
  1148.8 357.6 %collective-permute-start.11 = (f32[512,10,128]{0,2,1:T(8,128)}, f32[512,10,128]{0,2,1:T(8,128)S(1)}, u32[]{:S(2)}, u32[]{:S(2)}) collective-permute-start(f32[512,10,128]{0,2,1:T(8,128)} %pad_maximum_fusion.3), channel_id=1, source_target_pairs={{16,0},{20,4},{24,8},{28,12},{17,1},{21,5},{25,9},{29,13},{18,2},{... | collective-permute-start | bytes 7864328 | tf_op jit(solution)/shard_map/ppermute | solution.py:25
  1151.9 354.5 %collective-permute-start.10 = (f32[512,10,128]{0,2,1:T(8,128)}, f32[512,10,128]{0,2,1:T(8,128)S(1)}, u32[]{:S(2)}, u32[]{:S(2)}) collective-permute-start(f32[512,10,128]{0,2,1:T(8,128)} %pad_maximum_fusion.2), channel_id=1, source_target_pairs={{12,0},{16,4},{20,8},{24,12},{28,16},{13,1},{17,5},{21,9},{25,13},... | collective-permute-start | bytes 7864328 | tf_op jit(solution)/shard_map/ppermute | solution.py:25
  1155.0 351.4 %collective-permute-start.9 = (f32[512,10,128]{0,2,1:T(8,128)}, f32[512,10,128]{0,2,1:T(8,128)}, u32[]{:S(2)}, u32[]{:S(2)}) collective-permute-start(f32[512,10,128]{0,2,1:T(8,128)} %pad_maximum_fusion.1), channel_id=1, source_target_pairs={{8,0},{12,4},{16,8},{20,12},{24,16},{28,20},{9,1},{13,5},{17,9},{2... | collective-permute-start | bytes 7864328 | tf_op jit(solution)/shard_map/ppermute | solution.py:25
  1158.2 348.2 %collective-permute-start.8 = (f32[512,10,128]{0,2,1:T(8,128)}, f32[512,10,128]{0,2,1:T(8,128)}, u32[]{:S(2)}, u32[]{:S(2)}) collective-permute-start(f32[512,10,128]{0,2,1:T(8,128)} %pad_maximum_fusion), channel_id=1, source_target_pairs={{4,0},{8,4},{12,8},{16,12},{20,16},{24,20},{28,24},{5,1},{9,5},{13... | collective-permute-start | bytes 7864328 | tf_op jit(solution)/shard_map/ppermute | solution.py:25
  1167.7 158.4 %collective-permute-start.14 = (f32[512,32]{0,1:T(8,128)S(1)}, f32[512,32]{0,1:T(8,128)S(1)}, u32[]{:S(2)}, u32[]{:S(2)}) collective-permute-start(f32[512,32]{0,1:T(8,128)S(1)} %slice_reduce_fusion.1), channel_id=1, source_target_pairs={{12,0},{16,4},{20,8},{24,12},{28,16},{13,1},{17,5},{21,9},{25,13},... | collective-permute-start | bytes 196616 | tf_op jit(solution)/shard_map/ppermute | solution.py:25
  1512.8 175.4 %reduce-scatter.12.cloned.1.call-start = ((), (), s32[]{:S(2)}) async-start(), calls=%async_computation.17 | async-start | bytes 6553600 | tf_op jit(solution)/shard_map/reduce_scatter | solution.py:214
  1523.2 184.7 %reduce-scatter.28.cloned.1.call-start = ((), (), s32[]{:S(2)}) async-start(), calls=%async_computation.28 | async-start | bytes 4423680
  1571.9 204.3 %reduce-scatter.18.cloned.1.call-start = ((), (), s32[]{:S(2)}) async-start(), calls=%async_computation.22 | async-start | bytes 1474560 | tf_op jit(solution)/shard_map/reduce_scatter | solution.py:336
  1576.2 277.6 %reduce-scatter.16.cloned.1.call-start = ((), (), s32[]{:S(2)}) async-start(), calls=%async_computation.21 | async-start | bytes 3538944 | tf_op jit(solution)/shard_map/reduce_scatter | solution.py:335
  1580.7 398.4 %reduce-scatter.20.cloned.1.call-start = ((), (), s32[]{:S(2)}) async-start(), calls=%async_computation.23 | async-start | bytes 7372800 | tf_op jit(solution)/shard_map/reduce_scatter | solution.py:337
  1588.6 533.7 %reduce-scatter.14.cloned.1.call-start = ((), (), s32[]{:S(2)}) async-start(), calls=%async_computation.20 | async-start | bytes 8847360 | tf_op jit(solution)/shard_map/reduce_scatter | solution.py:331
  1597.3 816.4 %reduce-scatter.22.cloned.1.call-start = ((), (), s32[]{:S(2)}) async-start(), calls=%async_computation.24 | async-start | bytes 19169280 | tf_op jit(solution)/shard_map/reduce_scatter | solution.py:339
  1609.1 1096.2 %reduce-scatter.24.cloned.1.call-start = ((), (), s32[]{:S(2)}) async-start(), calls=%async_computation.25 | async-start | bytes 19169280 | tf_op jit(solution)/shard_map/reduce_scatter | solution.py:340
  1619.3 1377.4 %reduce-scatter.26.cloned.1.call-start = ((), (), s32[]{:S(2)}) async-start(), calls=%async_computation.26 | async-start | bytes 19169280 | tf_op jit(solution)/shard_map/reduce_scatter | solution.py:341
  (173 other events, 4483.8 us)
Sparse Core Ops, SparseCore 0:
  10.9 51.1 all-gather.26
  63.7 23.7 all-gather.10
  89.7 94.1 all-gather.12
  185.9 46.5 all-gather.14
  235.0 60.7 all-gather.16
  316.8 101.7 all-reduce.14
  420.7 126.8 all-gather.18
  549.7 124.8 all-gather.20
  676.2 38.6 all-gather.24
  716.8 126.6 all-gather.22
  876.7 100.6 all-reduce.16
  1512.9 51.8 all-reduce.18
  1567.4 51.4 reduce-scatter.11
  1622.5 85.3 reduce-scatter.27
  1712.1 64.0 reduce-scatter.17
  1780.6 73.1 reduce-scatter.15
  1858.3 120.7 reduce-scatter.19
  1983.2 139.0 reduce-scatter.13
  2126.8 286.8 reduce-scatter.21
  2418.4 286.8 reduce-scatter.23
  2709.8 286.8 reduce-scatter.25
where the time goes:
time: 3010 us; the launch traced here: 3000 us
  waiting for transfers between devices  2340 us (78%)
  matrix products  311 us (10%)
  other arithmetic  131 us (4%)
  blocking collectives  109 us (4%)
  starting transfers between devices  46.8 us (2%)
  local copies, waits for them, and re-layouts  45.7 us (2%)
    ppermute x16, waiting for transfers between devices, from_behind(): lax.ppermute(value, axis, [(source, source + steps) for source in range(i...  343 us
    reduce_scatter x1, waiting for transfers between devices, shards(): lax.psum_scatter(slope_up_local, 'row', scatter_dimension=0, tiled=True)  292 us
    reduce_scatter x1, waiting for transfers between devices, shards(): lax.psum_scatter(slope_down_local, 'row', scatter_dimension=1, tiled=True)  291 us
    reduce_scatter x1, waiting for transfers between devices, shards(): lax.psum_scatter(slope_gate_local, 'row', scatter_dimension=0, tiled=True)  291 us
    reduce_scatter x1, waiting for transfers between devices, shards(): lax.psum_scatter(slope_query_down, 'row', scatter_dimension=0, tiled=True)  143 us
    all_gather x1, waiting for transfers between devices, shards(): lax.all_gather(halves[11], 'row', axis=1, tiled=True)  129 us
    reduce_scatter x1, waiting for transfers between devices, shards(): lax.psum_scatter(slope_output, 'row', scatter_dimension=1, tiled=True)  125 us
    all_gather x1, waiting for transfers between devices, shards(): lax.all_gather(halves[9], 'row', axis=0, tiled=True)  123 us
  transfers between devices with their start and end apart: 37, of which 22 were waited for; matrix products, arithmetic and copies ran while one was open for 9% of the time, Pallas kernels for 0%

commit v1 on v0

v1 whole, which is shorter than its diff:
```python
import functools
import math

import jax
import jax.numpy as jnp
from jax import lax
from jax.experimental import pallas as pl
from jax.experimental.pallas import tpu as pltpu
from jax.sharding import PartitionSpec as P

DN = 64
DR = 32
DV = 64
QR = 768
KR = 256
SEQ_LEN = 4096
DOC_MOST = 2000
EPS = 1e-05
RES = 1.4 / math.sqrt(62.0)
THETA = 10000.0
NEG = -1e30
LOG2E = math.log2(math.e)
SCALE = (DN + DR) ** (-0.5)
VMEM_LIMIT = 56 << 20
bf = jnp.bfloat16
f32 = jnp.float32


def ring_place(row, rows):
    return row // 2 + (row % 2) * (rows - 1 - 2 * (row // 2))


def ring_row(place, rows):
    side = place // (rows // 2)
    return 2 * (place + side * (rows - 1 - 2 * place)) + side


def ring_links(rows):
    order = [ring_row(p, rows) for p in range(rows)]
    ahead = [(order[p], order[(p + 1) % rows]) for p in range(rows)]
    return (ahead, [(b, a) for a, b in ahead])


class Gather:
    def __init__(self, block):
        self.rows = lax.axis_size("row")
        self.place = ring_place(lax.axis_index("row"), self.rows)
        self.shape = block.shape
        half = block.shape[0] // 2
        self.links = ring_links(self.rows)
        self.moving = [block[:half], block[half:]]
        self.whole = jnp.zeros((self.rows, 2, half, block.shape[1]), block.dtype)
        self.put(0)
        self.step = 0

    def put(self, step):
        for side in (0, 1):
            origin = ring_row((self.place + (step if side else self.rows - step)) % self.rows, self.rows)
            self.whole = lax.dynamic_update_slice(
                self.whole, self.moving[side][None, None], (origin, side, 0, 0)
            )

    def advance(self):
        self.moving = [lax.ppermute(self.moving[side], "row", self.links[side]) for side in (0, 1)]
        self.step += 1
        self.put(self.step)

    def result(self):
        return self.whole.reshape(self.rows * self.shape[0], self.shape[1])


def gather_rows(*blocks):
    flows = [Gather(block) for block in blocks]
    for _ in range(flows[0].rows - 1):
        for flow in flows:
            flow.advance()
    return [flow.result() for flow in flows]


class Scatter:
    def __init__(self, left, right, transposed=False):
        self.rows = lax.axis_size("row")
        self.place = ring_place(lax.axis_index("row"), self.rows)
        half = left.shape[0] // self.rows // 2
        self.left = left.reshape(self.rows, 2, half, left.shape[1])
        self.right = right
        self.transposed = transposed
        self.links = ring_links(self.rows)
        self.moving = [self.part(0, side).astype(bf) for side in (0, 1)]
        self.step = 0

    def part(self, step, side):
        place = self.place + 1 + step if side else self.place + 2 * self.rows - 1 - step
        target = ring_row(place % self.rows, self.rows)
        piece = lax.dynamic_slice(self.left, (target, side, 0, 0), (1, 1) + self.left.shape[2:])[0, 0]
        contract = ((1,), (1,)) if self.transposed else ((1,), (0,))
        return lax.dot_general(piece, self.right, (contract, ((), ())), preferred_element_type=f32)

    def advance(self):
        self.step += 1
        last = self.step == self.rows - 1
        for side in (0, 1):
            arrived = lax.ppermute(self.moving[side], "row", self.links[side])
            total = arrived.astype(f32) + self.part(self.step, side)
            self.moving[side] = total if last else total.astype(bf)

    def result(self):
        return jnp.concatenate(self.moving, axis=0)


def scatter_rows(*flows):
    for _ in range(flows[0].rows - 1):
        for flow in flows:
            flow.advance()
    return [flow.result() for flow in flows]


def from_behind(value, steps):
    count = lax.axis_size("row")
    initial, last = (max(0, -steps), min(count, count - steps))
    return lax.ppermute(value, "row", [(source, source + steps) for source in range(initial, last)])


def swap_col(value, bit):
    return lax.ppermute(value, "col", [(c, c ^ bit) for c in range(lax.axis_size("col"))])


def by_owner(pieces):
    column = lax.axis_index("col")
    bit = 1
    pieces = list(pieces)
    while bit < len(pieces):
        odd = (column // bit) % 2 == 1
        pieces = [jnp.where(odd, pieces[k ^ bit], pieces[k]) for k in range(len(pieces))]
        bit *= 2
    return pieces


def pick(pieces):
    return by_owner(pieces)[0]


def col_gather(own):
    across = swap_col(own, 2)
    beside = swap_col(own, 1)
    return by_owner([own, beside, across, swap_col(across, 1)])


def col_scatter(pieces):
    mine = by_owner(pieces)
    low = [piece.astype(bf) for piece in mine]
    across = mine[2].astype(f32) + swap_col(low[3], 1).astype(f32)
    beside = mine[0].astype(f32) + swap_col(low[1], 1).astype(f32)
    return beside + swap_col(across.astype(bf), 2).astype(f32)


def col_exchange(pieces):
    mine = by_owner(pieces)
    return by_owner([mine[0]] + [swap_col(mine[k], k) for k in range(1, len(mine))])


def quarters(value, axis):
    return jnp.split(value, lax.axis_size("col"), axis=axis)


def dot(left, right, dims):
    return lax.dot_general(left, right, (dims, ((), ())), preferred_element_type=f32)


def multiply(left, right):
    return dot(left, right, ((1,), (0,)))


def against(left, right):
    return dot(left, right, ((1,), (1,)))


def over_rows(left, right):
    return dot(left, right, ((0,), (0,)))


def inverse_of(value, axis):
    return lax.rsqrt(jnp.mean(value * value, axis=axis, keepdims=True) + EPS)


def norm_back(value, inverse, gain, upstream, axis):
    unit = value * inverse
    scaled = upstream * gain
    inward = inverse * (scaled - unit * jnp.mean(scaled * unit, axis=axis, keepdims=True))
    return (inward, jnp.sum(upstream * unit, axis=1 - axis))


def angles(start, count):
    place = ((start + jnp.arange(count, dtype=jnp.int32)) % SEQ_LEN).astype(f32)
    half = DR // 2
    freq = jnp.exp(jnp.arange(half, dtype=f32) * (-math.log(THETA) / half))
    turn = freq[:, None] * place[None, :]
    return (jnp.cos(turn), jnp.sin(turn))


def rotate(front, behind, cosine, sine):
    return (front * cosine - behind * sine, behind * cosine + front * sine)


def query_columns(heads):
    tiles = -(-heads // 4)
    column = lax.iota(jnp.int32, heads * DN + tiles * 128)
    plain = (column // DN) * (DN + DR) + column % DN
    rest = column - heads * DN
    head = (rest // 128) * 4 + (rest % 64) // 16
    turned = head * (DN + DR) + DN + ((rest % 128) // 64) * 16 + rest % 16
    turned = jnp.where(head < heads, turned, -1)
    return jnp.where(column < heads * DN, plain, turned)


def latent_columns(heads):
    column = lax.iota(jnp.int32, heads * (DN + DV))
    rest = column % (heads * DN)
    return (rest // DN) * (DN + DV) + rest % DN + (column // (heads * DN)) * DN


def chosen(origin, width):
    return lax.broadcasted_iota(jnp.int32, (width, origin.shape[0]), 0) == origin[None, :]


BLOCK = 512


def head_rows(step, side, shape, axis):
    place = lax.broadcasted_iota(jnp.int32, shape, axis)
    plain = (place // DN == side).astype(f32).astype(bf)
    turned = ((place % 64) // 16 == 2 * (step % 2) + side).astype(f32).astype(bf)
    return (plain, turned)


def attend_kernel(blocks, first_ref, qn_ref, qr_ref, k_ref, kr_ref, vt_ref, bias_ref, o_ref, lse_ref, s_ref):
    step = pl.program_id(0)
    first = first_ref[0]
    count = qn_ref.shape[1]
    for side in (0, 1):
        plain, turned = head_rows(step, side, qn_ref.shape, 0)
        right = jnp.concatenate([qn_ref[...] * plain, qr_ref[...] * turned], axis=0)

        def score(j, top):
            rows = pl.ds(pl.multiple_of(j * BLOCK, BLOCK), BLOCK)
            left = jnp.concatenate([k_ref[rows, :], kr_ref[rows, :]], axis=1)
            s = multiply(left, right) * (SCALE * LOG2E) + bias_ref[rows, :]
            s_ref[rows, :] = s
            return jnp.maximum(top, jnp.max(s, axis=0, keepdims=True))

        top = lax.fori_loop(first, blocks, score, jnp.full((1, count), NEG, f32))

        def gather(j, carry):
            total, out = carry
            rows = pl.ds(pl.multiple_of(j * BLOCK, BLOCK), BLOCK)
            chance = jnp.exp2(s_ref[rows, :] - top)
            total = total + jnp.sum(chance, axis=0, keepdims=True)
            out = out + multiply(vt_ref[side * DV : (side + 1) * DV, rows], chance.astype(bf))
            return (total, out)

        total, out = lax.fori_loop(
            first, blocks, gather, (jnp.zeros((1, count), f32), jnp.zeros((DV, count), f32))
        )
        o_ref[side * DV : (side + 1) * DV, :] = (out / total).astype(bf)
        lse_ref[0, side : side + 1, :] = top + jnp.log2(total)


def attend(first, query, keys, turned_keys, values_t, bias, heads):
    count, kl = query.shape[1], keys.shape[0]
    pairs, base = heads // 2, heads * DN // 128
    grid = pltpu.PrefetchScalarGridSpec(
        num_scalar_prefetch=1,
        grid=(pairs,),
        in_specs=[
            pl.BlockSpec((128, count), lambda p, s: (p, 0)),
            pl.BlockSpec((128, count), lambda p, s: (base + p // 2, 0)),
            pl.BlockSpec((kl, 128), lambda p, s: (0, p)),
            pl.BlockSpec((kl, 128), lambda p, s: (0, 0)),
            pl.BlockSpec((128, kl), lambda p, s: (p, 0)),
            pl.BlockSpec((kl, count), lambda p, s: (0, 0)),
        ],
        out_specs=[
            pl.BlockSpec((128, count), lambda p, s: (p, 0)),
            pl.BlockSpec((1, 2, count), lambda p, s: (p, 0, 0)),
        ],
        scratch_shapes=[pltpu.VMEM((kl, count), f32)],
    )
    return pl.pallas_call(
        functools.partial(attend_kernel, kl // BLOCK),
        grid_spec=grid,
        out_shape=[
            jax.ShapeDtypeStruct((heads * DV, count), bf),
            jax.ShapeDtypeStruct((pairs, 2, count), f32),
        ],
        compiler_params=pltpu.CompilerParams(vmem_limit_bytes=VMEM_LIMIT),
        cost_estimate=pl.CostEstimate(
            flops=heads * kl * count * 2 * 512, bytes_accessed=16 << 20, transcendentals=heads * kl * count
        ),
        name="attend",
    )(first, query, query, keys, turned_keys, values_t, bias)


def attend_back_kernel(
    blocks, first_ref, qn_ref, qr_ref, qnn_ref, qrn_ref, k_ref, kr_ref, kt_ref, krt_ref, v_ref, dot_ref, do_ref,
    bias_ref, lse_ref, dqn_ref, dqr_ref, dk_ref, dv_ref, dkr_ref, p_ref, dp_ref,
):
    step = pl.program_id(0)
    first = first_ref[0]
    count = qn_ref.shape[1]

    @pl.when(step == 0)
    def _():
        dkr_ref[...] = jnp.zeros_like(dkr_ref)

    @pl.when(step % 2 == 0)
    def _():
        dqr_ref[...] = jnp.zeros_like(dqr_ref)

    dk_ref[...] = jnp.zeros_like(dk_ref)
    dv_ref[...] = jnp.zeros_like(dv_ref)
    for side in (0, 1):
        plain, turned = head_rows(step, side, qn_ref.shape, 0)
        right = jnp.concatenate([qn_ref[...] * plain, qr_ref[...] * turned], axis=0)
        out_right = dot_ref[...] * plain
        lse = lse_ref[0, side : side + 1, :]

        def score(j, delta):
            rows = pl.ds(pl.multiple_of(j * BLOCK, BLOCK), BLOCK)
            left = jnp.concatenate([k_ref[rows, :], kr_ref[rows, :]], axis=1)
            s = multiply(left, right) * (SCALE * LOG2E) + bias_ref[rows, :]
            chance = jnp.exp2(s - lse)
            p_ref[rows, :] = chance
            back = multiply(v_ref[rows, :], out_right)
            dp_ref[rows, :] = back
            return delta + jnp.sum(chance * back, axis=0, keepdims=True)

        delta = lax.fori_loop(first, blocks, score, jnp.zeros((1, count), f32))
        plain_l, turned_l = head_rows(step, side, qnn_ref.shape, 1)
        query_right = jnp.concatenate([qnn_ref[...] * plain_l, qrn_ref[...] * turned_l], axis=1)
        value_right = do_ref[...] * plain_l

        def spread(j, dq):
            rows = pl.ds(pl.multiple_of(j * BLOCK, BLOCK), BLOCK)
            chance = p_ref[rows, :]
            ds = (chance * (dp_ref[rows, :] - delta)).astype(bf)
            left = jnp.concatenate([kt_ref[:, rows], krt_ref[:, rows]], axis=0)
            dq = dq + multiply(left, ds)
            dk = multiply(ds, query_right)
            dk_ref[rows, :] += (dk[:, :128] * SCALE).astype(bf)
            dkr_ref[rows, :] += dk[:, 128:] * SCALE
            dv_ref[rows, :] += multiply(chance.astype(bf), value_right).astype(bf)
            return dq

        dq = lax.fori_loop(first, blocks, spread, jnp.zeros((256, count), f32)) * SCALE
        dqn_ref[side * DN : (side + 1) * DN, :] = dq[side * DN : (side + 1) * DN]
        place = lax.broadcasted_iota(jnp.int32, (128, count), 0)
        dqr_ref[...] += jnp.where((place % 64) // 16 == 2 * (step % 2) + side, dq[128:], 0.0)


def attend_back(first, query, query_n, keys, turned_keys, keys_t, turned_keys_t, values, do_t, do, bias, lse, heads):
    count, kl = query.shape[1], keys.shape[0]
    pairs, base, tiles = heads // 2, heads * DN // 128, -(-heads // 4)
    across = lambda p, s: (0, p)
    along = lambda p, s: (p, 0)
    fixed = lambda p, s: (0, 0)
    grid = pltpu.PrefetchScalarGridSpec(
        num_scalar_prefetch=1,
        grid=(pairs,),
        in_specs=[
            pl.BlockSpec((128, count), along),
            pl.BlockSpec((128, count), lambda p, s: (base + p // 2, 0)),
            pl.BlockSpec((count, 128), across),
            pl.BlockSpec((count, 128), lambda p, s: (0, base + p // 2)),
            pl.BlockSpec((kl, 128), across),
            pl.BlockSpec((kl, 128), fixed),
            pl.BlockSpec((128, kl), along),
            pl.BlockSpec((128, kl), fixed),
            pl.BlockSpec((kl, 128), across),
            pl.BlockSpec((128, count), along),
            pl.BlockSpec((count, 128), across),
            pl.BlockSpec((kl, count), fixed),
            pl.BlockSpec((1, 2, count), lambda p, s: (p, 0, 0)),
        ],
        out_specs=[
            pl.BlockSpec((128, count), along),
            pl.BlockSpec((128, count), lambda p, s: (p // 2, 0)),
            pl.BlockSpec((kl, 128), across),
            pl.BlockSpec((kl, 128), across),
            pl.BlockSpec((kl, 128), fixed),
        ],
        scratch_shapes=[pltpu.VMEM((kl, count), f32), pltpu.VMEM((kl, count), f32)],
    )
    return pl.pallas_call(
        functools.partial(attend_back_kernel, kl // BLOCK),
        grid_spec=grid,
        out_shape=[
            jax.ShapeDtypeStruct((heads * DN, count), f32),
            jax.ShapeDtypeStruct((tiles * 128, count), f32),
            jax.ShapeDtypeStruct((kl, heads * DN), bf),
            jax.ShapeDtypeStruct((kl, heads * DV), bf),
            jax.ShapeDtypeStruct((kl, 128), f32),
        ],
        compiler_params=pltpu.CompilerParams(vmem_limit_bytes=VMEM_LIMIT),
        cost_estimate=pl.CostEstimate(
            flops=heads * kl * count * 2 * 1280, bytes_accessed=32 << 20, transcendentals=heads * kl * count
        ),
        name="attend_back",
    )(first, query, query, query_n, query_n, keys, turned_keys, keys_t, turned_keys_t, values, do_t, do, bias, lse)


def shards(
    tokens, document_ids, gain_first, query_down, query_gain, latent_down, latent_gain, query_up, latent_up,
    output_weight, gain_second, gate_weight, up_weight, down_weight, cotangent,
):
    count, own_width = tokens.shape
    rows, cols = lax.axis_size("row"), lax.axis_size("col")
    row, column = lax.axis_index("row"), lax.axis_index("col")
    start = row * count
    heads = query_up.shape[1] // (DN + DR)
    reach = -(-(DOC_MOST - 1) // count)
    blocks = reach + 1
    wide = heads * DN
    quarter = count // cols
    cosine, sine = angles(start, count)

    both_down = jnp.concatenate([query_down, latent_down], axis=1).astype(bf)
    down_slice = pick(quarters(both_down, 1))
    slice_width = down_slice.shape[1]
    small = jnp.concatenate([query_gain, latent_gain]).astype(bf)
    small = jnp.pad(small, (0, gain_first.shape[0] - small.shape[0]))
    gains = jnp.stack([gain_first.astype(bf), gain_second.astype(bf), small], axis=1)
    query_one = chosen(query_columns(heads), heads * (DN + DR))
    latent_one = chosen(latent_columns(heads), heads * (DN + DV))
    query_up_low = multiply(query_up.astype(bf), query_one.astype(bf)).astype(bf)
    latent_up_low = multiply(latent_up.astype(bf), latent_one.astype(bf)).astype(bf)
    (wide_down,) = gather_rows(jnp.concatenate([down_slice, gains], axis=1))
    wide_query_up, wide_latent_up = gather_rows(query_up_low, latent_up_low)
    (wide_output,) = gather_rows(output_weight.astype(bf).T)
    wide_gate, wide_up, wide_back = gather_rows(
        gate_weight.astype(bf), up_weight.astype(bf), down_weight.astype(bf).T
    )
    gain_one = wide_down[:, slice_width].astype(f32)
    gain_two = wide_down[:, slice_width + 1].astype(f32)
    small_gains = wide_down[:, slice_width + 2].reshape(rows, -1).astype(f32)
    own_q = query_gain.shape[0]
    query_scale = small_gains[:, :own_q].reshape(-1)[:, None]
    latent_scale = small_gains[:, own_q : own_q + latent_gain.shape[0]].reshape(-1)[:, None]
    wide_down = wide_down[:, :slice_width]

    features = jnp.concatenate(col_gather(tokens), axis=1)
    own_up = jnp.concatenate(col_exchange(quarters(cotangent, 0)), axis=1)
    back_down = jnp.concatenate(col_gather((RES * cotangent).astype(bf)), axis=1)
    residual = features.astype(f32)
    first_in = (residual * inverse_of(residual, 1) * gain_one).astype(bf)
    own_residual = pick(quarters(features, 0)).astype(f32)

    latents = jnp.concatenate(col_gather(dot(wide_down, first_in, ((0,), (1,)))), axis=0)
    query_latent, latent_part = latents[:QR], latents[QR : QR + KR]
    inverse_query, inverse_latent = inverse_of(query_latent, 0), inverse_of(latent_part, 0)
    query_in = (query_latent * inverse_query * query_scale).astype(bf)
    latent_in = (latent_part * inverse_latent * latent_scale).astype(bf)
    half = DR // 2
    key_front, key_back = rotate(latents[QR + KR : QR + KR + half], latents[QR + KR + half :], cosine, sine)
    key_part = jnp.concatenate([latent_in, key_front.astype(bf), key_back.astype(bf)], axis=0)
    key_parts = jnp.concatenate([from_behind(key_part, step) for step in range(reach, 0, -1)] + [key_part], axis=1)
    latent_all = key_parts[:KR]
    turned_t = jnp.concatenate([key_parts[KR : KR + half]] * 4 + [key_parts[KR + half :]] * 4, axis=0)
    turned = turned_t.T

    key_place = start - reach * count + jnp.arange(blocks * count, dtype=jnp.int32)
    place = start + jnp.arange(count, dtype=jnp.int32)
    key_doc = lax.dynamic_slice_in_dim(jnp.pad(document_ids, (reach * count, 0)), start, blocks * count)
    doc = lax.dynamic_slice_in_dim(document_ids, start, count)
    allowed = (key_doc[:, None] == doc[None, :]) & (key_place[:, None] <= place[None, :])
    allowed = allowed & (key_place[:, None] >= (place // SEQ_LEN * SEQ_LEN)[None, :])
    bias = jnp.where(allowed, 0.0, NEG).astype(f32)
    doc_start = jnp.sum((document_ids < doc[0]).astype(jnp.int32))
    first = jnp.clip((doc_start - (start - reach * count)) // BLOCK, 0, reach).reshape(1)

    raw = over_rows(wide_query_up, query_in)
    tiles = raw[wide:].reshape(-1, 2, 64, count)
    cos_tile, sin_tile = jnp.tile(cosine, (4, 1)), jnp.tile(sine, (4, 1))
    query_turned = jnp.stack(rotate(tiles[:, 0], tiles[:, 1], cos_tile, sin_tile), axis=1).reshape(-1, count)
    query = jnp.concatenate([raw[:wide], query_turned], axis=0).astype(bf)
    up_keys, up_values = wide_latent_up[:, :wide], wide_latent_up[:, wide:]
    keys = over_rows(latent_all, up_keys).astype(bf)
    values_t = over_rows(up_values, latent_all).astype(bf)
    out_t, lse = attend(first, query, keys, turned, values_t, bias, heads)

    branch = dot(out_t, wide_output, ((0,), (1,)))
    middle = own_residual + RES * col_scatter(quarters(branch, 0))
    inverse_second = inverse_of(middle, 1)
    second_in = jnp.concatenate(col_gather((middle * inverse_second * gain_two).astype(bf)), axis=0)

    gate = multiply(second_in, wide_gate)
    upward = multiply(second_in, wide_up)
    sigma = jax.nn.sigmoid(gate)
    hidden = (gate * sigma * upward).astype(bf)
    middle_own = jnp.concatenate(col_exchange(quarters(middle, 1)), axis=0)
    result = middle_own + RES * col_scatter(quarters(against(hidden, wide_back), 1))
    back_hidden = multiply(back_down, wide_back)
    back_gate = (back_hidden * upward * sigma * (1.0 + gate * (1.0 - sigma))).astype(bf)
    back_upward = (back_hidden * gate * sigma).astype(bf)
    ffn = (
        Scatter(second_in.T, back_gate),
        Scatter(second_in.T, back_upward),
        Scatter(back_down.T, hidden),
    )
    slope_gate, slope_up, slope_down = scatter_rows(*ffn)

    back_second = col_scatter(quarters(against(back_gate, wide_gate) + against(back_upward, wide_up), 0))
    back_norm, gain_second_part = norm_back(middle, inverse_second, gain_two, back_second, 1)
    back_middle = own_up + back_norm
    back_branch = jnp.concatenate(col_gather((RES * back_middle).astype(bf)), axis=0)

    out = out_t.T
    back_out = multiply(back_branch, wide_output).astype(bf)
    keys_t = over_rows(up_keys, latent_all).astype(bf)
    values = over_rows(latent_all, up_values).astype(bf)
    back_query_n, back_query_r, back_keys, back_values, back_turned = attend_back(
        first, query, query.T, keys, turned, keys_t, turned_t, values, back_out.T, back_out, bias, lse, heads
    )
    tiles = back_query_r.reshape(-1, 2, 64, count)
    back_turn = jnp.stack(rotate(tiles[:, 0], tiles[:, 1], cos_tile, -sin_tile), axis=1).reshape(-1, count)
    back_raw = jnp.concatenate([back_query_n, back_turn], axis=0).astype(bf)
    query_part = multiply(wide_query_up, back_raw)
    latent_back = against(up_keys, back_keys) + against(up_values, back_values)
    turned_back = jnp.sum(back_turned.T.reshape(2, 4, half, blocks * count), axis=1).reshape(DR, blocks * count)
    far = jnp.concatenate([latent_back, turned_back], axis=0)
    to_send = jnp.concatenate(
        [query_part] + [far[:, b * count : (b + 1) * count] for b in range(blocks)], axis=0
    )
    summed = col_scatter(quarters(to_send, 1))
    back_query_in = summed[:QR]
    wide_far = KR + DR
    parts = [summed[QR + b * wide_far : QR + (b + 1) * wide_far] for b in range(blocks)]
    back_key = parts[reach]
    for step in range(1, reach + 1):
        back_key = back_key + from_behind(parts[reach - step], -step)

    own_latents = pick(quarters(latents, 1))
    own_query, own_latent = own_latents[:QR], own_latents[QR : QR + KR]
    back_query_latent, query_gain_part = norm_back(
        own_query, inverse_of(own_query, 0), query_scale, back_query_in, 0
    )
    back_latent, latent_gain_part = norm_back(
        own_latent, inverse_of(own_latent, 0), latent_scale, back_key[:KR], 0
    )
    own_cosine, own_sine = pick(quarters(cosine, 1)), pick(quarters(sine, 1))
    back_front, back_behind = rotate(back_key[KR : KR + half], back_key[KR + half :], own_cosine, -own_sine)
    back_latents = jnp.concatenate([back_query_latent, back_latent, back_front, back_behind], axis=0).astype(bf)
    back_latents = jnp.concatenate(col_gather(back_latents), axis=1)
    back_slice = lax.dynamic_slice_in_dim(back_latents, column * slice_width, slice_width, 0)
    back_first = col_scatter(quarters(dot(back_slice, wide_down, ((0,), (1,))), 0))
    back_norm_first, gain_first_part = norm_back(own_residual, inverse_of(own_residual, 1), gain_one, back_first, 1)
    back_tokens = jnp.concatenate(col_exchange(quarters(back_middle + back_norm_first, 1)), axis=0)

    attention = (
        Scatter(back_branch.T, out),
        Scatter(query_in, back_raw, True),
        Scatter(latent_all, jnp.concatenate([back_keys, back_values], axis=1)),
        Scatter(first_in.T, back_slice, True),
    )
    slope_output, slope_query_up, slope_latent_up, slope_down_slice = scatter_rows(*attention)
    slope_both = jnp.concatenate(col_gather(slope_down_slice), axis=1)

    packed = jnp.concatenate(
        [part.reshape(rows, -1) for part in (gain_first_part, gain_second_part, query_gain_part, latent_gain_part)],
        axis=1,
    )
    bit = rows // 2
    while bit >= 1:
        upper = (row // bit) % 2 == 1
        low_half, high_half = packed[:bit], packed[bit:]
        away = jnp.where(upper, low_half, high_half)
        stay = jnp.where(upper, high_half, low_half)
        packed = stay + lax.ppermute(away, "row", [(r, r ^ bit) for r in range(rows)])
        bit //= 2
    packed = packed[0]
    bit = 1
    while bit < cols:
        packed = packed + swap_col(packed, bit)
        bit *= 2
    n = gain_first.shape[0]
    m = query_gain.shape[0]

    exact = functools.partial(
        lax.dot_general,
        dimension_numbers=(((1,), (1,)), ((), ())),
        precision=lax.Precision.HIGHEST,
        preferred_element_type=f32,
    )
    return (
        result,
        back_tokens,
        packed[:n],
        slope_both[:, :QR],
        packed[2 * n : 2 * n + m],
        slope_both[:, QR:],
        packed[2 * n + m :],
        exact(slope_query_up, query_one.astype(f32)),
        exact(slope_latent_up, latent_one.astype(f32)),
        slope_output.T,
        packed[n : 2 * n],
        slope_gate,
        slope_up,
        slope_down.T,
    )


def solution(mesh):
    placed = (
        P("row", "col"), P(), P("row"), P("row", None), P("row"), P("row", None), P("row"), P("row", "col"),
        P("row", "col"), P("col", "row"), P("row"), P("row", "col"), P("row", "col"), P("col", "row"),
        P("row", "col"),
    )
    outs = (
        P("row", "col"), P("row", "col"), P("row"), P("row", None), P("row"), P("row", None), P("row"),
        P("row", "col"), P("row", "col"), P("col", "row"), P("row"), P("row", "col"), P("row", "col"),
        P("col", "row"),
    )
    return jax.shard_map(shards, mesh=mesh, in_specs=placed, out_specs=outs, check_vma=False)
```

time: 3010 us -> 1520 us (0.50)
  waiting for transfers between devices: 2340 us -> 501 us
  starting transfers between devices: 46.8 us -> 340 us
  local copies, waits for them, and re-layouts: 45.7 us -> 292 us
  blocking collectives: 109 us -> 0 us
  matrix products: 311 us -> 234 us
  other arithmetic: 131 us -> 90 us
  Pallas kernels: 0 us -> 30.8 us
    reduce_scatter x8 -> x0, waiting for transfers between devices: 1290 us -> none  [the longest x1 292 us: shards(): lax.psum_scatter(slope_up_local, 'row', scatter_dimension=0, tiled=True)]
    all_gather x9 -> x0, waiting for transfers between devices: 457 us -> none  [the longest x1 129 us: shards(): lax.all_gather(halves[11], 'row', axis=1, tiled=True)]
    ppermute x16 -> x254, starting transfers between devices: 45.4 us -> 340 us  [the longest x98 153 us: advance(): arrived = lax.ppermute(self.moving[side], 'row', self.links[side])]
    psum x3 -> x0, waiting for transfers between devices: 235 us -> none  [the longest x1 101 us: shards(): lax.psum(against(back_gate, wide_gate) + against(back_upward, wide_up), '...]
    dynamic_update_slice x0 -> x112, local copies, waits for them, and re-layouts: none -> 200 us  [put(): lax.dynamic_update_slice(self.whole, self.moving[side][None, None], (orig...]
    ppermute x16 -> x254, waiting for transfers between devices: 343 us -> 501 us  [the longest x98 232 us: advance(): arrived = lax.ppermute(self.moving[side], 'row', self.links[side])]
    unnamed x2 -> x0, blocking collectives: 77.3 us -> none
    dot_general x57 -> x134, matrix products: 307 us -> 234 us  [the longest x112 128 us: part(): lax.dot_general(piece, self.right, (contract, ((), ())), preferred_elemen...]
  transfers between devices with their start and end apart: 37 -> 254, of which waited for: 22 -> 117; matrix products, arithmetic and copies ran while one was open for 9% -> 34% of each run, Pallas kernels for 0% -> 2%
where the time goes in v1:
time: 1520 us; the launch traced here: 1490 us
  waiting for transfers between devices  501 us (33%)
  starting transfers between devices  340 us (22%)
  local copies, waits for them, and re-layouts  292 us (19%)
  matrix products  234 us (15%)
  other arithmetic  90 us (6%)
  Pallas kernels  30.8 us (2%)
    ppermute x98, waiting for transfers between devices, advance(): arrived = lax.ppermute(self.moving[side], 'row', self.links[side])  232 us
    dynamic_update_slice x112, local copies, waits for them, and re-layouts, put(): lax.dynamic_update_slice(self.whole, self.moving[side][None, None], (orig...  200 us
    ppermute x98, waiting for transfers between devices, advance(): lax.ppermute(self.moving[side], 'row', self.links[side])  170 us
    ppermute x98, starting transfers between devices, advance(): arrived = lax.ppermute(self.moving[side], 'row', self.links[side])  153 us
    ppermute x98, starting transfers between devices, advance(): lax.ppermute(self.moving[side], 'row', self.links[side])  148 us
    dot_general x112, matrix products, part(): lax.dot_general(piece, self.right, (contract, ((), ())), preferred_elemen...  128 us
    dot_general x20, matrix products, dot(): lax.dot_general(left, right, (dims, ((), ())), preferred_element_type=f32)  99.3 us
    ppermute x47, waiting for transfers between devices, swap_col(): lax.ppermute(value, 'col', [(c, c ^ bit) for c in range(lax.axis_size('co...  79.4 us
  transfers between devices with their start and end apart: 254, of which 117 were waited for; matrix products, arithmetic and copies ran while one was open for 34% of the time, Pallas kernels for 2%

profile of v1, /device:TPU:0, one launch (start us, length us, event | category | flops | bytes accessed | tf_op | source)
XLA Modules:
  0.0 1492.5 jit_solution(18290198246849394232)
XLA Ops:
  193.6 10.1 collective-permute-done.23
  465.7 9.0 collective-permute-done.95
  578.5 10.9 attend.1
  601.0 11.1 collective-permute-start.86
  649.7 10.8 collective-permute-done.115
  670.7 9.6 fusion.42
  682.3 13.5 collective-permute-done.68
  700.4 14.1 collective-permute-done.72
  729.2 9.6 fusion.763
  738.8 14.6 multiply_convert_fusion.1
  809.9 10.4 fusion.780
  832.3 9.6 convolution_add_fusion
  869.4 20.9 %collective-permute-done.227 = bf16[160,1600]{1,0:T(8,128)(2,1)S(1)} collective-permute-done((bf16[160,1600]{1,0:T(8,128)(2,1)S(1)}, bf16[160,1600]{1,0:T(8,128)(2,1)S(1)}, u32[]{:S(2)}, u32[]{:S(2)}) %collective-permute-start.227) | collective-permute-done | bytes 512032 | tf_op jit(solution)/shard_map/ppermute | solution.py:103
  893.1 11.0 collective-permute-done.234
  905.5 11.5 collective-permute-done.213
  1000.8 8.7 collective-permute-done.244
  1056.8 20.0 %attend_back.1 = (f32[640,512]{1,0:T(8,128)}, f32[384,512]{1,0:T(8,128)}, bf16[2560,640]{1,0:T(8,128)(2,1)}, bf16[2560,640]{1,0:T(8,128)(2,1)}, f32[2560,128]{1,0:T(8,128)}) custom-call(s32[1]{0:T(128)} %bitcast.1.first_ref, bf16[1024,512]{1,0:T(8,128)(2,1)} %copy.89.qn_ref.qr_ref, bf16[1024,512]{1,0:T(8,128)(2,1)} %copy.89.qn_ref.qr_ref, ...), custom_call_target="tpu_custom_call" | custom-call | flops 33554432000 | bytes 33554432 | tf_op jit(solution)/shard_map/attend_back/pallas_call | solution.py:393
  1086.2 11.9 collective-permute-start.184
  1121.7 22.6 %collective-permute-done.191 = bf16[16,1280]{1,0:T(8,128)(2,1)S(1)} collective-permute-done((bf16[16,1280]{1,0:T(8,128)(2,1)S(1)}, bf16[16,1280]{1,0:T(8,128)(2,1)S(1)}, u32[]{:S(2)}, u32[]{:S(2)}) %collective-permute-start.191) | collective-permute-done | bytes 40992 | tf_op jit(solution)/shard_map/ppermute | solution.py:103
  1148.3 10.9 collective-permute-start.192
  1288.8 9.7 collective-permute-done.175
  1309.3 8.0 collective-permute-done.176
  1438.6 10.1 collective-permute-done.167
  1476.8 12.4 collective-permute-done.152
  (1262 shorter events, 1196.5 us)
Async XLA Ops:
  2.8 143.6 %collective-permute-start.52 = (bf16[160,640]{1,0:T(8,128)(2,1)}, bf16[160,640]{1,0:T(8,128)(2,1)}, u32[]{:S(2)}, u32[]{:S(2)}) collective-permute-start(bf16[160,640]{1,0:T(8,128)(2,1)} %get-tuple-element.186), channel_id=1, source_target_pairs={{0,8},{8,16},{16,24},{24,28},{28,20},{20,12},{12,4},{4,0},{1,9},{9... | collective-permute-start | bytes 614408 | tf_op jit(solution)/shard_map/ppermute | solution.py:64
  5.8 142.9 %collective-permute-start.53 = (bf16[160,640]{1,0:T(8,128)(2,1)}, bf16[160,640]{1,0:T(8,128)(2,1)}, u32[]{:S(2)}, u32[]{:S(2)}) collective-permute-start(bf16[160,640]{1,0:T(8,128)(2,1)} %get-tuple-element.185), channel_id=1, source_target_pairs={{8,0},{16,8},{24,16},{28,24},{20,28},{12,20},{4,12},{0,4},{9,1},{1... | collective-permute-start | bytes 614408 | tf_op jit(solution)/shard_map/ppermute | solution.py:64
  7.8 77.6 %collective-permute-start.17 = (bf16[160,267]{1,0:T(8,128)(2,1)}, bf16[160,267]{1,0:T(8,128)(2,1)}, u32[]{:S(2)}, u32[]{:S(2)}) collective-permute-start(bf16[160,267]{1,0:T(8,128)(2,1)} %get-tuple-element.190), channel_id=1, source_target_pairs={{0,8},{8,16},{16,24},{24,28},{28,20},{20,12},{12,4},{4,0},{1,9},{9... | collective-permute-start | bytes 256328 | tf_op jit(solution)/shard_map/ppermute | solution.py:64
  9.8 77.4 %collective-permute-start.18 = (bf16[160,267]{1,0:T(8,128)(2,1)}, bf16[160,267]{1,0:T(8,128)(2,1)}, u32[]{:S(2)}, u32[]{:S(2)}) collective-permute-start(bf16[160,267]{1,0:T(8,128)(2,1)} %get-tuple-element.187), channel_id=1, source_target_pairs={{8,0},{16,8},{24,16},{28,24},{20,28},{12,20},{4,12},{0,4},{9,1},{1... | collective-permute-start | bytes 256328 | tf_op jit(solution)/shard_map/ppermute | solution.py:64
  11.1 60.0 %collective-permute-start.38 = (bf16[16,1280]{1,0:T(8,128)(2,1)S(1)}, bf16[16,1280]{1,0:T(8,128)(2,1)}, u32[]{:S(2)}, u32[]{:S(2)}) collective-permute-start(bf16[16,1280]{1,0:T(8,128)(2,1)S(1)} %get-tuple-element.194), channel_id=1, source_target_pairs={{0,8},{8,16},{16,24},{24,28},{28,20},{20,12},{12,4},{4,0},{1,9},{9... | collective-permute-start | bytes 122888 | tf_op jit(solution)/shard_map/ppermute | solution.py:64
  116.4 266.0 %collective-permute-start = (bf16[512,640]{1,0:T(8,128)(2,1)}, bf16[512,640]{1,0:T(8,128)(2,1)}, u32[]{:S(2)}, u32[]{:S(2)}) collective-permute-start(bf16[512,640]{1,0:T(8,128)(2,1)} %param.15), channel_id=1, source_target_pairs={{0,2},{1,3},{2,0},{3,1},{4,6},{5,7},{6,4},{7,5},{8,10},{9,11},{10,... | collective-permute-start | bytes 1966088 | tf_op jit(solution)/shard_map/ppermute | solution.py:125
  118.2 70.7 %collective-permute-start.120 = (f32[128,640]{1,0:T(8,128)}, f32[128,640]{1,0:T(8,128)}, u32[]{:S(2)}, u32[]{:S(2)}) collective-permute-start(f32[128,640]{1,0:T(8,128)} %get-tuple-element.158), channel_id=1, source_target_pairs={{0,3},{1,2},{2,1},{3,0},{4,7},{5,6},{6,5},{7,4},{8,11},{9,10},{10,... | collective-permute-start | bytes 983048 | tf_op jit(solution)/shard_map/ppermute | solution.py:125
  187.0 66.0 %collective-permute-start.89 = (bf16[160,1600]{1,0:T(8,128)(2,1)}, bf16[160,1600]{1,0:T(8,128)(2,1)}, u32[]{:S(2)}, u32[]{:S(2)}) collective-permute-start(bf16[160,1600]{1,0:T(8,128)(2,1)} %get-tuple-element.176), channel_id=1, source_target_pairs={{0,8},{8,16},{16,24},{24,28},{28,20},{20,12},{12,4},{4,0},{1,9},{9... | collective-permute-start | bytes 1536008 | tf_op jit(solution)/shard_map/ppermute | solution.py:64
  231.7 184.3 %collective-permute-start.2 = (bf16[512,640]{1,0:T(8,128)(2,1)}, bf16[512,640]{1,0:T(8,128)(2,1)}, u32[]{:S(2)}, u32[]{:S(2)}) collective-permute-start(bf16[512,640]{1,0:T(8,128)(2,1)} %param.15), channel_id=1, source_target_pairs={{0,1},{1,0},{2,3},{3,2},{4,5},{5,4},{6,7},{7,6},{8,9},{9,8},{10,11... | collective-permute-start | bytes 1966088 | tf_op jit(solution)/shard_map/ppermute | solution.py:125
  302.6 79.7 %collective-permute-start.123 = (bf16[512,640]{1,0:T(8,128)(2,1)}, bf16[512,640]{1,0:T(8,128)(2,1)}, u32[]{:S(2)}, u32[]{:S(2)}) collective-permute-start(bf16[512,640]{1,0:T(8,128)(2,1)} %multiply_convert_fusion.5), channel_id=1, source_target_pairs={{0,2},{1,3},{2,0},{3,1},{4,6},{5,7},{6,4},{7,5},{8,10},{9,11},{10,... | collective-permute-start | bytes 1966088 | tf_op jit(solution)/shard_map/ppermute | solution.py:125
  546.1 67.8 %collective-permute-start.100 = (bf16[160,1600]{1,0:T(8,128)(2,1)}, bf16[160,1600]{1,0:T(8,128)(2,1)}, u32[]{:S(2)}, u32[]{:S(2)}) collective-permute-start(bf16[160,1600]{1,0:T(8,128)(2,1)} %collective-permute-done.98), channel_id=1, source_target_pairs={{8,0},{16,8},{24,16},{28,24},{20,28},{12,20},{4,12},{0,4},{9,1},{1... | collective-permute-start | bytes 1536008 | tf_op jit(solution)/shard_map/ppermute | solution.py:64
  548.1 67.7 %collective-permute-start.113 = (bf16[160,1600]{1,0:T(8,128)(2,1)}, bf16[160,1600]{1,0:T(8,128)(2,1)}, u32[]{:S(2)}, u32[]{:S(2)}) collective-permute-start(bf16[160,1600]{1,0:T(8,128)(2,1)} %collective-permute-done.111), channel_id=1, source_target_pairs={{0,8},{8,16},{16,24},{24,28},{28,20},{20,12},{12,4},{4,0},{1,9},{9... | collective-permute-start | bytes 1536008 | tf_op jit(solution)/shard_map/ppermute | solution.py:64
  550.8 67.4 %collective-permute-start.114 = (bf16[160,1600]{1,0:T(8,128)(2,1)}, bf16[160,1600]{1,0:T(8,128)(2,1)}, u32[]{:S(2)}, u32[]{:S(2)}) collective-permute-start(bf16[160,1600]{1,0:T(8,128)(2,1)} %collective-permute-done.112), channel_id=1, source_target_pairs={{8,0},{16,8},{24,16},{28,24},{20,28},{12,20},{4,12},{0,4},{9,1},{1... | collective-permute-start | bytes 1536008 | tf_op jit(solution)/shard_map/ppermute | solution.py:64
  558.6 69.5 %collective-permute-start.85 = (bf16[160,1600]{1,0:T(8,128)(2,1)}, bf16[160,1600]{1,0:T(8,128)(2,1)}, u32[]{:S(2)}, u32[]{:S(2)}) collective-permute-start(bf16[160,1600]{1,0:T(8,128)(2,1)} %collective-permute-done.83), channel_id=1, source_target_pairs={{0,8},{8,16},{16,24},{24,28},{28,20},{20,12},{12,4},{4,0},{1,9},{9... | collective-permute-start | bytes 1536008 | tf_op jit(solution)/shard_map/ppermute | solution.py:64
  615.8 66.5 %collective-permute-start.66 = (bf16[128,2560]{1,0:T(8,128)(2,1)S(1)}, bf16[128,2560]{1,0:T(8,128)(2,1)S(1)}, u32[]{:S(2)}, u32[]{:S(2)}) collective-permute-start(bf16[128,2560]{1,0:T(8,128)(2,1)S(1)} %get-tuple-element.112), channel_id=1, source_target_pairs={{0,1},{1,0},{2,3},{3,2},{4,5},{5,4},{6,7},{7,6},{8,9},{9,8},{10,11... | collective-permute-start | bytes 1966088 | tf_op jit(solution)/shard_map/ppermute | solution.py:125
  618.2 62.1 %collective-permute-start.101 = (bf16[160,1600]{1,0:T(8,128)(2,1)}, bf16[160,1600]{1,0:T(8,128)(2,1)S(1)}, u32[]{:S(2)}, u32[]{:S(2)}) collective-permute-start(bf16[160,1600]{1,0:T(8,128)(2,1)} %collective-permute-done.99), channel_id=1, source_target_pairs={{0,8},{8,16},{16,24},{24,28},{28,20},{20,12},{12,4},{4,0},{1,9},{9... | collective-permute-start | bytes 1536008 | tf_op jit(solution)/shard_map/ppermute | solution.py:64
  854.9 75.8 %collective-permute-start.126 = (bf16[128,2560]{1,0:T(8,128)(2,1)S(1)}, bf16[128,2560]{1,0:T(8,128)(2,1)S(1)}, u32[]{:S(2)}, u32[]{:S(2)}) collective-permute-start(bf16[128,2560]{1,0:T(8,128)(2,1)S(1)} %get-tuple-element.108), channel_id=1, source_target_pairs={{0,1},{1,0},{2,3},{3,2},{4,5},{5,4},{6,7},{7,6},{8,9},{9,8},{10,11... | collective-permute-start | bytes 1966088 | tf_op jit(solution)/shard_map/ppermute | solution.py:125
  862.6 78.1 %collective-permute-start.117 = (bf16[512,640]{1,0:T(8,128)(2,1)}, bf16[512,640]{1,0:T(8,128)(2,1)}, u32[]{:S(2)}, u32[]{:S(2)}) collective-permute-start(bf16[512,640]{1,0:T(8,128)(2,1)} %get-tuple-element.110), channel_id=1, source_target_pairs={{0,1},{1,0},{2,3},{3,2},{4,5},{5,4},{6,7},{7,6},{8,9},{9,8},{10,11... | collective-permute-start | bytes 1966088 | tf_op jit(solution)/shard_map/ppermute | solution.py:125
  958.9 77.2 %collective-permute-start.131 = (bf16[128,2560]{1,0:T(8,128)(2,1)S(1)}, bf16[128,2560]{1,0:T(8,128)(2,1)S(1)}, u32[]{:S(2)}, u32[]{:S(2)}) collective-permute-start(bf16[128,2560]{1,0:T(8,128)(2,1)S(1)} %get-tuple-element.90), channel_id=1, source_target_pairs={{0,1},{1,0},{2,3},{3,2},{4,5},{5,4},{6,7},{7,6},{8,9},{9,8},{10,11... | collective-permute-start | bytes 1966088 | tf_op jit(solution)/shard_map/ppermute | solution.py:125
  1023.0 246.4 %collective-permute-start.245 = (bf16[160,1600]{1,0:T(8,128)(2,1)}, bf16[160,1600]{1,0:T(8,128)(2,1)}, u32[]{:S(2)}, u32[]{:S(2)}) collective-permute-start(bf16[160,1600]{1,0:T(8,128)(2,1)} %add_convert_fusion.12), channel_id=1, source_target_pairs={{0,8},{8,16},{16,24},{24,28},{28,20},{20,12},{12,4},{4,0},{1,9},{9... | collective-permute-start | bytes 1536008 | tf_op jit(solution)/shard_map/ppermute | solution.py:103
  1032.3 246.6 %collective-permute-start.252 = (bf16[160,1600]{1,0:T(8,128)(2,1)}, bf16[160,1600]{1,0:T(8,128)(2,1)}, u32[]{:S(2)}, u32[]{:S(2)}) collective-permute-start(bf16[160,1600]{1,0:T(8,128)(2,1)} %add_convert_fusion.6), channel_id=1, source_target_pairs={{8,0},{16,8},{24,16},{28,24},{20,28},{12,20},{4,12},{0,4},{9,1},{1... | collective-permute-start | bytes 1536008 | tf_op jit(solution)/shard_map/ppermute | solution.py:103
  1034.4 237.0 %collective-permute-start.231 = (bf16[160,1600]{1,0:T(8,128)(2,1)}, bf16[160,1600]{1,0:T(8,128)(2,1)}, u32[]{:S(2)}, u32[]{:S(2)}) collective-permute-start(bf16[160,1600]{1,0:T(8,128)(2,1)} %add_convert_fusion.24), channel_id=1, source_target_pairs={{0,8},{8,16},{16,24},{24,28},{28,20},{20,12},{12,4},{4,0},{1,9},{9... | collective-permute-start | bytes 1536008 | tf_op jit(solution)/shard_map/ppermute | solution.py:103
  1036.1 236.7 %collective-permute-start.238 = (bf16[160,1600]{1,0:T(8,128)(2,1)}, bf16[160,1600]{1,0:T(8,128)(2,1)}, u32[]{:S(2)}, u32[]{:S(2)}) collective-permute-start(bf16[160,1600]{1,0:T(8,128)(2,1)} %add_convert_fusion.18), channel_id=1, source_target_pairs={{8,0},{16,8},{24,16},{28,24},{20,28},{12,20},{4,12},{0,4},{9,1},{1... | collective-permute-start | bytes 1536008 | tf_op jit(solution)/shard_map/ppermute | solution.py:103
  1272.9 87.1 %collective-permute-start.132 = (bf16[2208,128]{1,0:T(8,128)(2,1)S(1)}, bf16[2208,128]{1,0:T(8,128)(2,1)S(1)}, u32[]{:S(2)}, u32[]{:S(2)}) collective-permute-start(bf16[2208,128]{1,0:T(8,128)(2,1)S(1)} %get-tuple-element.114), channel_id=1, source_target_pairs={{0,1},{1,0},{2,3},{3,2},{4,5},{5,4},{6,7},{7,6},{8,9},{9,8},{10,11... | collective-permute-start | bytes 1695752 | tf_op jit(solution)/shard_map/ppermute | solution.py:125
  (382 other events, 6461.2 us)

commit v2 on v1

--- a/solution.py
+++ b/solution.py
@@ -22,6 +22,7 @@
 LOG2E = math.log2(math.e)
 SCALE = (DN + DR) ** (-0.5)
 VMEM_LIMIT = 56 << 20
+MESH = pl.DeviceIdType.MESH
 bf = jnp.bfloat16
 f32 = jnp.float32
 
@@ -35,84 +36,154 @@
     return 2 * (place + side * (rows - 1 - 2 * place)) + side
 
 
-def ring_links(rows):
-    order = [ring_row(p, rows) for p in range(rows)]
-    ahead = [(order[p], order[(p + 1) % rows]) for p in range(rows)]
-    return (ahead, [(b, a) for a, b in ahead])
-
-
-class Gather:
-    def __init__(self, block):
-        self.rows = lax.axis_size("row")
-        self.place = ring_place(lax.axis_index("row"), self.rows)
-        self.shape = block.shape
-        half = block.shape[0] // 2
-        self.links = ring_links(self.rows)
-        self.moving = [block[:half], block[half:]]
-        self.whole = jnp.zeros((self.rows, 2, half, block.shape[1]), block.dtype)
-        self.put(0)
-        self.step = 0
-
-    def put(self, step):
+def ring_barrier(ahead, behind, column):
+    barrier = pltpu.get_barrier_semaphore()
+    for other in (ahead, behind):
+        pl.semaphore_signal(barrier, inc=1, device_id=(other, column), device_id_type=MESH)
+    pl.semaphore_wait(barrier, 2)
+
+
+def ring_gather_kernel(rows, n, *refs):
+    blocks, wholes, (own_sem, send_sem, recv_sem) = refs[:n], refs[n : 2 * n], refs[2 * n :]
+    row, column = lax.axis_index("row"), lax.axis_index("col")
+    place = ring_place(row, rows)
+    ends = (ring_row((place + 1) % rows, rows), ring_row((place + rows - 1) % rows, rows))
+    ring_barrier(ends[0], ends[1], column)
+
+    def own(k):
+        return pltpu.make_async_copy(blocks[k], wholes[k].at[row], own_sem.at[k])
+
+    def hop(step, side, k):
+        origin = ring_row((place + (step if side else rows - step)) % rows, rows)
+        return pltpu.make_async_remote_copy(
+            src_ref=wholes[k].at[origin, side],
+            dst_ref=wholes[k].at[origin, side],
+            send_sem=send_sem.at[step, side, k],
+            recv_sem=recv_sem.at[step, side, k],
+            device_id=(ends[side], column),
+            device_id_type=MESH,
+        )
+
+    for k in range(n):
+        own(k).start()
+    for k in range(n):
+        own(k).wait()
         for side in (0, 1):
-            origin = ring_row((self.place + (step if side else self.rows - step)) % self.rows, self.rows)
-            self.whole = lax.dynamic_update_slice(
-                self.whole, self.moving[side][None, None], (origin, side, 0, 0)
-            )
-
-    def advance(self):
-        self.moving = [lax.ppermute(self.moving[side], "row", self.links[side]) for side in (0, 1)]
-        self.step += 1
-        self.put(self.step)
-
-    def result(self):
-        return self.whole.reshape(self.rows * self.shape[0], self.shape[1])
-
-
-def gather_rows(*blocks):
-    flows = [Gather(block) for block in blocks]
-    for _ in range(flows[0].rows - 1):
-        for flow in flows:
-            flow.advance()
-    return [flow.result() for flow in flows]
-
-
-class Scatter:
-    def __init__(self, left, right, transposed=False):
-        self.rows = lax.axis_size("row")
-        self.place = ring_place(lax.axis_index("row"), self.rows)
-        half = left.shape[0] // self.rows // 2
-        self.left = left.reshape(self.rows, 2, half, left.shape[1])
-        self.right = right
-        self.transposed = transposed
-        self.links = ring_links(self.rows)
-        self.moving = [self.part(0, side).astype(bf) for side in (0, 1)]
-        self.step = 0
-
-    def part(self, step, side):
-        place = self.place + 1 + step if side else self.place + 2 * self.rows - 1 - step
-        target = ring_row(place % self.rows, self.rows)
-        piece = lax.dynamic_slice(self.left, (target, side, 0, 0), (1, 1) + self.left.shape[2:])[0, 0]
-        contract = ((1,), (1,)) if self.transposed else ((1,), (0,))
-        return lax.dot_general(piece, self.right, (contract, ((), ())), preferred_element_type=f32)
-
-    def advance(self):
-        self.step += 1
-        last = self.step == self.rows - 1
+            hop(0, side, k).start()
+
+    def advance(step, carry):
+        for k in range(n):
+            for side in (0, 1):
+                hop(step - 1, side, k).wait_recv()
+                hop(step, side, k).start()
+        return carry
+
+    lax.fori_loop(1, rows - 1, advance, 0)
+    for k in range(n):
         for side in (0, 1):
-            arrived = lax.ppermute(self.moving[side], "row", self.links[side])
-            total = arrived.astype(f32) + self.part(self.step, side)
-            self.moving[side] = total if last else total.astype(bf)
-
-    def result(self):
-        return jnp.concatenate(self.moving, axis=0)
-
-
-def scatter_rows(*flows):
-    for _ in range(flows[0].rows - 1):
-        for flow in flows:
-            flow.advance()
-    return [flow.result() for flow in flows]
+            hop(rows - 2, side, k).wait_recv()
+
+    def drain(step, carry):
+        for k in range(n):
+            for side in (0, 1):
+                hop(step, side, k).wait_send()
+        return carry
+
+    lax.fori_loop(0, rows - 1, drain, 0)
+
+
+def ring_gather(*blocks):
+    rows, n = lax.axis_size("row"), len(blocks)
+    halves = [block.reshape(2, block.shape[0] // 2, block.shape[1]) for block in blocks]
+    wholes = pl.pallas_call(
+        functools.partial(ring_gather_kernel, rows, n),
+        out_shape=[jax.ShapeDtypeStruct((rows,) + half.shape, half.dtype) for half in halves],
+        in_specs=[pl.BlockSpec(memory_space=pl.ANY)] * n,
+        out_specs=[pl.BlockSpec(memory_space=pl.ANY)] * n,
+        scratch_shapes=[
+            pltpu.SemaphoreType.DMA((n,)),
+            pltpu.SemaphoreType.DMA((rows - 1, 2, n)),
+            pltpu.SemaphoreType.DMA((rows - 1, 2, n)),
+        ],
+        compiler_params=pltpu.CompilerParams(collective_id=0, has_side_effects=True),
+        name="ring_gather",
+    )(*halves)
+    return [whole.reshape(rows * block.shape[0], block.shape[1]) for whole, block in zip(wholes, blocks)]
+
+
+def ring_scatter_kernel(rows, n, *refs):
+    terms, sums, slots, (send_sem, recv_sem) = refs[:n], refs[n : 2 * n], refs[2 * n : 3 * n], refs[3 * n :]
+    row, column = lax.axis_index("row"), lax.axis_index("col")
+    place = ring_place(row, rows)
+    ends = (ring_row((place + 1) % rows, rows), ring_row((place + rows - 1) % rows, rows))
+    ring_barrier(ends[0], ends[1], column)
+
+    def target(step, side):
+        return ring_row((place + (1 + step if side else 2 * rows - 1 - step)) % rows, rows)
+
+    def hop(step, side, k, source):
+        return pltpu.make_async_remote_copy(
+            src_ref=source,
+            dst_ref=slots[k].at[step, side],
+            send_sem=send_sem.at[step, side, k],
+            recv_sem=recv_sem.at[step, side, k],
+            device_id=(ends[side], column),
+            device_id_type=MESH,
+        )
+
+    def first(side, k):
+        return hop(0, side, k, terms[k].at[target(0, side), side])
+
+    def later(step, side, k):
+        return hop(step, side, k, slots[k].at[step - 1, side])
+
+    for k in range(n):
+        for side in (0, 1):
+            first(side, k).start()
+
+    def arrive(step, side, k):
+        return hop(step, side, k, slots[k].at[step, side])
+
+    def advance(step, carry):
+        for k in range(n):
+            for side in (0, 1):
+                arrive(step - 1, side, k).wait_recv()
+                total = slots[k][step - 1, side].astype(f32) + terms[k][target(step, side), side].astype(f32)
+                slots[k][step - 1, side] = total.astype(bf)
+                later(step, side, k).start()
+        return carry
+
+    lax.fori_loop(1, rows - 1, advance, 0)
+    for k in range(n):
+        for side in (0, 1):
+            arrive(rows - 2, side, k).wait_recv()
+            sums[k][side] = slots[k][rows - 2, side].astype(f32) + terms[k][row, side].astype(f32)
+
+    def drain(step, carry):
+        for k in range(n):
+            for side in (0, 1):
+                arrive(step, side, k).wait_send()
+        return carry
+
+    lax.fori_loop(0, rows - 1, drain, 0)
+
+
+def ring_scatter(*terms):
+    rows, n = lax.axis_size("row"), len(terms)
+    split = [term.reshape(rows, 2, term.shape[0] // rows // 2, term.shape[1]) for term in terms]
+    sums = pl.pallas_call(
+        functools.partial(ring_scatter_kernel, rows, n),
+        out_shape=[jax.ShapeDtypeStruct(term.shape[1:], f32) for term in split],
+        in_specs=[pl.BlockSpec(memory_space=pltpu.VMEM)] * n,
+        out_specs=[pl.BlockSpec(memory_space=pltpu.VMEM)] * n,
+        scratch_shapes=[pltpu.VMEM((rows - 1,) + term.shape[1:], bf) for term in split]
+        + [pltpu.SemaphoreType.DMA((rows - 1, 2, n)), pltpu.SemaphoreType.DMA((rows - 1, 2, n))],
+        compiler_params=pltpu.CompilerParams(
+            collective_id=1, has_side_effects=True, vmem_limit_bytes=VMEM_LIMIT
+        ),
+        name="ring_scatter",
+    )(*split)
+    return [total.reshape(total.shape[0] * total.shape[1], total.shape[2]) for total in sums]
 
 
 def from_behind(value, steps):
@@ -125,12 +196,12 @@
     return lax.ppermute(value, "col", [(c, c ^ bit) for c in range(lax.axis_size("col"))])
 
 
-def by_owner(pieces):
-    column = lax.axis_index("col")
+def by_owner(pieces, own=None):
+    own = lax.axis_index("col") if own is None else own
     bit = 1
     pieces = list(pieces)
     while bit < len(pieces):
-        odd = (column // bit) % 2 == 1
+        odd = (own // bit) % 2 == 1
         pieces = [jnp.where(odd, pieces[k ^ bit], pieces[k]) for k in range(len(pieces))]
         bit *= 2
     return pieces
@@ -161,6 +232,115 @@
 
 def quarters(value, axis):
     return jnp.split(value, lax.axis_size("col"), axis=axis)
+
+
+PAIR = 2
+
+
+def group_row(group, side):
+    return (group // 2) * 4 + side * PAIR + group % 2
+
+
+def own_group():
+    row = lax.axis_index("row")
+    return ((row // 4) * 2 + row % 2, (row // PAIR) % 2)
+
+
+def swap_row(value, mask):
+    return lax.ppermute(value, "row", [(r, r ^ mask) for r in range(lax.axis_size("row"))])
+
+
+def group_masks():
+    bits = (lax.axis_size("row") // 2).bit_length() - 1
+    return [(1 << b, group_row(1 << b, 0)) for b in reversed(range(bits))]
+
+
+def after(value, other):
+    return lax.optimization_barrier((value, other))[0]
+
+
+def features_by_group(value):
+    rows = lax.axis_size("row")
+    chunks = jnp.split(value, rows, axis=1)
+    groups = [
+        jnp.concatenate([chunks[group_row(g, side)] for side in (0, 1)], axis=1) for g in range(rows // 2)
+    ]
+    return jnp.concatenate(by_owner(groups, own_group()[0]), axis=1)
+
+
+def features_in_order(value):
+    rows = lax.axis_size("row")
+    groups = by_owner(jnp.split(value, rows // 2, axis=1), own_group()[0])
+    chunks = [None] * rows
+    for g, group in enumerate(groups):
+        for side, chunk in enumerate(jnp.split(group, 2, axis=1)):
+            chunks[group_row(g, side)] = chunk
+    return jnp.concatenate(chunks, axis=1)
+
+
+def group_gather(own):
+    pieces = []
+    for piece in (own, swap_row(own, PAIR)):
+        across = swap_col(piece, 2)
+        pieces += [piece, swap_col(piece, 1), across, swap_col(across, 1)]
+    return jnp.concatenate(pieces, axis=0)
+
+
+def group_scatter(value):
+    x = jnp.split(value, 2 * lax.axis_size("col"), axis=0)
+    beside = swap_col(jnp.concatenate([x[1], x[3], x[5], x[7]], axis=0).astype(bf), 1).astype(f32)
+    y = [term + got for term, got in zip((x[0], x[2], x[4], x[6]), jnp.split(beside, 4, axis=0))]
+    across = swap_col(jnp.concatenate([y[1], y[3]], axis=0).astype(bf), 2).astype(f32)
+    z = [term + got for term, got in zip((y[0], y[2]), jnp.split(across, 2, axis=0))]
+    return z[0] + swap_row(z[1].astype(bf), PAIR).astype(f32)
+
+
+def gather_hidden(block, turn):
+    low, high = jnp.split(block, 2, axis=0)
+    upper = own_group()[1] == 1
+    mine = jnp.where(upper, high, low)
+    came = swap_row(jnp.where(upper, low, high), PAIR)
+    pieces = {0: jnp.concatenate([jnp.where(upper, came, mine), jnp.where(upper, mine, came)], axis=1)}
+    if turn is not None:
+        pieces[0] = after(pieces[0], turn)
+    first = None
+    for bit, mask in group_masks():
+        for k in list(pieces):
+            pieces[k ^ bit] = swap_row(pieces[k], mask)
+            first = pieces[k ^ bit] if first is None else first
+    return (jnp.concatenate([pieces[k] for k in range(len(pieces))], axis=1), first)
+
+
+def scatter_hidden(left, right, turn):
+    groups = lax.axis_size("row") // 2
+    chunks = jnp.split(right, groups, axis=1)
+    pieces = {}
+    kept = list(range(groups))
+    first = None
+    for bit, mask in reversed(group_masks()):
+        away, stay = [k for k in kept if k & bit], [k for k in kept if not k & bit]
+        for k in kept:
+            if k not in pieces:
+                pieces[k] = None
+        if first is None:
+            wide = lambda ks: jnp.concatenate([chunks[k] for k in ks], axis=1)
+            leaving = over_rows(left, wide(away)).astype(bf)
+            staying = over_rows(left, wide(stay))
+            if turn is not None:
+                leaving = after(leaving, turn)
+        else:
+            leaving = jnp.concatenate([pieces[k] for k in away], axis=1).astype(bf)
+            staying = jnp.concatenate([pieces[k] for k in stay], axis=1)
+        came = swap_row(leaving, mask)
+        first = came if first is None else first
+        total = staying + came.astype(f32)
+        pieces = dict(zip(stay, jnp.split(total, len(stay), axis=1)))
+        kept = stay
+    low, high = jnp.split(pieces[0], 2, axis=1)
+    upper = own_group()[1] == 1
+    mine = jnp.where(upper, high, low)
+    came = swap_row(jnp.where(upper, low, high).astype(bf), PAIR).astype(f32)
+    return (jnp.concatenate([jnp.where(upper, came, mine), jnp.where(upper, mine, came)], axis=0), first)
 
 
 def dot(left, right, dims):
@@ -433,12 +613,14 @@
     latent_one = chosen(latent_columns(heads), heads * (DN + DV))
     query_up_low = multiply(query_up.astype(bf), query_one.astype(bf)).astype(bf)
     latent_up_low = multiply(latent_up.astype(bf), latent_one.astype(bf)).astype(bf)
-    (wide_down,) = gather_rows(jnp.concatenate([down_slice, gains], axis=1))
-    wide_query_up, wide_latent_up = gather_rows(query_up_low, latent_up_low)
-    (wide_output,) = gather_rows(output_weight.astype(bf).T)
-    wide_gate, wide_up, wide_back = gather_rows(
-        gate_weight.astype(bf), up_weight.astype(bf), down_weight.astype(bf).T
-    )
+    down_block = jnp.concatenate([down_slice, gains], axis=1)
+    down_block = jnp.pad(down_block, ((0, 0), (0, -down_block.shape[1] % 128)))
+    wide_down, wide_query_up, wide_latent_up, wide_output = ring_gather(
+        down_block, query_up_low, latent_up_low, output_weight.astype(bf).T
+    )
+    gate_t, turn = gather_hidden(after(gate_weight.astype(bf).T, wide_down), None)
+    up_t, turn = gather_hidden(up_weight.astype(bf).T, turn)
+    wide_back, turn = gather_hidden(down_weight.astype(bf), turn)
     gain_one = wide_down[:, slice_width].astype(f32)
     gain_two = wide_down[:, slice_width + 1].astype(f32)
     small_gains = wide_down[:, slice_width + 2].reshape(rows, -1).astype(f32)
@@ -449,7 +631,7 @@
 
     features = jnp.concatenate(col_gather(tokens), axis=1)
     own_up = jnp.concatenate(col_exchange(quarters(cotangent, 0)), axis=1)
-    back_down = jnp.concatenate(col_gather((RES * cotangent).astype(bf)), axis=1)
+    back_down = group_gather(features_by_group((RES * own_up).astype(bf)))
     residual = features.astype(f32)
     first_in = (residual * inverse_of(residual, 1) * gain_one).astype(bf)
     own_residual = pick(quarters(features, 0)).astype(f32)
@@ -490,25 +672,21 @@
     branch = dot(out_t, wide_output, ((0,), (1,)))
     middle = own_residual + RES * col_scatter(quarters(branch, 0))
     inverse_second = inverse_of(middle, 1)
-    second_in = jnp.concatenate(col_gather((middle * inverse_second * gain_two).astype(bf)), axis=0)
-
-    gate = multiply(second_in, wide_gate)
-    upward = multiply(second_in, wide_up)
+    second_in = group_gather(features_by_group((middle * inverse_second * gain_two).astype(bf)))
+
+    gate = against(second_in, gate_t)
+    upward = against(second_in, up_t)
     sigma = jax.nn.sigmoid(gate)
     hidden = (gate * sigma * upward).astype(bf)
-    middle_own = jnp.concatenate(col_exchange(quarters(middle, 1)), axis=0)
-    result = middle_own + RES * col_scatter(quarters(against(hidden, wide_back), 1))
-    back_hidden = multiply(back_down, wide_back)
+    own_result = middle + RES * features_in_order(group_scatter(multiply(hidden, wide_back)))
+    result = jnp.concatenate(col_exchange(quarters(own_result, 1)), axis=0)
+    slope_down, turn = scatter_hidden(hidden, back_down, None)
+    back_hidden = against(back_down, wide_back)
     back_gate = (back_hidden * upward * sigma * (1.0 + gate * (1.0 - sigma))).astype(bf)
     back_upward = (back_hidden * gate * sigma).astype(bf)
-    ffn = (
-        Scatter(second_in.T, back_gate),
-        Scatter(second_in.T, back_upward),
-        Scatter(back_down.T, hidden),
-    )
-    slope_gate, slope_up, slope_down = scatter_rows(*ffn)
-
-    back_second = col_scatter(quarters(against(back_gate, wide_gate) + against(back_upward, wide_up), 0))
+    slope_gate, turn = scatter_hidden(back_gate, second_in, turn)
+    slope_up, turn = scatter_hidden(back_upward, second_in, turn)
+    back_second = features_in_order(group_scatter(multiply(back_gate, gate_t) + multiply(back_upward, up_t)))
     back_norm, gain_second_part = norm_back(middle, inverse_second, gain_two, back_second, 1)
     back_middle = own_up + back_norm
     back_branch = jnp.concatenate(col_gather((RES * back_middle).astype(bf)), axis=0)
@@ -555,13 +733,14 @@
     back_norm_first, gain_first_part = norm_back(own_residual, inverse_of(own_residual, 1), gain_one, back_first, 1)
     back_tokens = jnp.concatenate(col_exchange(quarters(back_middle + back_norm_first, 1)), axis=0)
 
-    attention = (
-        Scatter(back_branch.T, out),
-        Scatter(query_in, back_raw, True),
-        Scatter(latent_all, jnp.concatenate([back_keys, back_values], axis=1)),
-        Scatter(first_in.T, back_slice, True),
-    )
-    slope_output, slope_query_up, slope_latent_up, slope_down_slice = scatter_rows(*attention)
+    back_slice_n = jnp.pad(back_slice.T, ((0, 0), (0, -slice_width % 128)))
+    slope_output, slope_query_up, slope_latent_up, slope_down_slice = ring_scatter(
+        over_rows(back_branch, out).astype(bf),
+        against(query_in, back_raw).astype(bf),
+        multiply(latent_all, jnp.concatenate([back_keys, back_values], axis=1)).astype(bf),
+        over_rows(first_in, back_slice_n).astype(bf),
+    )
+    slope_down_slice = slope_down_slice[:, :slice_width]
     slope_both = jnp.concatenate(col_gather(slope_down_slice), axis=1)
 
     packed = jnp.concatenate(
@@ -602,9 +781,9 @@
         exact(slope_latent_up, latent_one.astype(f32)),
         slope_output.T,
         packed[n : 2 * n],
-        slope_gate,
-        slope_up,
-        slope_down.T,
+        slope_gate.T,
+        slope_up.T,
+        slope_down,
     )
 
 

time: 1520 us -> 1090 us (0.72); the launches traced: 1490 us -> 1090 us
  waiting for transfers between devices: 501 us -> 276 us
  Pallas kernels: 30.8 us -> 211 us
  starting transfers between devices: 340 us -> 181 us
  local copies, waits for them, and re-layouts: 292 us -> 140 us
  matrix products: 234 us -> 137 us
  other arithmetic: 90 us -> 142 us
    ppermute x196 -> x25, waiting for transfers between devices: 402 us -> 183 us  [swap_row(): lax.ppermute(value, 'row', [(r, r ^ mask) for r in range(lax.axis_size('r...]
    dynamic_update_slice x112 -> x0, local copies, waits for them, and re-layouts: 200 us -> none  [put(): lax.dynamic_update_slice(self.whole, self.moving[side][None, None], (orig...]
    pallas_call x0 -> x2, Pallas kernels: none -> 180 us  [the longest x1 99.5 us: ring_gather(): pl.pallas_call(functools.partial(ring_gather_kernel, rows, n), out_shape=...]
    ppermute x196 -> x25, starting transfers between devices: 301 us -> 131 us  [swap_row(): lax.ppermute(value, 'row', [(r, r ^ mask) for r in range(lax.axis_size('r...]
    dot_general x112 -> x0, matrix products: 128 us -> none  [part(): lax.dot_general(piece, self.right, (contract, ((), ())), preferred_elemen...]
    unnamed x318 -> x329, local copies, waits for them, and re-layouts: 16.7 us -> 55.3 us
    dot_general x20 -> x30, matrix products: 99.3 us -> 131 us  [dot(): lax.dot_general(left, right, (dims, ((), ())), preferred_element_type=f32)]
    ppermute x0 -> x12, local copies, waits for them, and re-layouts: none -> 31.1 us  [swap_row(): lax.ppermute(value, 'row', [(r, r ^ mask) for r in range(lax.axis_size('r...]
  transfers between devices with their start and end apart: 254 -> 87, of which waited for: 117 -> 26; matrix products, arithmetic and copies ran while one was open for 34% -> 32% of each run, Pallas kernels for 2% -> 19%
where the time goes in v2:
time: 1090 us
  waiting for transfers between devices  276 us (25%)
  Pallas kernels  211 us (19%)
  starting transfers between devices  181 us (17%)
  other arithmetic  142 us (13%)
  local copies, waits for them, and re-layouts  140 us (13%)
  matrix products  137 us (13%)
    ppermute x25, waiting for transfers between devices, swap_row(): lax.ppermute(value, 'row', [(r, r ^ mask) for r in range(lax.axis_size('r...  183 us
    ppermute x25, starting transfers between devices, swap_row(): lax.ppermute(value, 'row', [(r, r ^ mask) for r in range(lax.axis_size('r...  131 us
    dot_general x30, matrix products, dot(): lax.dot_general(left, right, (dims, ((), ())), preferred_element_type=f32)  131 us
    pallas_call x1, Pallas kernels, ring_gather(): pl.pallas_call(functools.partial(ring_gather_kernel, rows, n), out_shape=...  99.5 us
    pallas_call x1, Pallas kernels, ring_scatter(): pl.pallas_call(functools.partial(ring_scatter_kernel, rows, n), out_shape...  80.5 us
    ppermute x51, waiting for transfers between devices, swap_col(): lax.ppermute(value, 'col', [(c, c ^ bit) for c in range(lax.axis_size('co...  56.1 us
    unnamed x329, local copies, waits for them, and re-layouts  55.3 us
    ppermute x8, waiting for transfers between devices, from_behind(): lax.ppermute(value, 'row', [(source, source + steps) for source in range(...  32 us
  transfers between devices with their start and end apart: 87, of which 26 were waited for; matrix products, arithmetic and copies ran while one was open for 32% of the time, Pallas kernels for 19%

profile of v2, /device:TPU:0, one launch (start us, length us, event | category | flops | bytes accessed | tf_op | source)
XLA Modules:
  0.0 1091.7 jit_solution(3534615094261434168)
XLA Ops:
  17.8 99.5 %ring_gather.1 = (bf16[8,2,160,384]{3,2,1,0:T(8,128)(2,1)}, bf16[8,2,48,1024]{3,2,1,0:T(8,128)(2,1)}, bf16[8,2,16,1280]{3,2,1,0:T(8,128)(2,1)}, bf16[8,2,160,640]{3,2,1,0:T(8,128)(2,1)}) custom-call(bf16[2,160,384]{2,1,0:T(8,128)(2,1)} %bitcast.102, bf16[2,48,1024]{2,1,0:T(8,128)(2,1)} %bitcast.111, bf16[2,16,1280]{2,1,0:T(8,128)(2,1)} %bitcast.112, ...), custom_call_target="tpu_custom_call" | custom-call | tf_op jit(solution)/shard_map/ring_gather/pallas_call | solution.py:98
  157.6 11.0 %collective-permute-done.24 = bf16[800,320]{0,1:T(8,128)(2,1)S(1)} collective-permute-done((bf16[800,320]{0,1:T(8,128)(2,1)S(1)}, bf16[800,320]{0,1:T(8,128)(2,1)S(1)}, u32[]{:S(2)}, u32[]{:S(2)}) %collective-permute-start.24) | collective-permute-done | bytes 512032 | tf_op jit(solution)/shard_map/ppermute | solution.py:250
  170.5 9.2 collective-permute-done.20
  211.2 22.4 %collective-permute-done.22 = bf16[800,640]{1,0:T(8,128)(2,1)S(1)} collective-permute-done((bf16[800,640]{1,0:T(8,128)(2,1)}, bf16[800,640]{1,0:T(8,128)(2,1)S(1)}, u32[]{:S(2)}, u32[]{:S(2)}) %collective-permute-start.22) | collective-permute-done | bytes 1024032 | tf_op jit(solution)/shard_map/ppermute | solution.py:250
  278.8 26.3 %collective-permute-start.25 = (bf16[800,640]{1,0:T(8,128)(2,1)}, bf16[800,640]{1,0:T(8,128)(2,1)}, u32[]{:S(2)}, u32[]{:S(2)}) collective-permute-start(bf16[800,640]{1,0:T(8,128)(2,1)} %copy.152), channel_id=1, source_target_pairs={{0,4},{4,0},{8,12},{12,8},{16,20},{20,16},{24,28},{28,24},{1,5},{5... | collective-permute-start | bytes 3072008 | tf_op jit(solution)/shard_map/ppermute | solution.py:250
  319.7 11.2 %attend.1 = (bf16[640,512]{1,0:T(8,128)(2,1)}, f32[5,2,512]{2,1,0:T(2,128)}) custom-call(s32[1]{0:T(128)} %bitcast.1.first_ref, bf16[1024,512]{1,0:T(8,128)(2,1)} %copy.144.qn_ref.qr_ref, bf16[1024,512]{1,0:T(8,128)(2,1)} %copy.144.qn_ref.qr_ref, bf16[2560,640]{1,0:T(8,128)(2,1)} %convolution_convert_fusion.4.k_ref, bf16[2560,128]{1,0:T(8,128)(2,1)} %copy.146.kr_ref, ...), custom_call_target="tpu_custom_call" | custom-call | flops 13421772800 | bytes 16777216 | tf_op jit(solution)/shard_map/attend/pallas_call | solution.py:468
  341.4 39.5 %collective-permute-start.30 = (bf16[800,640]{1,0:T(8,128)(2,1)}, bf16[800,640]{1,0:T(8,128)(2,1)}, u32[]{:S(2)}, u32[]{:S(2)}) collective-permute-start(bf16[800,640]{1,0:T(8,128)(2,1)} %copy.157), channel_id=1, source_target_pairs={{0,16},{4,20},{8,24},{12,28},{16,0},{20,4},{24,8},{28,12},{1,17},{... | collective-permute-start | bytes 3072008 | tf_op jit(solution)/shard_map/ppermute | solution.py:250
  409.9 11.3 %collective-permute-start.31 = (bf16[800,640]{1,0:T(8,128)(2,1)}, bf16[800,640]{1,0:T(8,128)(2,1)S(1)}, u32[]{:S(2)}, u32[]{:S(2)}) collective-permute-start(bf16[800,640]{1,0:T(8,128)(2,1)} %collective-permute-done.30), channel_id=1, source_target_pairs={{0,4},{4,0},{8,12},{12,8},{16,20},{20,16},{24,28},{28,24},{1,5},{5... | collective-permute-start | bytes 3072008 | tf_op jit(solution)/shard_map/ppermute | solution.py:250
  440.8 11.4 %collective-permute-done.31 = bf16[800,640]{1,0:T(8,128)(2,1)S(1)} collective-permute-done((bf16[800,640]{1,0:T(8,128)(2,1)}, bf16[800,640]{1,0:T(8,128)(2,1)S(1)}, u32[]{:S(2)}, u32[]{:S(2)}) %collective-permute-start.31) | collective-permute-done | bytes 1024032 | tf_op jit(solution)/shard_map/ppermute | solution.py:250
  454.1 9.8 fusion.47
  467.9 13.4 %collective-permute-done.18 = bf16[128,2560]{1,0:T(8,128)(2,1)S(1)} collective-permute-done((bf16[128,2560]{1,0:T(8,128)(2,1)}, bf16[128,2560]{1,0:T(8,128)(2,1)S(1)}, u32[]{:S(2)}, u32[]{:S(2)}) %collective-permute-start.18) | collective-permute-done | bytes 655392 | tf_op jit(solution)/shard_map/ppermute | solution.py:196
  499.9 11.9 %fusion.49 = f32[1024,2560]{1,0:T(8,128)} fusion(bf16[1024,800]{0,1:T(8,128)(2,1)S(1)} %get-tuple-element.159, bf16[800,640]{0,1:T(8,128)(2,1)S(1)} %copy-done.77, bf16[800,640]{0,1:T(8,128)(2,1)S(1)} %copy-done.74, bf16[800,640]{0,1:T(8,128)(2,1)S(1)} %copy-done.75, bf16[800,640]{0,1:T(8,128)(2,1)S(1)} %copy-done.32), kind=kOutput, calls=%fused_computation.179 | convolution fusion | flops 4210688000 | bytes 16220160 | tf_op jit(solution)/shard_map/dot_general | solution.py:347
  511.8 11.2 %fusion.186 = (bf16[1024,2560]{1,0:T(8,128)(2,1)S(1)}, f32[1024,2560]{1,0:T(8,128)}) fusion(f32[1024,2560]{1,0:T(8,128)} %fusion.49, bf16[1024,800]{0,1:T(8,128)(2,1)} %get-tuple-element.157, bf16[800,2560]{1,0:T(8,128)(2,1)S(1)} %copy-done.35), kind=kOutput, calls=%fused_computation.591 | convolution fusion | flops 4199546880 | bytes 31948800 | tf_op jit(solution)/shard_map/dot_general | solution.py:347
  525.6 11.9 %fusion.187 = (bf16[1024,2560]{1,0:T(8,128)(2,1)S(1)}, f32[1024,2560]{1,0:T(8,128)}) fusion(bf16[1024,800]{0,1:T(8,128)(2,1)} %get-tuple-element.158, bf16[800,640]{0,1:T(8,128)(2,1)} %copy.161, bf16[800,640]{0,1:T(8,128)(2,1)S(1)} %copy-done.76, bf16[800,640]{0,1:T(8,128)(2,1)} %copy.159, bf16[800,640]{0,1:T(8,128)(2,1)S(1)} %copy-done.30), kind=kOutput, calls=%fused_computation.592 | convolution fusion | flops 4213309440 | bytes 21463040 | tf_op jit(solution)/shard_map/dot_general | solution.py:347
  550.0 37.8 %collective-permute-done.78 = bf16[800,1280]{1,0:T(8,128)(2,1)S(1)} collective-permute-done((bf16[800,1280]{1,0:T(8,128)(2,1)S(1)}, bf16[800,1280]{1,0:T(8,128)(2,1)S(1)}, u32[]{:S(2)}, u32[]{:S(2)}) %collective-permute-start.78) | collective-permute-done | bytes 2048032 | tf_op jit(solution)/shard_map/ppermute | solution.py:250
  619.1 23.8 %collective-permute-done.85 = bf16[800,640]{1,0:T(8,128)(2,1)} collective-permute-done((bf16[800,640]{1,0:T(8,128)(2,1)}, bf16[800,640]{1,0:T(8,128)(2,1)}, u32[]{:S(2)}, u32[]{:S(2)}) %collective-permute-start.85) | collective-permute-done | bytes 1024032 | tf_op jit(solution)/shard_map/ppermute | solution.py:250
  652.4 9.6 collective-permute-done.86
  668.4 10.3 collective-permute-done.33
  720.4 23.9 %collective-permute-done.80 = bf16[800,640]{1,0:T(8,128)(2,1)} collective-permute-done((bf16[800,640]{1,0:T(8,128)(2,1)}, bf16[800,640]{1,0:T(8,128)(2,1)}, u32[]{:S(2)}, u32[]{:S(2)}) %collective-permute-start.80) | collective-permute-done | bytes 1024032 | tf_op jit(solution)/shard_map/ppermute | solution.py:250
  771.2 20.2 %attend_back.1 = (f32[640,512]{1,0:T(8,128)}, f32[384,512]{1,0:T(8,128)}, bf16[2560,640]{1,0:T(8,128)(2,1)}, bf16[2560,640]{1,0:T(8,128)(2,1)}, f32[2560,128]{1,0:T(8,128)}) custom-call(s32[1]{0:T(128)} %bitcast.1.first_ref, bf16[1024,512]{1,0:T(8,128)(2,1)} %copy.144.qn_ref.qr_ref, bf16[1024,512]{1,0:T(8,128)(2,1)} %copy.144.qn_ref.qr_ref, ...), custom_call_target="tpu_custom_call" | custom-call | flops 33554432000 | bytes 33554432 | tf_op jit(solution)/shard_map/attend_back/pallas_call | solution.py:573
  836.7 33.5 %collective-permute-start.83 = (bf16[800,640]{1,0:T(8,128)(2,1)S(1)}, bf16[800,640]{1,0:T(8,128)(2,1)S(1)}, u32[]{:S(2)}, u32[]{:S(2)}) collective-permute-start(bf16[800,640]{1,0:T(8,128)(2,1)S(1)} %copy.174), channel_id=1, source_target_pairs={{0,16},{4,20},{8,24},{12,28},{16,0},{20,4},{24,8},{28,12},{1,17},{... | collective-permute-start | bytes 3072008 | tf_op jit(solution)/shard_map/ppermute | solution.py:250
  879.1 25.8 %collective-permute-done.60 = f32[288,128]{1,0:T(8,128)S(1)} collective-permute-done((f32[288,128]{1,0:T(8,128)S(1)}, f32[288,128]{1,0:T(8,128)S(1)}, u32[]{:S(2)}, u32[]{:S(2)}) %collective-permute-start.60) | collective-permute-done | bytes 147488 | tf_op jit(solution)/shard_map/ppermute | solution.py:192
  941.1 80.5 %ring_scatter.1 = (f32[2,160,640]{2,1,0:T(8,128)}, f32[2,48,1024]{2,1,0:T(8,128)}, f32[2,16,1280]{2,1,0:T(8,128)}, f32[2,160,384]{2,1,0:T(8,128)}) custom-call(bf16[8,2,160,640]{3,2,1,0:T(8,128)(2,1)} %bitcast.92, bf16[8,2,48,1024]{3,2,1,0:T(8,128)(2,1)} %bitcast.97, bf16[8,2,16,1280]{3,2,1,0:T(8,128)(2,1)} %bitcast.105, bf16[8,2,160,384]{3,2,1,0:T(8,128)(2,1)} %bitcast.94), custom_call_target="tpu_custom_call" | custom-call | tf_op jit(solution)/shard_map/ring_scatter/pallas_call | solution.py:174
  1074.6 11.5 %collective-permute-done.74 = f32[768]{0:T(1024)S(1)} collective-permute-done((f32[768]{0:T(1024)S(1)}, f32[768]{0:T(1024)S(1)}, u32[]{:S(2)}, u32[]{:S(2)}) %collective-permute-start.74) | collective-permute-done | bytes 3104 | tf_op jit(solution)/shard_map/ppermute | solution.py:196
  (739 shorter events, 511.0 us)
Async XLA Ops:
  0.7 186.6 %collective-permute-start = (bf16[512,640]{1,0:T(8,128)(2,1)}, bf16[512,640]{1,0:T(8,128)(2,1)}, u32[]{:S(2)}, u32[]{:S(2)}) collective-permute-start(bf16[512,640]{1,0:T(8,128)(2,1)} %param.15), channel_id=1, source_target_pairs={{0,2},{1,3},{2,0},{3,1},{4,6},{5,7},{6,4},{7,5},{8,10},{9,11},{10,... | collective-permute-start | bytes 1966088 | tf_op jit(solution)/shard_map/ppermute | solution.py:196
  3.7 190.6 %collective-permute-start.2 = (bf16[512,640]{1,0:T(8,128)(2,1)}, bf16[512,640]{1,0:T(8,128)(2,1)}, u32[]{:S(2)}, u32[]{:S(2)}) collective-permute-start(bf16[512,640]{1,0:T(8,128)(2,1)} %param.15), channel_id=1, source_target_pairs={{0,1},{1,0},{2,3},{3,2},{4,5},{5,4},{6,7},{7,6},{8,9},{9,8},{10,11... | collective-permute-start | bytes 1966088 | tf_op jit(solution)/shard_map/ppermute | solution.py:196
  6.2 134.2 %collective-permute-start.38 = (f32[128,640]{1,0:T(8,128)}, f32[128,640]{1,0:T(8,128)}, u32[]{:S(2)}, u32[]{:S(2)}) collective-permute-start(f32[128,640]{1,0:T(8,128)} %get-tuple-element.236), channel_id=1, source_target_pairs={{0,3},{1,2},{2,1},{3,0},{4,7},{5,6},{6,5},{7,4},{8,11},{9,10},{10,... | collective-permute-start | bytes 983048 | tf_op jit(solution)/shard_map/ppermute | solution.py:196
  6.4 135.6 %collective-permute-start.39 = (f32[128,640]{1,0:T(8,128)}, f32[128,640]{1,0:T(8,128)}, u32[]{:S(2)}, u32[]{:S(2)}) collective-permute-start(f32[128,640]{1,0:T(8,128)} %get-tuple-element.237), channel_id=1, source_target_pairs={{0,2},{1,3},{2,0},{3,1},{4,6},{5,7},{6,4},{7,5},{8,10},{9,11},{10,... | collective-permute-start | bytes 983048 | tf_op jit(solution)/shard_map/ppermute | solution.py:196
  8.4 134.1 %collective-permute-start.40 = (f32[128,640]{1,0:T(8,128)}, f32[128,640]{1,0:T(8,128)}, u32[]{:S(2)}, u32[]{:S(2)}) collective-permute-start(f32[128,640]{1,0:T(8,128)} %get-tuple-element.235), channel_id=1, source_target_pairs={{0,1},{1,0},{2,3},{3,2},{4,5},{5,4},{6,7},{7,6},{8,9},{9,8},{10,11... | collective-permute-start | bytes 983048 | tf_op jit(solution)/shard_map/ppermute | solution.py:196
  187.3 46.4 %collective-permute-start.22 = (bf16[800,640]{1,0:T(8,128)(2,1)}, bf16[800,640]{1,0:T(8,128)(2,1)S(1)}, u32[]{:S(2)}, u32[]{:S(2)}) collective-permute-start(bf16[800,640]{1,0:T(8,128)(2,1)} %copy.148), channel_id=1, source_target_pairs={{0,16},{4,20},{8,24},{12,28},{16,0},{20,4},{24,8},{28,12},{1,17},{... | collective-permute-start | bytes 3072008 | tf_op jit(solution)/shard_map/ppermute | solution.py:250
  190.8 196.3 %collective-permute-start.21 = (bf16[800,640]{1,0:T(8,128)(2,1)}, bf16[800,640]{1,0:T(8,128)(2,1)}, u32[]{:S(2)}, u32[]{:S(2)}) collective-permute-start(bf16[800,640]{1,0:T(8,128)(2,1)} %copy.148), channel_id=1, source_target_pairs={{0,4},{4,0},{8,12},{12,8},{16,20},{20,16},{24,28},{28,24},{1,5},{5... | collective-permute-start | bytes 3072008 | tf_op jit(solution)/shard_map/ppermute | solution.py:250
  241.4 97.7 %collective-permute-start.26 = (bf16[800,640]{1,0:T(8,128)(2,1)}, bf16[800,640]{1,0:T(8,128)(2,1)}, u32[]{:S(2)}, u32[]{:S(2)}) collective-permute-start(bf16[800,640]{1,0:T(8,128)(2,1)} %copy.152), channel_id=1, source_target_pairs={{0,16},{4,20},{8,24},{12,28},{16,0},{20,4},{24,8},{28,12},{1,17},{... | collective-permute-start | bytes 3072008 | tf_op jit(solution)/shard_map/ppermute | solution.py:250
  278.8 104.6 %collective-permute-start.25 = (bf16[800,640]{1,0:T(8,128)(2,1)}, bf16[800,640]{1,0:T(8,128)(2,1)}, u32[]{:S(2)}, u32[]{:S(2)}) collective-permute-start(bf16[800,640]{1,0:T(8,128)(2,1)} %copy.152), channel_id=1, source_target_pairs={{0,4},{4,0},{8,12},{12,8},{16,20},{20,16},{24,28},{28,24},{1,5},{5... | collective-permute-start | bytes 3072008 | tf_op jit(solution)/shard_map/ppermute | solution.py:250
  306.1 81.7 %collective-permute-start.23 = (bf16[800,640]{1,0:T(8,128)(2,1)}, bf16[800,640]{1,0:T(8,128)(2,1)}, u32[]{:S(2)}, u32[]{:S(2)}) collective-permute-start(bf16[800,640]{1,0:T(8,128)(2,1)} %copy-done.80), channel_id=1, source_target_pairs={{0,4},{4,0},{8,12},{12,8},{16,20},{20,16},{24,28},{28,24},{1,5},{5... | collective-permute-start | bytes 3072008 | tf_op jit(solution)/shard_map/ppermute | solution.py:250
  337.9 57.3 %collective-permute-start.11 = (bf16[128,2560]{1,0:T(8,128)(2,1)}, bf16[128,2560]{1,0:T(8,128)(2,1)}, u32[]{:S(2)}, u32[]{:S(2)}) collective-permute-start(bf16[128,2560]{1,0:T(8,128)(2,1)} %get-tuple-element.179), channel_id=1, source_target_pairs={{0,1},{1,0},{2,3},{3,2},{4,5},{5,4},{6,7},{7,6},{8,9},{9,8},{10,11... | collective-permute-start | bytes 1966088 | tf_op jit(solution)/shard_map/ppermute | solution.py:196
  341.4 68.5 %collective-permute-start.30 = (bf16[800,640]{1,0:T(8,128)(2,1)}, bf16[800,640]{1,0:T(8,128)(2,1)}, u32[]{:S(2)}, u32[]{:S(2)}) collective-permute-start(bf16[800,640]{1,0:T(8,128)(2,1)} %copy.157), channel_id=1, source_target_pairs={{0,16},{4,20},{8,24},{12,28},{16,0},{20,4},{24,8},{28,12},{1,17},{... | collective-permute-start | bytes 3072008 | tf_op jit(solution)/shard_map/ppermute | solution.py:250
  387.1 44.0 %collective-permute-start.27 = (bf16[800,640]{1,0:T(8,128)(2,1)}, bf16[800,640]{1,0:T(8,128)(2,1)}, u32[]{:S(2)}, u32[]{:S(2)}) collective-permute-start(bf16[800,640]{1,0:T(8,128)(2,1)} %collective-permute-done.26), channel_id=1, source_target_pairs={{0,4},{4,0},{8,12},{12,8},{16,20},{20,16},{24,28},{28,24},{1,5},{5... | collective-permute-start | bytes 3072008 | tf_op jit(solution)/shard_map/ppermute | solution.py:250
  525.1 77.7 %collective-permute-start.48 = (bf16[512,2560]{1,0:T(8,128)(2,1)}, bf16[512,2560]{1,0:T(8,128)(2,1)}, u32[]{:S(2)}, u32[]{:S(2)}) collective-permute-start(bf16[512,2560]{1,0:T(8,128)(2,1)} %pad_maximum_fusion.4), channel_id=1, source_target_pairs={{0,1},{1,0},{2,3},{3,2},{4,5},{5,4},{6,7},{7,6},{8,9},{9,8},{10,11... | collective-permute-start | bytes 7864328 | tf_op jit(solution)/shard_map/ppermute | solution.py:196
  541.2 46.6 %collective-permute-start.78 = (bf16[800,1280]{1,0:T(8,128)(2,1)S(1)}, bf16[800,1280]{1,0:T(8,128)(2,1)S(1)}, u32[]{:S(2)}, u32[]{:S(2)}) collective-permute-start(bf16[800,1280]{1,0:T(8,128)(2,1)S(1)} %convolution_convert_fusion.7), channel_id=1, source_target_pairs={{0,4},{4,0},{8,12},{12,8},{16,20},{20,16},{24,28},{28,24},{1,5},{5... | collective-permute-start | bytes 6144008 | tf_op jit(solution)/shard_map/ppermute | solution.py:250
  544.4 67.4 %collective-permute-start.32 = (bf16[512,2560]{1,0:T(8,128)(2,1)}, bf16[512,2560]{1,0:T(8,128)(2,1)}, u32[]{:S(2)}, u32[]{:S(2)}) collective-permute-start(bf16[512,2560]{1,0:T(8,128)(2,1)} %pad_maximum_fusion.3), channel_id=1, source_target_pairs={{0,1},{1,0},{2,3},{3,2},{4,5},{5,4},{6,7},{7,6},{8,9},{9,8},{10,11... | collective-permute-start | bytes 7864328 | tf_op jit(solution)/shard_map/ppermute | solution.py:196
  587.8 95.9 %collective-permute-start.79 = (bf16[800,1280]{1,0:T(8,128)(2,1)}, bf16[800,1280]{1,0:T(8,128)(2,1)}, u32[]{:S(2)}, u32[]{:S(2)}) collective-permute-start(bf16[800,1280]{1,0:T(8,128)(2,1)} %convolution_convert_fusion.8), channel_id=1, source_target_pairs={{0,4},{4,0},{8,12},{12,8},{16,20},{20,16},{24,28},{28,24},{1,5},{5... | collective-permute-start | bytes 6144008 | tf_op jit(solution)/shard_map/ppermute | solution.py:250
  610.3 53.2 %collective-permute-start.49 = (bf16[256,2560]{1,0:T(8,128)(2,1)}, bf16[256,2560]{1,0:T(8,128)(2,1)}, u32[]{:S(2)}, u32[]{:S(2)}) collective-permute-start(bf16[256,2560]{1,0:T(8,128)(2,1)} %pad_maximum_fusion.19), channel_id=1, source_target_pairs={{0,2},{1,3},{2,0},{3,1},{4,6},{5,7},{6,4},{7,5},{8,10},{9,11},{10,... | collective-permute-start | bytes 3932168 | tf_op jit(solution)/shard_map/ppermute | solution.py:196
  697.8 46.5 %collective-permute-start.80 = (bf16[800,640]{1,0:T(8,128)(2,1)}, bf16[800,640]{1,0:T(8,128)(2,1)}, u32[]{:S(2)}, u32[]{:S(2)}) collective-permute-start(bf16[800,640]{1,0:T(8,128)(2,1)} %copy.170), channel_id=1, source_target_pairs={{0,16},{4,20},{8,24},{12,28},{16,0},{20,4},{24,8},{28,12},{1,17},{... | collective-permute-start | bytes 3072008 | tf_op jit(solution)/shard_map/ppermute | solution.py:250
  751.3 71.2 %collective-permute-start.82 = (bf16[800,1280]{1,0:T(8,128)(2,1)}, bf16[800,1280]{1,0:T(8,128)(2,1)}, u32[]{:S(2)}, u32[]{:S(2)}) collective-permute-start(bf16[800,1280]{1,0:T(8,128)(2,1)} %convolution_convert_fusion.6), channel_id=1, source_target_pairs={{0,4},{4,0},{8,12},{12,8},{16,20},{20,16},{24,28},{28,24},{1,5},{5... | collective-permute-start | bytes 6144008 | tf_op jit(solution)/shard_map/ppermute | solution.py:250
  815.6 54.6 %collective-permute-start.54 = (bf16[2208,128]{1,0:T(8,128)(2,1)}, bf16[2208,128]{1,0:T(8,128)(2,1)}, u32[]{:S(2)}, u32[]{:S(2)}) collective-permute-start(bf16[2208,128]{1,0:T(8,128)(2,1)} %get-tuple-element.180), channel_id=1, source_target_pairs={{0,1},{1,0},{2,3},{3,2},{4,5},{5,4},{6,7},{7,6},{8,9},{9,8},{10,11... | collective-permute-start | bytes 1695752 | tf_op jit(solution)/shard_map/ppermute | solution.py:196
  836.7 79.4 %collective-permute-start.83 = (bf16[800,640]{1,0:T(8,128)(2,1)S(1)}, bf16[800,640]{1,0:T(8,128)(2,1)S(1)}, u32[]{:S(2)}, u32[]{:S(2)}) collective-permute-start(bf16[800,640]{1,0:T(8,128)(2,1)S(1)} %copy.174), channel_id=1, source_target_pairs={{0,16},{4,20},{8,24},{12,28},{16,0},{20,4},{24,8},{28,12},{1,17},{... | collective-permute-start | bytes 3072008 | tf_op jit(solution)/shard_map/ppermute | solution.py:250
  924.0 101.1 %collective-permute-start.84 = (bf16[800,320]{0,1:T(8,128)(2,1)}, bf16[800,320]{0,1:T(8,128)(2,1)}, u32[]{:S(2)}, u32[]{:S(2)}) collective-permute-start(bf16[800,320]{0,1:T(8,128)(2,1)} %select_convert_fusion.5), channel_id=1, source_target_pairs={{0,8},{4,12},{8,0},{12,4},{16,24},{20,28},{24,16},{28,20},{1,9},{5... | collective-permute-start | bytes 1536008 | tf_op jit(solution)/shard_map/ppermute | solution.py:250
  935.7 99.2 %collective-permute-start.65 = (bf16[128,2560]{1,0:T(8,128)(2,1)}, bf16[128,2560]{1,0:T(8,128)(2,1)}, u32[]{:S(2)}, u32[]{:S(2)}) collective-permute-start(bf16[128,2560]{1,0:T(8,128)(2,1)} %get-tuple-element.169), channel_id=1, source_target_pairs={{0,1},{1,0},{2,3},{3,2},{4,5},{5,4},{6,7},{7,6},{8,9},{9,8},{10,11... | collective-permute-start | bytes 1966088 | tf_op jit(solution)/shard_map/ppermute | solution.py:196
  (213 other events, 3476.7 us)

commit v3 on v2

--- a/solution.py
+++ b/solution.py
@@ -36,19 +36,51 @@
     return 2 * (place + side * (rows - 1 - 2 * place)) + side
 
 
-def ring_barrier(ahead, behind, column):
+def flip(value, bit):
+    return value + bit * (1 - 2 * ((value // bit) % 2))
+
+
+def ring_barrier(others):
     barrier = pltpu.get_barrier_semaphore()
-    for other in (ahead, behind):
-        pl.semaphore_signal(barrier, inc=1, device_id=(other, column), device_id_type=MESH)
-    pl.semaphore_wait(barrier, 2)
+    for other in others:
+        pl.semaphore_signal(barrier, inc=1, device_id=other, device_id_type=MESH)
+    pl.semaphore_wait(barrier, len(others))
 
 
 def ring_gather_kernel(rows, n, *refs):
-    blocks, wholes, (own_sem, send_sem, recv_sem) = refs[:n], refs[n : 2 * n], refs[2 * n :]
+    blocks, (tokens_ref, back_ref), refs = refs[:n], refs[n : n + 2], refs[n + 2 :]
+    wholes, (features_ref, own_back_ref), refs = refs[:n], refs[n : n + 2], refs[n + 2 :]
+    own_sem, send_sem, recv_sem, col_send, col_recv = refs
     row, column = lax.axis_index("row"), lax.axis_index("col")
     place = ring_place(row, rows)
     ends = (ring_row((place + 1) % rows, rows), ring_row((place + rows - 1) % rows, rows))
-    ring_barrier(ends[0], ends[1], column)
+    cols = features_ref.shape[1] // tokens_ref.shape[1]
+    quarter = back_ref.shape[0] // cols
+    peers = [flip(flip(column, 1) if k & 1 else column, 2) if k & 2 else flip(column, 1) for k in range(1, cols)]
+    ring_barrier([(ends[0], column), (ends[1], column)] + [(row, peer) for peer in peers])
+    lanes = pl.ds(pl.multiple_of(column * tokens_ref.shape[1], 128), tokens_ref.shape[1])
+
+    def to_col(k, target):
+        part = back_ref.at[pl.ds(pl.multiple_of(target * quarter, 128), quarter)]
+        return [(tokens_ref, features_ref.at[:, lanes]), (part, own_back_ref.at[:, lanes])]
+
+    crossing = []
+    for k, peer in enumerate(peers):
+        for which, (source, there) in enumerate(to_col(k, peer)):
+            crossing.append(
+                pltpu.make_async_remote_copy(
+                    src_ref=source,
+                    dst_ref=there,
+                    send_sem=col_send.at[which, k],
+                    recv_sem=col_recv.at[which, k],
+                    device_id=(row, peer),
+                    device_id_type=MESH,
+                )
+            )
+    staying = [
+        pltpu.make_async_copy(source, there, own_sem.at[n + which])
+        for which, (source, there) in enumerate(to_col(-1, column))
+    ]
 
     def own(k):
         return pltpu.make_async_copy(blocks[k], wholes[k].at[row], own_sem.at[k])
@@ -70,6 +102,8 @@
         own(k).wait()
         for side in (0, 1):
             hop(0, side, k).start()
+    for copy in crossing + staying:
+        copy.start()
 
     def advance(step, carry):
         for k in range(n):
@@ -90,25 +124,35 @@
         return carry
 
     lax.fori_loop(0, rows - 1, drain, 0)
-
-
-def ring_gather(*blocks):
-    rows, n = lax.axis_size("row"), len(blocks)
+    for copy in crossing + staying:
+        copy.wait()
+
+
+def ring_gather(blocks, tokens, back):
+    rows, cols, n = lax.axis_size("row"), lax.axis_size("col"), len(blocks)
     halves = [block.reshape(2, block.shape[0] // 2, block.shape[1]) for block in blocks]
-    wholes = pl.pallas_call(
+    anywhere = pl.BlockSpec(memory_space=pl.ANY)
+    *wholes, features, own_back = pl.pallas_call(
         functools.partial(ring_gather_kernel, rows, n),
-        out_shape=[jax.ShapeDtypeStruct((rows,) + half.shape, half.dtype) for half in halves],
-        in_specs=[pl.BlockSpec(memory_space=pl.ANY)] * n,
-        out_specs=[pl.BlockSpec(memory_space=pl.ANY)] * n,
+        out_shape=[jax.ShapeDtypeStruct((rows,) + half.shape, half.dtype) for half in halves]
+        + [
+            jax.ShapeDtypeStruct((tokens.shape[0], cols * tokens.shape[1]), tokens.dtype),
+            jax.ShapeDtypeStruct((back.shape[0] // cols, cols * back.shape[1]), back.dtype),
+        ],
+        in_specs=[anywhere] * (n + 2),
+        out_specs=[anywhere] * (n + 2),
         scratch_shapes=[
-            pltpu.SemaphoreType.DMA((n,)),
+            pltpu.SemaphoreType.DMA((n + 2,)),
             pltpu.SemaphoreType.DMA((rows - 1, 2, n)),
             pltpu.SemaphoreType.DMA((rows - 1, 2, n)),
+            pltpu.SemaphoreType.DMA((2, cols - 1)),
+            pltpu.SemaphoreType.DMA((2, cols - 1)),
         ],
         compiler_params=pltpu.CompilerParams(collective_id=0, has_side_effects=True),
         name="ring_gather",
-    )(*halves)
-    return [whole.reshape(rows * block.shape[0], block.shape[1]) for whole, block in zip(wholes, blocks)]
+    )(*halves, tokens, back)
+    wholes = [whole.reshape(rows * block.shape[0], block.shape[1]) for whole, block in zip(wholes, blocks)]
+    return wholes, features, own_back
 
 
 def ring_scatter_kernel(rows, n, *refs):
@@ -116,7 +160,7 @@
     row, column = lax.axis_index("row"), lax.axis_index("col")
     place = ring_place(row, rows)
     ends = (ring_row((place + 1) % rows, rows), ring_row((place + rows - 1) % rows, rows))
-    ring_barrier(ends[0], ends[1], column)
+    ring_barrier([(ends[0], column), (ends[1], column)])
 
     def target(step, side):
         return ring_row((place + (1 + step if side else 2 * rows - 1 - step)) % rows, rows)
@@ -149,7 +193,7 @@
             for side in (0, 1):
                 arrive(step - 1, side, k).wait_recv()
                 total = slots[k][step - 1, side].astype(f32) + terms[k][target(step, side), side].astype(f32)
-                slots[k][step - 1, side] = total.astype(bf)
+                slots[k][step - 1, side] = total.astype(slots[k].dtype)
                 later(step, side, k).start()
         return carry
 
@@ -176,7 +220,7 @@
         out_shape=[jax.ShapeDtypeStruct(term.shape[1:], f32) for term in split],
         in_specs=[pl.BlockSpec(memory_space=pltpu.VMEM)] * n,
         out_specs=[pl.BlockSpec(memory_space=pltpu.VMEM)] * n,
-        scratch_shapes=[pltpu.VMEM((rows - 1,) + term.shape[1:], bf) for term in split]
+        scratch_shapes=[pltpu.VMEM((rows - 1,) + term.shape[1:], term.dtype) for term in split]
         + [pltpu.SemaphoreType.DMA((rows - 1, 2, n)), pltpu.SemaphoreType.DMA((rows - 1, 2, n))],
         compiler_params=pltpu.CompilerParams(
             collective_id=1, has_side_effects=True, vmem_limit_bytes=VMEM_LIMIT
@@ -278,69 +322,349 @@
     return jnp.concatenate(chunks, axis=1)
 
 
-def group_gather(own):
-    pieces = []
-    for piece in (own, swap_row(own, PAIR)):
-        across = swap_col(piece, 2)
-        pieces += [piece, swap_col(piece, 1), across, swap_col(across, 1)]
-    return jnp.concatenate(pieces, axis=0)
-
-
-def group_scatter(value):
-    x = jnp.split(value, 2 * lax.axis_size("col"), axis=0)
-    beside = swap_col(jnp.concatenate([x[1], x[3], x[5], x[7]], axis=0).astype(bf), 1).astype(f32)
-    y = [term + got for term, got in zip((x[0], x[2], x[4], x[6]), jnp.split(beside, 4, axis=0))]
-    across = swap_col(jnp.concatenate([y[1], y[3]], axis=0).astype(bf), 2).astype(f32)
-    z = [term + got for term, got in zip((y[0], y[2]), jnp.split(across, 2, axis=0))]
-    return z[0] + swap_row(z[1].astype(bf), PAIR).astype(f32)
-
-
-def gather_hidden(block, turn):
-    low, high = jnp.split(block, 2, axis=0)
+def group_gather(own, mark):
+    both = after(jnp.concatenate([own, swap_row(own, PAIR)], axis=0), mark)
+    across = swap_col(both, 2)
+    pieces = [both, swap_col(both, 1), across, swap_col(across, 1)]
+    return jnp.concatenate([p for half in zip(*(jnp.split(piece, 2, axis=0) for piece in pieces)) for p in half], axis=0)
+
+
+class GroupScatter:
+    def __init__(self, value):
+        x = jnp.split(value, 2 * lax.axis_size("col"), axis=0)
+        self.kept = (x[0], x[2], x[4], x[6])
+        self.came = swap_col(jnp.concatenate([x[1], x[3], x[5], x[7]], axis=0).astype(bf), 1)
+
+    def add(self, mark):
+        self.came = after(self.came, mark)
+        return [a + b.astype(f32) for a, b in zip(self.kept, jnp.split(self.came, len(self.kept), axis=0))]
+
+    def across(self, mark):
+        y = self.add(mark)
+        self.kept = (y[0], y[2])
+        self.came = swap_col(jnp.concatenate([y[1], y[3]], axis=0).astype(bf), 2)
+
+    def partner(self, mark):
+        z = self.add(mark)
+        self.kept = (z[0],)
+        self.came = swap_row(z[1].astype(bf), PAIR)
+
+    def result(self):
+        return self.kept[0] + self.came.astype(f32)
+
+
+def pair_halves(value, axis):
+    low, high = jnp.split(value, 2, axis=axis)
     upper = own_group()[1] == 1
-    mine = jnp.where(upper, high, low)
-    came = swap_row(jnp.where(upper, low, high), PAIR)
-    pieces = {0: jnp.concatenate([jnp.where(upper, came, mine), jnp.where(upper, mine, came)], axis=1)}
-    if turn is not None:
-        pieces[0] = after(pieces[0], turn)
-    first = None
-    for bit, mask in group_masks():
-        for k in list(pieces):
-            pieces[k ^ bit] = swap_row(pieces[k], mask)
-            first = pieces[k ^ bit] if first is None else first
-    return (jnp.concatenate([pieces[k] for k in range(len(pieces))], axis=1), first)
-
-
-def scatter_hidden(left, right, turn):
-    groups = lax.axis_size("row") // 2
-    chunks = jnp.split(right, groups, axis=1)
-    pieces = {}
-    kept = list(range(groups))
-    first = None
-    for bit, mask in reversed(group_masks()):
-        away, stay = [k for k in kept if k & bit], [k for k in kept if not k & bit]
-        for k in kept:
-            if k not in pieces:
-                pieces[k] = None
-        if first is None:
-            wide = lambda ks: jnp.concatenate([chunks[k] for k in ks], axis=1)
-            leaving = over_rows(left, wide(away)).astype(bf)
-            staying = over_rows(left, wide(stay))
-            if turn is not None:
-                leaving = after(leaving, turn)
-        else:
-            leaving = jnp.concatenate([pieces[k] for k in away], axis=1).astype(bf)
-            staying = jnp.concatenate([pieces[k] for k in stay], axis=1)
-        came = swap_row(leaving, mask)
-        first = came if first is None else first
-        total = staying + came.astype(f32)
-        pieces = dict(zip(stay, jnp.split(total, len(stay), axis=1)))
-        kept = stay
-    low, high = jnp.split(pieces[0], 2, axis=1)
+    return (jnp.where(upper, high, low), jnp.where(upper, low, high))
+
+
+def in_pair_order(mine, came, axis):
     upper = own_group()[1] == 1
-    mine = jnp.where(upper, high, low)
-    came = swap_row(jnp.where(upper, low, high).astype(bf), PAIR).astype(f32)
-    return (jnp.concatenate([jnp.where(upper, came, mine), jnp.where(upper, mine, came)], axis=0), first)
+    return jnp.concatenate([jnp.where(upper, came, mine), jnp.where(upper, mine, came)], axis=axis)
+
+
+class HiddenGather:
+    def __init__(self, blocks, late):
+        self.late = late
+        mine, self.away = pair_halves(blocks, 1)
+        self.came = swap_row(self.away, PAIR)
+        self.own = in_pair_order(mine, self.came, 2)
+
+    def near_own(self, mark):
+        self.beside = swap_row(after(self.own, mark), group_masks()[-1][1])
+
+    def far(self, late, mark):
+        n = self.own.shape[0]
+        own = after(self.own[n - self.late :] if late else self.own[: n - self.late], mark)
+        pieces = {0: own}
+        for bit, mask in group_masks()[:-1]:
+            for k in list(pieces):
+                pieces[k ^ bit] = swap_row(pieces[k], mask)
+        return pieces
+
+    def near(self, pieces, late, mark):
+        n = self.own.shape[0]
+        part = slice(n - self.late, n) if late else slice(0, n - self.late)
+        done = {0: self.own[part], 1: self.beside[part]}
+        for k in pieces:
+            if k:
+                done[k] = pieces[k]
+                done[k ^ 1] = swap_row(after(pieces[k], mark), group_masks()[-1][1])
+        return [done[k] for k in range(len(done))]
+
+
+class HiddenScatter:
+    def __init__(self, left, right):
+        groups = lax.axis_size("row") // 2
+        chunks = jnp.split(right, groups, axis=1)
+        self.kept = [k for k in range(groups) if not k & 1]
+        self.away = over_rows(left, jnp.concatenate([chunks[k | 1] for k in self.kept], axis=1)).astype(bf)
+        self.total = over_rows(left, jnp.concatenate([chunks[k] for k in self.kept], axis=1))
+
+    def near(self, mark):
+        self.came = swap_row(after(self.away, mark), group_masks()[-1][1])
+
+    def add(self):
+        pieces = jnp.split(self.total + self.came.astype(f32), len(self.kept), axis=1)
+        return dict(zip(self.kept, pieces))
+
+    def far(self, mark):
+        for bit, mask in reversed(group_masks()[:-1]):
+            self.came = after(self.came, mark)
+            pieces = self.add()
+            away = [k for k in self.kept if k & bit]
+            self.kept = [k for k in self.kept if not k & bit]
+            self.total = jnp.concatenate([pieces[k] for k in self.kept], axis=1)
+            self.came = swap_row(jnp.concatenate([pieces[k] for k in away], axis=1).astype(bf), mask)
+
+    def halves(self):
+        return pair_halves(self.add()[0].astype(bf), 1)
+
+
+COLS = (("col", 1), ("col", 2))
+GROUP = COLS + (("row", PAIR),)
+
+
+class Cube:
+    def __init__(self, dims, parts):
+        self.dims, self.parts = dims, parts
+        self.row, self.column = lax.axis_index("row"), lax.axis_index("col")
+        self.masks = range(1, 1 << len(dims))
+
+    def device(self, mask):
+        row, column = self.row, self.column
+        for k, (axis, bit) in enumerate(self.dims):
+            if mask >> k & 1:
+                row, column = (flip(row, bit), column) if axis == "row" else (row, flip(column, bit))
+        return (row, column)
+
+    def partner(self):
+        return (flip(self.row, PAIR), self.column)
+
+    def greet(self, cargo):
+        others = [self.device(1 << k) for k in range(len(self.dims))] + [self.partner()] * cargo
+        barrier = pltpu.get_barrier_semaphore()
+        for other in others:
+            pl.semaphore_signal(barrier, inc=1, device_id=other, device_id_type=MESH)
+        pl.semaphore_wait(barrier, len(others))
+
+    def ship(self, cargo):
+        return [
+            pltpu.make_async_remote_copy(
+                src_ref=cargo[0],
+                dst_ref=cargo[1],
+                send_sem=cargo[2],
+                recv_sem=cargo[3],
+                device_id=self.partner(),
+                device_id_type=MESH,
+            )
+        ] if cargo else []
+
+    def order(self, part):
+        slow = list(range(1, len(self.dims)))
+        return [0] + (slow[::-1] if part % 2 else slow)
+
+
+def cut(ref, index, rows, width):
+    if width is None:
+        return ref.at[index, rows]
+    return ref.at[rows, pl.ds(pl.multiple_of(index * width, 128), width)]
+
+
+def unpack(cargo, refs, inputs, outputs):
+    if not cargo:
+        return (refs, ())
+    own, swapped = refs[inputs], refs[inputs + 1 + outputs]
+    rest = refs[:inputs] + refs[inputs + 1 : inputs + 1 + outputs] + refs[inputs + outputs + 2 : -2]
+    return (rest, (own, swapped) + tuple(refs[-2:]))
+
+
+def spread_kernel(dims, parts, lanes, relative, cargo, *refs):
+    (own_ref, all_ref, own_sem, send_sem, recv_sem), cargo = unpack(cargo, refs, 1, 1)
+    cube = Cube(dims, parts)
+    cube.greet(len(cargo) > 0)
+    ship = cube.ship(cargo)
+    for copy in ship:
+        copy.start()
+    height, width = own_ref.shape
+    size = height // parts
+    width = width if lanes else None
+
+    def index(mask):
+        return mask if relative else cube.device(mask)[1]
+
+    def rows(part):
+        return pl.ds(part * size, size)
+
+    own = pltpu.make_async_copy(own_ref, cut(all_ref, index(0), pl.ds(0, height), width), own_sem)
+    own.start()
+
+    def hop(part, mask, k):
+        there = mask | 1 << k
+        target = there if relative else index(mask)
+        source = cut(all_ref, index(mask), rows(part), width) if mask else own_ref.at[rows(part)]
+        return pltpu.make_async_remote_copy(
+            src_ref=source,
+            dst_ref=cut(all_ref, target, rows(part), width),
+            send_sem=send_sem.at[part, there],
+            recv_sem=recv_sem.at[part, there],
+            device_id=cube.device(1 << k),
+            device_id_type=MESH,
+        )
+
+    def arrival(part, mask):
+        view = cut(all_ref, index(mask), rows(part), width)
+        return pltpu.make_async_remote_copy(
+            src_ref=view,
+            dst_ref=view,
+            send_sem=send_sem.at[part, mask],
+            recv_sem=recv_sem.at[part, mask],
+            device_id=cube.device(1),
+            device_id_type=MESH,
+        )
+
+    sent = []
+    for part in range(parts):
+        for k in cube.order(part)[::-1]:
+            sent.append(hop(part, 0, k))
+            sent[-1].start()
+    last = []
+    for bits in range(1, len(dims)):
+        for part in range(parts):
+            order = cube.order(part)[::-1]
+            for mask in cube.masks:
+                if bin(mask).count("1") != bits:
+                    continue
+                further = order[max(order.index(k) for k in range(len(dims)) if mask >> k & 1) + 1 :]
+                if not further:
+                    last.append((part, mask))
+                    continue
+                arrival(part, mask).wait_recv()
+                for k in further:
+                    sent.append(hop(part, mask, k))
+                    sent[-1].start()
+    last += [(part, cube.masks[-1]) for part in range(parts)]
+    for part, mask in last:
+        arrival(part, mask).wait_recv()
+    for copy in sent:
+        copy.wait_send()
+    own.wait()
+    for copy in ship:
+        copy.wait()
+
+
+def cargo_parts(cargo):
+    if cargo is None:
+        return ([], [], [])
+    anywhere = pl.BlockSpec(memory_space=pl.ANY)
+    return ([anywhere], [jax.ShapeDtypeStruct(cargo.shape, cargo.dtype)], [pltpu.SemaphoreType.DMA] * 2)
+
+
+def spread(own, dims, parts, number, lanes=False, relative=False, cargo=None):
+    specs, shapes, semaphores = cargo_parts(cargo)
+    count = 1 << len(dims)
+    shape = (own.shape[0], count * own.shape[1]) if lanes else (count,) + own.shape
+    whole, *swapped = pl.pallas_call(
+        functools.partial(spread_kernel, dims, parts, lanes, relative, cargo is not None),
+        out_shape=[jax.ShapeDtypeStruct(shape, own.dtype)] + shapes,
+        in_specs=[pl.BlockSpec(memory_space=pl.ANY)] + specs,
+        out_specs=[pl.BlockSpec(memory_space=pl.ANY)] + specs,
+        scratch_shapes=[
+            pltpu.SemaphoreType.DMA,
+            pltpu.SemaphoreType.DMA((parts, count)),
+            pltpu.SemaphoreType.DMA((parts, count)),
+        ]
+        + semaphores,
+        compiler_params=pltpu.CompilerParams(collective_id=number, has_side_effects=True),
+        name=f"spread{number}",
+    )(*([own] if cargo is None else [own, cargo]))
+    whole = whole if lanes else whole.reshape(count * own.shape[0], own.shape[1])
+    return (whole, swapped[0]) if swapped else whole
+
+
+def fold_kernel(dims, parts, lanes, relative, cargo, *refs):
+    (terms_ref, sum_ref, arrive_ref, leave_ref, send_sem, recv_sem), cargo = unpack(cargo, refs, 1, 1)
+    cube = Cube(dims, parts)
+    cube.greet(len(cargo) > 0)
+    ship = cube.ship(cargo)
+    for copy in ship:
+        copy.start()
+    height, width = sum_ref.shape
+    size = height // parts
+    width = width if lanes else None
+
+    def term(part, mask):
+        return cut(terms_ref, mask if relative else cube.device(mask)[1], pl.ds(part * size, size), width)
+
+    def hop(part, mask, k, source):
+        return pltpu.make_async_remote_copy(
+            src_ref=source,
+            dst_ref=arrive_ref.at[mask, pl.ds(part * size, size)],
+            send_sem=send_sem.at[part, mask],
+            recv_sem=recv_sem.at[part, mask],
+            device_id=cube.device(1 << k),
+            device_id_type=MESH,
+        )
+
+    sent = []
+    for stage in range(len(dims) + 1):
+        for part in range(parts):
+            rows = pl.ds(part * size, size)
+            order = cube.order(part)
+            done = sum(1 << k for k in order[:stage])
+            if stage:
+                for mask in range(1 << len(dims)):
+                    if not mask & done:
+                        there = mask | 1 << order[stage - 1]
+                        hop(part, there, order[stage - 1], arrive_ref.at[there, rows]).wait_recv()
+            going = [0] if stage == len(dims) else [m for m in cube.masks if not m & done and m >> order[stage] & 1]
+            for mask in going:
+                source = term(part, mask)
+                if stage:
+                    total = source[...].astype(f32)
+                    for k in order[:stage]:
+                        total = total + arrive_ref[mask | 1 << k, rows].astype(f32)
+                    if mask == 0:
+                        sum_ref[rows] = total
+                        continue
+                    leave_ref[mask, rows] = total.astype(bf)
+                    source = leave_ref.at[mask, rows]
+                sent.append(hop(part, mask, order[stage], source))
+                sent[-1].start()
+    for copy in sent:
+        copy.wait_send()
+    for copy in ship:
+        copy.wait()
+
+
+def fold(terms, dims, parts, number, lanes=False, relative=False, cargo=None):
+    count = 1 << len(dims)
+    terms = terms.astype(bf)
+    if lanes:
+        shape = (terms.shape[0], terms.shape[1] // count)
+    else:
+        shape = (terms.shape[0] // count, terms.shape[1])
+        terms = terms.reshape((count,) + shape)
+    specs, shapes, semaphores = cargo_parts(cargo)
+    total, *swapped = pl.pallas_call(
+        functools.partial(fold_kernel, dims, parts, lanes, relative, cargo is not None),
+        out_shape=[jax.ShapeDtypeStruct(shape, f32)] + shapes,
+        in_specs=[pl.BlockSpec(memory_space=pltpu.VMEM)] + specs,
+        out_specs=[pl.BlockSpec(memory_space=pltpu.VMEM)] + specs,
+        scratch_shapes=[
+            pltpu.VMEM((count,) + shape, bf),
+            pltpu.VMEM((count,) + shape, bf),
+            pltpu.SemaphoreType.DMA((parts, count)),
+            pltpu.SemaphoreType.DMA((parts, count)),
+        ]
+        + semaphores,
+        compiler_params=pltpu.CompilerParams(
+            collective_id=number, has_side_effects=True, vmem_limit_bytes=VMEM_LIMIT
+        ),
+        name=f"fold{number}",
+    )(*([terms] if cargo is None else [terms, cargo]))
+    return (total, swapped[0]) if swapped else total
 
 
 def dot(left, right, dims):
@@ -473,9 +797,6 @@
             jax.ShapeDtypeStruct((pairs, 2, count), f32),
         ],
         compiler_params=pltpu.CompilerParams(vmem_limit_bytes=VMEM_LIMIT),
-        cost_estimate=pl.CostEstimate(
-            flops=heads * kl * count * 2 * 512, bytes_accessed=16 << 20, transcendentals=heads * kl * count
-        ),
         name="attend",
     )(first, query, query, keys, turned_keys, values_t, bias)
 
@@ -581,11 +902,87 @@
             jax.ShapeDtypeStruct((kl, 128), f32),
         ],
         compiler_params=pltpu.CompilerParams(vmem_limit_bytes=VMEM_LIMIT),
-        cost_estimate=pl.CostEstimate(
-            flops=heads * kl * count * 2 * 1280, bytes_accessed=32 << 20, transcendentals=heads * kl * count
-        ),
         name="attend_back",
     )(first, query, query, query_n, query_n, keys, turned_keys, keys_t, turned_keys_t, values, do_t, do, bias, lse)
+
+
+TOKENS = 256
+
+
+def dot_pieces(left, pieces, which):
+    width = pieces[0].shape[2]
+    total = None
+    for k, piece in enumerate(pieces):
+        term = against(left[:, k * width : (k + 1) * width], piece[which])
+        total = term if total is None else total + term
+    return total
+
+
+def ffn_kernel(n, x_ref, *refs):
+    pieces, (gate_ref, up_ref, hidden_ref) = refs[:n], refs[n:]
+    gate = dot_pieces(x_ref, pieces, 0)
+    upward = dot_pieces(x_ref, pieces, 1)
+    gate_ref[...] = gate
+    up_ref[...] = upward
+    hidden_ref[...] = (gate / (1.0 + jnp.exp(-gate)) * upward).astype(bf)
+
+
+def piece_specs(pieces, count):
+    shape = (count,) + pieces[0].shape[1:]
+    return [pl.BlockSpec(shape, lambda i: (0, 0, 0), pipeline_mode=pl.Buffered(1)) for _ in pieces]
+
+
+def ffn(x, pieces):
+    tokens, hidden = x.shape[0], pieces[0].shape[1]
+    tile = lambda width: pl.BlockSpec((TOKENS, width), lambda i: (i, 0))
+    return pl.pallas_call(
+        functools.partial(ffn_kernel, len(pieces)),
+        grid=(tokens // TOKENS,),
+        out_shape=[
+            jax.ShapeDtypeStruct((tokens, hidden), f32),
+            jax.ShapeDtypeStruct((tokens, hidden), f32),
+            jax.ShapeDtypeStruct((tokens, hidden), bf),
+        ],
+        in_specs=[tile(x.shape[1])] + piece_specs(pieces, 2),
+        out_specs=[tile(hidden)] * 3,
+        compiler_params=pltpu.CompilerParams(vmem_limit_bytes=VMEM_LIMIT),
+        name="ffn",
+    )(x, *pieces)
+
+
+def ffn_back_kernel(n, dm_ref, gate_ref, up_ref, hidden_ref, *refs):
+    first, down, (dgate_ref, dup_ref, dx_ref, out_ref) = refs[:n], refs[n : 2 * n], refs[2 * n :]
+    width = down[0].shape[2]
+    back_hidden = dot_pieces(dm_ref, down, 0)
+    gate, upward = gate_ref[...], up_ref[...]
+    sigma = 1.0 / (1.0 + jnp.exp(-gate))
+    dgate_ref[...] = (back_hidden * upward * sigma * (1.0 + gate * (1.0 - sigma))).astype(bf)
+    dup_ref[...] = (back_hidden * gate * sigma).astype(bf)
+    for k in range(n):
+        lanes = slice(k * width, (k + 1) * width)
+        dx_ref[:, lanes] = (multiply(dgate_ref[...], first[k][0]) + multiply(dup_ref[...], first[k][1])).astype(bf)
+        out_ref[:, lanes] = multiply(hidden_ref[...], down[k][0]).astype(bf)
+
+
+def ffn_back(dm, gate, upward, hidden, pieces, down):
+    tokens, units = gate.shape
+    tile = lambda width: pl.BlockSpec((TOKENS, width), lambda i: (i, 0))
+    return pl.pallas_call(
+        functools.partial(ffn_back_kernel, len(pieces)),
+        grid=(tokens // TOKENS,),
+        out_shape=[
+            jax.ShapeDtypeStruct((tokens, units), bf),
+            jax.ShapeDtypeStruct((tokens, units), bf),
+            jax.ShapeDtypeStruct(dm.shape, bf),
+            jax.ShapeDtypeStruct(dm.shape, bf),
+        ],
+        in_specs=[tile(dm.shape[1]), tile(units), tile(units), tile(units)]
+        + piece_specs(pieces, 2)
+        + piece_specs(down, 1),
+        out_specs=[tile(units), tile(units), tile(dm.shape[1]), tile(dm.shape[1])],
+        compiler_params=pltpu.CompilerParams(vmem_limit_bytes=VMEM_LIMIT),
+        name="ffn_back",
+    )(dm, gate, upward, hidden, *pieces, *down)
 
 
 def shards(
@@ -615,12 +1012,13 @@
     latent_up_low = multiply(latent_up.astype(bf), latent_one.astype(bf)).astype(bf)
     down_block = jnp.concatenate([down_slice, gains], axis=1)
     down_block = jnp.pad(down_block, ((0, 0), (0, -down_block.shape[1] % 128)))
-    wide_down, wide_query_up, wide_latent_up, wide_output = ring_gather(
-        down_block, query_up_low, latent_up_low, output_weight.astype(bf).T
-    )
-    gate_t, turn = gather_hidden(after(gate_weight.astype(bf).T, wide_down), None)
-    up_t, turn = gather_hidden(up_weight.astype(bf).T, turn)
-    wide_back, turn = gather_hidden(down_weight.astype(bf), turn)
+    ffn_weights = HiddenGather(
+        jnp.stack([gate_weight.astype(bf).T, up_weight.astype(bf).T, down_weight.astype(bf)]), 1
+    )
+    (wide_down, wide_query_up, wide_latent_up), features, own_up = ring_gather(
+        (after(down_block, ffn_weights.away), query_up_low, latent_up_low), tokens, cotangent
+    )
+    wide_output = lax.all_gather(after(output_weight, wide_down).astype(bf).T, "row", axis=0, tiled=True)
     gain_one = wide_down[:, slice_width].astype(f32)
     gain_two = wide_down[:, slice_width + 1].astype(f32)
     small_gains = wide_down[:, slice_width + 2].reshape(rows, -1).astype(f32)
@@ -629,9 +1027,6 @@
     latent_scale = small_gains[:, own_q : own_q + latent_gain.shape[0]].reshape(-1)[:, None]
     wide_down = wide_down[:, :slice_width]
 
-    features = jnp.concatenate(col_gather(tokens), axis=1)
-    own_up = jnp.concatenate(col_exchange(quarters(cotangent, 0)), axis=1)
-    back_down = group_gather(features_by_group((RES * own_up).astype(bf)))
     residual = features.astype(f32)
     first_in = (residual * inverse_of(residual, 1) * gain_one).astype(bf)
     own_residual = pick(quarters(features, 0)).astype(f32)
@@ -644,7 +1039,11 @@
     half = DR // 2
     key_front, key_back = rotate(latents[QR + KR : QR + KR + half], latents[QR + KR + half :], cosine, sine)
     key_part = jnp.concatenate([latent_in, key_front.astype(bf), key_back.astype(bf)], axis=0)
+    key_part = after(key_part, ffn_weights.came)
     key_parts = jnp.concatenate([from_behind(key_part, step) for step in range(reach, 0, -1)] + [key_part], axis=1)
+    ffn_weights.near_own(key_parts)
+    far_first = ffn_weights.far(False, key_parts)
+    back_down = group_gather(features_by_group((RES * own_up).astype(bf)), key_parts)
     latent_all = key_parts[:KR]
     turned_t = jnp.concatenate([key_parts[KR : KR + half]] * 4 + [key_parts[KR + half :]] * 4, axis=0)
     turned = turned_t.T
@@ -669,35 +1068,51 @@
     values_t = over_rows(up_values, latent_all).astype(bf)
     out_t, lse = attend(first, query, keys, turned, values_t, bias, heads)
 
-    branch = dot(out_t, wide_output, ((0,), (1,)))
-    middle = own_residual + RES * col_scatter(quarters(branch, 0))
+    out_t = after(out_t, ffn_weights.beside)
+    branch = after(dot(out_t, wide_output, ((0,), (1,))), back_down)
+    middle = own_residual + RES * fold(branch, COLS, 4, 4)
+    middle = after(middle, [piece for k, piece in far_first.items() if k])
+    far_down = ffn_weights.far(True, middle)
+    first_pieces = ffn_weights.near(far_first, False, middle)
     inverse_second = inverse_of(middle, 1)
-    second_in = group_gather(features_by_group((middle * inverse_second * gain_two).astype(bf)))
-
-    gate = against(second_in, gate_t)
-    upward = against(second_in, up_t)
-    sigma = jax.nn.sigmoid(gate)
-    hidden = (gate * sigma * upward).astype(bf)
-    own_result = middle + RES * features_in_order(group_scatter(multiply(hidden, wide_back)))
-    result = jnp.concatenate(col_exchange(quarters(own_result, 1)), axis=0)
-    slope_down, turn = scatter_hidden(hidden, back_down, None)
-    back_hidden = against(back_down, wide_back)
-    back_gate = (back_hidden * upward * sigma * (1.0 + gate * (1.0 - sigma))).astype(bf)
-    back_upward = (back_hidden * gate * sigma).astype(bf)
-    slope_gate, turn = scatter_hidden(back_gate, second_in, turn)
-    slope_up, turn = scatter_hidden(back_upward, second_in, turn)
-    back_second = features_in_order(group_scatter(multiply(back_gate, gate_t) + multiply(back_upward, up_t)))
+    second_in = features_by_group((middle * inverse_second * gain_two).astype(bf))
+    second_in = spread(second_in, GROUP, 4, 5, relative=True)
+
+    gate, upward, hidden = ffn(second_in, first_pieces)
+    down_pieces = ffn_weights.near(far_down, True, second_in)
+    slope_down = HiddenScatter(hidden, back_down)
+    slope_down.near(hidden)
+    back_gate, back_upward, back_second, out_part = ffn_back(
+        back_down, gate, upward, hidden, first_pieces, down_pieces
+    )
+    slope_gate = HiddenScatter(back_gate, second_in)
+    slope_gate.near(back_gate)
+    back_second = after(back_second, slope_gate.away)
+    back_second = features_in_order(fold(back_second, GROUP, 4, 6, relative=True))
+    slope_up = HiddenScatter(back_upward, second_in)
+    own_result = GroupScatter(out_part)
     back_norm, gain_second_part = norm_back(middle, inverse_second, gain_two, back_second, 1)
     back_middle = own_up + back_norm
-    back_branch = jnp.concatenate(col_gather((RES * back_middle).astype(bf)), axis=0)
+    back_branch = after((RES * back_middle).astype(bf), (slope_down.came, own_result.came, slope_up.away))
+    slope_up.near(back_branch)
+    slope_down.far(back_branch)
+    back_branch = spread(back_branch, COLS, 4, 7)
+    own_result.across(back_branch)
 
     out = out_t.T
     back_out = multiply(back_branch, wide_output).astype(bf)
+    slope_output = lax.psum_scatter(
+        over_rows(back_branch, out).astype(bf), "row", scatter_dimension=0, tiled=True
+    )
+    slope_gate.far(back_out)
     keys_t = over_rows(up_keys, latent_all).astype(bf)
     values = over_rows(latent_all, up_values).astype(bf)
     back_query_n, back_query_r, back_keys, back_values, back_turned = attend_back(
         first, query, query.T, keys, turned, keys_t, turned_t, values, back_out.T, back_out, bias, lse, heads
     )
+    back_query_n = after(back_query_n, (slope_down.came, slope_up.came, own_result.came))
+    slope_up.far(back_query_n)
+    own_result.partner(back_query_n)
     tiles = back_query_r.reshape(-1, 2, 64, count)
     back_turn = jnp.stack(rotate(tiles[:, 0], tiles[:, 1], cos_tile, -sin_tile), axis=1).reshape(-1, count)
     back_raw = jnp.concatenate([back_query_n, back_turn], axis=0).astype(bf)
@@ -708,7 +1123,12 @@
     to_send = jnp.concatenate(
         [query_part] + [far[:, b * count : (b + 1) * count] for b in range(blocks)], axis=0
     )
-    summed = col_scatter(quarters(to_send, 1))
+    to_send = after(to_send, (slope_gate.came, own_result.came))
+    slope_down, away = slope_down.halves()
+    summed, came = fold(to_send, COLS, 3, 8, lanes=True, cargo=away)
+    slope_down = in_pair_order(slope_down, came, 0)
+    own_result = after(middle + RES * features_in_order(own_result.result()), summed)
+    result = jnp.concatenate(col_exchange(quarters(own_result, 1)), axis=0)
     back_query_in = summed[:QR]
     wide_far = KR + DR
     parts = [summed[QR + b * wide_far : QR + (b + 1) * wide_far] for b in range(blocks)]
@@ -727,41 +1147,38 @@
     own_cosine, own_sine = pick(quarters(cosine, 1)), pick(quarters(sine, 1))
     back_front, back_behind = rotate(back_key[KR : KR + half], back_key[KR + half :], own_cosine, -own_sine)
     back_latents = jnp.concatenate([back_query_latent, back_latent, back_front, back_behind], axis=0).astype(bf)
-    back_latents = jnp.concatenate(col_gather(back_latents), axis=1)
+    back_latents = spread(back_latents, COLS, 3, 9, lanes=True)
     back_slice = lax.dynamic_slice_in_dim(back_latents, column * slice_width, slice_width, 0)
-    back_first = col_scatter(quarters(dot(back_slice, wide_down, ((0,), (1,))), 0))
+    slope_gate, away = after(slope_gate.halves(), (result, slope_up.came))
+    back_first, came = fold(dot(back_slice, wide_down, ((0,), (1,))), COLS, 4, 10, cargo=away)
+    slope_gate = in_pair_order(slope_gate, came, 0)
     back_norm_first, gain_first_part = norm_back(own_residual, inverse_of(own_residual, 1), gain_one, back_first, 1)
     back_tokens = jnp.concatenate(col_exchange(quarters(back_middle + back_norm_first, 1)), axis=0)
 
+    packed = jnp.concatenate(
+        [part.reshape(rows, -1) for part in (gain_first_part, gain_second_part, query_gain_part, latent_gain_part)],
+        axis=1,
+    )
+    packed = jnp.pad(packed, ((0, 0), (0, -packed.shape[1] % 256))).reshape(-1, 128)
     back_slice_n = jnp.pad(back_slice.T, ((0, 0), (0, -slice_width % 128)))
-    slope_output, slope_query_up, slope_latent_up, slope_down_slice = ring_scatter(
-        over_rows(back_branch, out).astype(bf),
+    slope_query_up, slope_latent_up, slope_down_slice, packed = ring_scatter(
         against(query_in, back_raw).astype(bf),
         multiply(latent_all, jnp.concatenate([back_keys, back_values], axis=1)).astype(bf),
         over_rows(first_in, back_slice_n).astype(bf),
-    )
-    slope_down_slice = slope_down_slice[:, :slice_width]
-    slope_both = jnp.concatenate(col_gather(slope_down_slice), axis=1)
-
-    packed = jnp.concatenate(
-        [part.reshape(rows, -1) for part in (gain_first_part, gain_second_part, query_gain_part, latent_gain_part)],
-        axis=1,
-    )
-    bit = rows // 2
-    while bit >= 1:
-        upper = (row // bit) % 2 == 1
-        low_half, high_half = packed[:bit], packed[bit:]
-        away = jnp.where(upper, low_half, high_half)
-        stay = jnp.where(upper, high_half, low_half)
-        packed = stay + lax.ppermute(away, "row", [(r, r ^ bit) for r in range(rows)])
-        bit //= 2
-    packed = packed[0]
+        packed,
+    )
+    slope_up, away = slope_up.halves()
+    slope_both, came = spread(slope_down_slice.astype(bf), COLS, 2, 11, lanes=True, cargo=away)
+    slope_up = in_pair_order(slope_up, came, 0)
+    slope_both = jnp.concatenate([piece[:, :slice_width] for piece in quarters(slope_both, 1)], axis=1).astype(f32)
+    packed = packed.reshape(-1)
     bit = 1
     while bit < cols:
         packed = packed + swap_col(packed, bit)
         bit *= 2
     n = gain_first.shape[0]
     m = query_gain.shape[0]
+    k = latent_gain.shape[0]
 
     exact = functools.partial(
         lax.dot_general,
@@ -776,14 +1193,14 @@
         slope_both[:, :QR],
         packed[2 * n : 2 * n + m],
         slope_both[:, QR:],
-        packed[2 * n + m :],
+        packed[2 * n + m : 2 * n + m + k],
         exact(slope_query_up, query_one.astype(f32)),
         exact(slope_latent_up, latent_one.astype(f32)),
-        slope_output.T,
+        slope_output.T.astype(f32),
         packed[n : 2 * n],
-        slope_gate.T,
-        slope_up.T,
-        slope_down,
+        slope_gate.T.astype(f32),
+        slope_up.T.astype(f32),
+        slope_down.astype(f32),
     )
 
 

time: 1090 us -> 983 us (0.902); the launches traced: 1090 us -> 967 us
  Pallas kernels: 211 us -> 414 us
  waiting for transfers between devices: 276 us -> 136 us
  starting transfers between devices: 181 us -> 105 us
  matrix products: 137 us -> 86.8 us
  other arithmetic: 142 us -> 99.1 us
  local copies, waits for them, and re-layouts: 140 us -> 109 us
  between operations: 3.93 us -> 16.8 us
    pallas_call x0 -> x10, Pallas kernels: none -> 271 us  [the longest x4 117 us: fold(): pl.pallas_call(functools.partial(fold_kernel, dims, parts, lanes, relativ...]
    ppermute x25 -> x14, waiting for transfers between devices: 183 us -> 119 us  [swap_row(): lax.ppermute(value, 'row', [(r, r ^ mask) for r in range(lax.axis_size('r...]
    ppermute x51 -> x16, waiting for transfers between devices: 56.1 us -> 0.04 us  [swap_col(): lax.ppermute(value, 'col', [(c, c ^ bit) for c in range(lax.axis_size('co...]
    ppermute x25 -> x14, starting transfers between devices: 131 us -> 76.2 us  [swap_row(): lax.ppermute(value, 'row', [(r, r ^ mask) for r in range(lax.axis_size('r...]
    dot_general x30 -> x24, matrix products: 131 us -> 80 us  [dot(): lax.dot_general(left, right, (dims, ((), ())), preferred_element_type=f32)]
    pallas_call x1, Pallas kernels: 99.5 us -> 64.1 us  [ring_gather(): pl.pallas_call(functools.partial(ring_gather_kernel, rows, n), out_shape=...]
    pallas_call x1, Pallas kernels: 80.5 us -> 47.6 us  [ring_scatter(): pl.pallas_call(functools.partial(ring_scatter_kernel, rows, n), out_shape...]
    ppermute x12 -> x1, local copies, waits for them, and re-layouts: 31.1 us -> 2.77 us  [swap_row(): lax.ppermute(value, 'row', [(r, r ^ mask) for r in range(lax.axis_size('r...]
  transfers between devices with their start and end apart: 87 -> 40, of which waited for: 26 -> 10; matrix products, arithmetic and copies ran while one was open for 32% -> 27% of each run, Pallas kernels for 19% -> 36%
where the time goes in v3:
time: 983 us; the launch traced here: 967 us
  Pallas kernels  414 us (42%)
  waiting for transfers between devices  136 us (14%)
  local copies, waits for them, and re-layouts  109 us (11%)
  starting transfers between devices  105 us (11%)
  other arithmetic  99.1 us (10%)
  matrix products  86.8 us (9%)
  between operations  16.8 us (2%)
    ppermute x14, waiting for transfers between devices, swap_row(): lax.ppermute(value, 'row', [(r, r ^ mask) for r in range(lax.axis_size('r...  119 us
    pallas_call x4, Pallas kernels, fold(): pl.pallas_call(functools.partial(fold_kernel, dims, parts, lanes, relativ...  117 us
    pallas_call x4, Pallas kernels, spread(): pl.pallas_call(functools.partial(spread_kernel, dims, parts, lanes, relat...  101 us
    dot_general x24, matrix products, dot(): lax.dot_general(left, right, (dims, ((), ())), preferred_element_type=f32)  80 us
    ppermute x14, starting transfers between devices, swap_row(): lax.ppermute(value, 'row', [(r, r ^ mask) for r in range(lax.axis_size('r...  76.2 us
    pallas_call x1, Pallas kernels, ring_gather(): pl.pallas_call(functools.partial(ring_gather_kernel, rows, n), out_shape=...  64.1 us
    pallas_call x1, Pallas kernels, ring_scatter(): pl.pallas_call(functools.partial(ring_scatter_kernel, rows, n), out_shape...  47.6 us
    unnamed x221, local copies, waits for them, and re-layouts  44 us
  transfers between devices with their start and end apart: 40, of which 10 were waited for; matrix products, arithmetic and copies ran while one was open for 27% of the time, Pallas kernels for 36%

profile of v3, /device:TPU:0, one launch (start us, length us, event | category | flops | bytes accessed | tf_op | source)
XLA Modules:
  0.0 966.7 jit_solution(524327537720117668)
XLA Ops:
  27.3 64.1 %ring_gather.1 = (bf16[8,2,160,384]{3,2,1,0:T(8,128)(2,1)}, bf16[8,2,48,1024]{3,2,1,0:T(8,128)(2,1)}, bf16[8,2,16,1280]{3,2,1,0:T(8,128)(2,1)}, bf16[512,2560]{1,0:T(8,128)(2,1)}, f32[128,2560]{1,0:T(8,128)}) custom-call(bf16[2,160,384]{2,1,0:T(8,128)(2,1)} %bitcast.109, bf16[2,48,1024]{2,1,0:T(8,128)(2,1)} %bitcast.116, bf16[2,16,1280]{2,1,0:T(8,128)(2,1)} %bitcast.118, ...), custom_call_target="tpu_custom_call" | custom-call | tf_op jit(solution)/shard_map/ring_gather/pallas_call | solution.py:135
  148.6 53.0 %collective-permute-done.3 = bf16[3,800,320]{1,2,0:T(8,128)(2,1)} collective-permute-done((bf16[3,800,320]{1,2,0:T(8,128)(2,1)}, bf16[3,800,320]{1,2,0:T(8,128)(2,1)}, u32[]{:S(2)}, u32[]{:S(2)}) %collective-permute-start.3) | collective-permute-done | bytes 1536032 | tf_op jit(solution)/shard_map/ppermute | solution.py:294
  249.5 15.5 %collective-permute-start.13 = (bf16[2,800,640]{2,1,0:T(8,128)(2,1)S(1)}, bf16[2,800,640]{2,1,0:T(8,128)(2,1)}, u32[]{:S(2)}, u32[]{:S(2)}) collective-permute-start(bf16[2,800,640]{2,1,0:T(8,128)(2,1)S(1)} %fusion.23.refs_0_), channel_id=1, source_target_pairs={{0,16},{4,20},{8,24},{12,28},{16,0},{20,4},{24,8},{28,12},{1,17},{... | collective-permute-start | bytes 6144008 | tf_op jit(solution)/shard_map/ppermute | solution.py:294
  265.0 11.3 %attend.1 = (bf16[640,512]{1,0:T(8,128)(2,1)}, f32[5,2,512]{2,1,0:T(2,128)}) custom-call(s32[1]{0:T(128)} %bitcast.11.first_ref, bf16[1024,512]{1,0:T(8,128)(2,1)} %copy.112.qn_ref.qr_ref, bf16[1024,512]{1,0:T(8,128)(2,1)} %copy.112.qn_ref.qr_ref, bf16[2560,640]{1,0:T(8,128)(2,1)} %convolution_convert_fusion.4.k_ref, bf16[2560,128]{1,0:T(8,128)(2,1)} %copy.114.kr_ref, ...), custom_call_target="tpu_custom_call" | custom-call | tf_op jit(solution)/shard_map/attend/pallas_call | solution.py:792
  287.8 26.1 %collective-permute-done.8 = bf16[3,800,640]{2,1,0:T(8,128)(2,1)} collective-permute-done((bf16[3,800,640]{2,1,0:T(8,128)(2,1)}, bf16[3,800,640]{2,1,0:T(8,128)(2,1)}, u32[]{:S(2)}, u32[]{:S(2)}) %collective-permute-start.8) | collective-permute-done | bytes 3072032 | tf_op jit(solution)/shard_map/ppermute | solution.py:294
  319.7 21.9 %fold4.1 = f32[128,2560]{1,0:T(8,128)} custom-call(bf16[4,128,2560]{2,1,0:T(8,128)(2,1)} %bitcast.99), custom_call_target="tpu_custom_call" | custom-call | tf_op jit(solution)/shard_map/fold4/pallas_call | solution.py:650
  343.0 10.9 %collective-permute-done.13.refs_2_ = bf16[2,800,640]{2,1,0:T(8,128)(2,1)} collective-permute-done((bf16[2,800,640]{2,1,0:T(8,128)(2,1)S(1)}, bf16[2,800,640]{2,1,0:T(8,128)(2,1)}, u32[]{:S(2)}, u32[]{:S(2)}) %collective-permute-start.13) | collective-permute-done | bytes 2048032 | tf_op jit(solution)/shard_map/ppermute | solution.py:294
  362.2 50.8 %spread5.1 = bf16[8,128,2560]{2,1,0:T(8,128)(2,1)} custom-call(bf16[128,2560]{1,0:T(8,128)(2,1)} %pad_maximum_fusion.21.refs_0_), custom_call_target="tpu_custom_call" | custom-call | tf_op jit(solution)/shard_map/spread5/pallas_call | solution.py:568
  427.8 19.2 %ffn.1 = (f32[1024,800]{1,0:T(8,128)}, f32[1024,800]{1,0:T(8,128)}, bf16[1024,800]{1,0:T(8,128)(2,1)}) custom-call(bf16[1024,2560]{1,0:T(8,128)(2,1)} %bitcast.75, bf16[2,800,640]{2,1,0:T(8,128)(2,1)} %copy-done.4, bf16[2,800,640]{2,1,0:T(8,128)(2,1)} %slice.244.refs_1_, bf16[2,800,640]{2,1,0:T(8,128)(2,1)} %collective-permute-done.13.refs_2_, ...), custom_call_target="tpu_custom_call" | custom-call | tf_op jit(solution)/shard_map/ffn/pallas_call | solution.py:938
  453.2 33.9 %ffn_back.1 = (bf16[1024,800]{1,0:T(8,128)(2,1)}, bf16[1024,800]{1,0:T(8,128)(2,1)}, bf16[1024,2560]{1,0:T(8,128)(2,1)}, bf16[1024,2560]{1,0:T(8,128)(2,1)}) custom-call(bf16[1024,2560]{1,0:T(8,128)(2,1)} %slice_dynamic-update-slice_fusion.dm_ref, f32[1024,800]{1,0:T(8,128)} %get-tuple-element.86.gate_ref, f32[1024,800]{1,0:T(8,128)} %get-tuple-element.87.up_ref, ...), custom_call_target="tpu_custom_call" | custom-call | tf_op jit(solution)/shard_map/ffn_back/pallas_call | solution.py:970
  492.3 30.8 %fold6.1 = f32[128,2560]{1,0:T(8,128)} custom-call(bf16[8,128,2560]{2,1,0:T(8,128)(2,1)} %bitcast.88), custom_call_target="tpu_custom_call" | custom-call | tf_op jit(solution)/shard_map/fold6/pallas_call | solution.py:650
  541.8 22.2 %spread7.1 = bf16[4,128,2560]{2,1,0:T(8,128)(2,1)} custom-call(bf16[128,2560]{1,0:T(8,128)(2,1)} %get-tuple-element.97.refs_0_), custom_call_target="tpu_custom_call" | custom-call | tf_op jit(solution)/shard_map/spread7/pallas_call | solution.py:568
  592.7 20.0 %attend_back.1 = (f32[640,512]{1,0:T(8,128)}, f32[384,512]{1,0:T(8,128)}, bf16[2560,640]{1,0:T(8,128)(2,1)}, bf16[2560,640]{1,0:T(8,128)(2,1)}, f32[2560,128]{1,0:T(8,128)}) custom-call(s32[1]{0:T(128)} %bitcast.11.first_ref, bf16[1024,512]{1,0:T(8,128)(2,1)} %copy.112.qn_ref.qr_ref, bf16[1024,512]{1,0:T(8,128)(2,1)} %copy.112.qn_ref.qr_ref, ...), custom_call_target="tpu_custom_call" | custom-call | tf_op jit(solution)/shard_map/attend_back/pallas_call | solution.py:894
  616.1 11.7 %collective-permute-start.21 = (bf16[800,1280]{1,0:T(8,128)(2,1)}, bf16[800,1280]{1,0:T(8,128)(2,1)}, u32[]{:S(2)}, u32[]{:S(2)}) collective-permute-start(bf16[800,1280]{1,0:T(8,128)(2,1)} %convolution_convert_fusion.7), channel_id=1, source_target_pairs={{0,4},{4,0},{8,12},{12,8},{16,20},{20,16},{24,28},{28,24},{1,5},{5... | collective-permute-start | bytes 6144008 | tf_op jit(solution)/shard_map/ppermute | solution.py:294
  645.5 18.0 %collective-permute-done.24 = bf16[800,640]{1,0:T(8,128)(2,1)} collective-permute-done((bf16[800,640]{1,0:T(8,128)(2,1)}, bf16[800,640]{1,0:T(8,128)(2,1)}, u32[]{:S(2)}, u32[]{:S(2)}) %collective-permute-start.24) | collective-permute-done | bytes 1024032 | tf_op jit(solution)/shard_map/ppermute | solution.py:294
  666.3 10.2 %collective-permute-done.21 = bf16[800,1280]{1,0:T(8,128)(2,1)} collective-permute-done((bf16[800,1280]{1,0:T(8,128)(2,1)}, bf16[800,1280]{1,0:T(8,128)(2,1)}, u32[]{:S(2)}, u32[]{:S(2)}) %collective-permute-start.21) | collective-permute-done | bytes 2048032 | tf_op jit(solution)/shard_map/ppermute | solution.py:294
  678.5 16.5 %collective-permute-start.22 = (bf16[128,2560]{1,0:T(8,128)(2,1)S(1)}, bf16[128,2560]{1,0:T(8,128)(2,1)S(1)}, u32[]{:S(2)}, u32[]{:S(2)}) collective-permute-start(bf16[128,2560]{1,0:T(8,128)(2,1)S(1)} %add_convert_fusion), channel_id=1, source_target_pairs={{0,8},{4,12},{8,0},{12,4},{16,24},{20,28},{24,16},{28,20},{1,9},{5... | collective-permute-start | bytes 1966088 | tf_op jit(solution)/shard_map/ppermute | solution.py:294
  703.9 16.5 %collective-permute-start.32 = (bf16[800,640]{1,0:T(8,128)(2,1)}, bf16[800,640]{1,0:T(8,128)(2,1)}, u32[]{:S(2)}, u32[]{:S(2)}) collective-permute-start(bf16[800,640]{1,0:T(8,128)(2,1)} %split.775), channel_id=1, source_target_pairs={{0,16},{4,20},{8,24},{12,28},{16,0},{20,4},{24,8},{28,12},{1,17},{... | collective-permute-start | bytes 3072008 | tf_op jit(solution)/shard_map/ppermute | solution.py:294
  724.9 43.0 %fold8.1 = (f32[2208,128]{1,0:T(8,128)}, bf16[800,320]{1,0:T(8,128)(2,1)}) custom-call(bf16[2208,512]{1,0:T(8,128)(2,1)} %fusion.58.refs_0_, bf16[800,320]{1,0:T(8,128)(2,1)} %broadcast_select_fusion.15.refs_1_), custom_call_target="tpu_custom_call" | custom-call | tf_op jit(solution)/shard_map/fold8/pallas_call | solution.py:650
  796.7 10.8 %collective-permute-done.31 = f32[288,128]{1,0:T(8,128)} collective-permute-done((f32[288,128]{1,0:T(8,128)}, f32[288,128]{1,0:T(8,128)}, u32[]{:S(2)}, u32[]{:S(2)}) %collective-permute-start.31) | collective-permute-done | bytes 147488 | tf_op jit(solution)/shard_map/ppermute | solution.py:236
  811.0 10.9 %spread9.1 = bf16[1056,512]{1,0:T(8,128)(2,1)} custom-call(bf16[1056,128]{1,0:T(8,128)(2,1)} %pad_maximum_fusion.27.refs_0_), custom_call_target="tpu_custom_call" | custom-call | tf_op jit(solution)/shard_map/spread9/pallas_call | solution.py:568
  833.5 21.3 %fold10.1 = (f32[128,2560]{1,0:T(8,128)}, bf16[800,320]{1,0:T(8,128)(2,1)}) custom-call(bf16[4,128,2560]{2,1,0:T(8,128)(2,1)} %bitcast.96, bf16[800,320]{1,0:T(8,128)(2,1)} %get-tuple-element.115.refs_1_), custom_call_target="tpu_custom_call" | custom-call | tf_op jit(solution)/shard_map/fold10/pallas_call | solution.py:650
  857.3 47.6 %ring_scatter.1 = (f32[2,48,1024]{2,1,0:T(8,128)}, f32[2,16,1280]{2,1,0:T(8,128)}, f32[2,160,384]{2,1,0:T(8,128)}, f32[2,3,128]{2,1,0:T(4,128)}) custom-call(bf16[8,2,48,1024]{3,2,1,0:T(8,128)(2,1)} %bitcast.104, bf16[8,2,16,1280]{3,2,1,0:T(8,128)(2,1)} %bitcast.112, bf16[8,2,160,384]{3,2,1,0:T(8,128)(2,1)} %bitcast.103, f32[8,2,3,128]{3,2,1,0:T(4,128)} %copy.123.refs_3_), custom_call_target="tpu_custom_call" | custom-call | tf_op jit(solution)/shard_map/ring_scatter/pallas_call | solution.py:218
  912.5 16.7 %spread11.1 = (bf16[320,1536]{1,0:T(8,128)(2,1)}, bf16[800,320]{1,0:T(8,128)(2,1)}) custom-call(bf16[320,384]{1,0:T(8,128)(2,1)} %bitcast.110, bf16[800,320]{1,0:T(8,128)(2,1)} %broadcast_select_fusion.12.refs_1_), custom_call_target="tpu_custom_call" | custom-call | tf_op jit(solution)/shard_map/spread11/pallas_call | solution.py:568
  (500 shorter events, 347.0 us)
Async XLA Ops:
  7.2 306.8 %all-gather.2.cloned.1.call-start = ((), (), s32[]{:S(2)}) async-start(), calls=%async_computation.1 | async-start | bytes 3686400 | tf_op jit(solution)/shard_map/all_gather | solution.py:1021
  101.5 28.9 %collective-permute-start.2 = (f32[264,512]{1,0:T(8,128)}, f32[264,512]{1,0:T(8,128)}, u32[]{:S(2)}, u32[]{:S(2)}) collective-permute-start(f32[264,512]{1,0:T(8,128)} %fusion.33), channel_id=1, source_target_pairs={{0,1},{1,0},{2,3},{3,2},{4,5},{5,4},{6,7},{7,6},{8,9},{9,8},{10,11... | collective-permute-start | bytes 1622024 | tf_op jit(solution)/shard_map/ppermute | solution.py:240
  113.4 88.3 %collective-permute-start.3 = (bf16[3,800,320]{1,2,0:T(8,128)(2,1)}, bf16[3,800,320]{1,2,0:T(8,128)(2,1)}, u32[]{:S(2)}, u32[]{:S(2)}) collective-permute-start(bf16[3,800,320]{1,2,0:T(8,128)(2,1)} %copy.111), channel_id=1, source_target_pairs={{0,8},{4,12},{8,0},{12,4},{16,24},{20,28},{24,16},{28,20},{1,9},{5... | collective-permute-start | bytes 4608008 | tf_op jit(solution)/shard_map/ppermute | solution.py:294
  115.7 841.7 %reduce-scatter.2.cloned.1.call-start = ((), (), s32[]{:S(2)}) async-start(), calls=%async_computation.2 | async-start | bytes 3686400 | tf_op jit(solution)/shard_map/reduce_scatter | solution.py:1104
  232.9 44.3 %collective-permute-start.10 = (bf16[256,2560]{1,0:T(8,128)(2,1)S(1)}, bf16[256,2560]{1,0:T(8,128)(2,1)}, u32[]{:S(2)}, u32[]{:S(2)}) collective-permute-start(bf16[256,2560]{1,0:T(8,128)(2,1)S(1)} %copy-done.26), channel_id=1, source_target_pairs={{0,1},{1,0},{2,3},{3,2},{4,5},{5,4},{6,7},{7,6},{8,9},{9,8},{10,11... | collective-permute-start | bytes 3932168 | tf_op jit(solution)/shard_map/ppermute | solution.py:240
  233.0 44.3 %collective-permute-start.11 = (bf16[256,2560]{1,0:T(8,128)(2,1)S(1)}, bf16[256,2560]{1,0:T(8,128)(2,1)}, u32[]{:S(2)}, u32[]{:S(2)}) collective-permute-start(bf16[256,2560]{1,0:T(8,128)(2,1)S(1)} %copy-done.26), channel_id=1, source_target_pairs={{0,2},{1,3},{2,0},{3,1},{4,6},{5,7},{6,4},{7,5},{8,10},{9,11},{10,... | collective-permute-start | bytes 3932168 | tf_op jit(solution)/shard_map/ppermute | solution.py:240
  245.0 68.9 %collective-permute-start.8 = (bf16[3,800,640]{2,1,0:T(8,128)(2,1)}, bf16[3,800,640]{2,1,0:T(8,128)(2,1)}, u32[]{:S(2)}, u32[]{:S(2)}) collective-permute-start(bf16[3,800,640]{2,1,0:T(8,128)(2,1)} %pad_maximum_fusion.1), channel_id=1, source_target_pairs={{0,4},{4,0},{8,12},{12,8},{16,20},{20,16},{24,28},{28,24},{1,5},{5... | collective-permute-start | bytes 9216008 | tf_op jit(solution)/shard_map/ppermute | solution.py:294
  249.5 104.4 %collective-permute-start.13 = (bf16[2,800,640]{2,1,0:T(8,128)(2,1)S(1)}, bf16[2,800,640]{2,1,0:T(8,128)(2,1)}, u32[]{:S(2)}, u32[]{:S(2)}) collective-permute-start(bf16[2,800,640]{2,1,0:T(8,128)(2,1)S(1)} %fusion.23.refs_0_), channel_id=1, source_target_pairs={{0,16},{4,20},{8,24},{12,28},{16,0},{20,4},{24,8},{28,12},{1,17},{... | collective-permute-start | bytes 6144008 | tf_op jit(solution)/shard_map/ppermute | solution.py:294
  354.1 59.0 %collective-permute-start.15 = (bf16[1,800,640]{2,1,0:T(8,128)(2,1)}, bf16[1,800,640]{2,1,0:T(8,128)(2,1)}, u32[]{:S(2)}, u32[]{:S(2)}) collective-permute-start(bf16[1,800,640]{2,1,0:T(8,128)(2,1)} %fusion.42.refs_4_), channel_id=1, source_target_pairs={{0,16},{4,20},{8,24},{12,28},{16,0},{20,4},{24,8},{28,12},{1,17},{... | collective-permute-start | bytes 3072008 | tf_op jit(solution)/shard_map/ppermute | solution.py:294
  360.1 66.4 %collective-permute-start.14 = (bf16[2,800,640]{2,1,0:T(8,128)(2,1)}, bf16[2,800,640]{2,1,0:T(8,128)(2,1)S(1)}, u32[]{:S(2)}, u32[]{:S(2)}) collective-permute-start(bf16[2,800,640]{2,1,0:T(8,128)(2,1)} %collective-permute-done.13.refs_2_), channel_id=1, source_target_pairs={{0,4},{4,0},{8,12},{12,8},{16,20},{20,16},{24,28},{28,24},{1,5},{5... | collective-permute-start | bytes 6144008 | tf_op jit(solution)/shard_map/ppermute | solution.py:294
  413.1 40.1 %collective-permute-start.16 = (bf16[1,800,640]{2,1,0:T(8,128)(2,1)}, bf16[1,800,640]{2,1,0:T(8,128)(2,1)}, u32[]{:S(2)}, u32[]{:S(2)}) collective-permute-start(bf16[1,800,640]{2,1,0:T(8,128)(2,1)} %collective-permute-done.15.refs_6_), channel_id=1, source_target_pairs={{0,4},{4,0},{8,12},{12,8},{16,20},{20,16},{24,28},{28,24},{1,5},{5... | collective-permute-start | bytes 3072008 | tf_op jit(solution)/shard_map/ppermute | solution.py:294
  452.5 89.3 %collective-permute-start.18 = (bf16[800,1280]{1,0:T(8,128)(2,1)}, bf16[800,1280]{1,0:T(8,128)(2,1)}, u32[]{:S(2)}, u32[]{:S(2)}) collective-permute-start(bf16[800,1280]{1,0:T(8,128)(2,1)} %convolution_convert_fusion.8), channel_id=1, source_target_pairs={{0,4},{4,0},{8,12},{12,8},{16,20},{20,16},{24,28},{28,24},{1,5},{5... | collective-permute-start | bytes 6144008 | tf_op jit(solution)/shard_map/ppermute | solution.py:294
  528.2 53.4 %collective-permute-start.23 = (bf16[800,1280]{1,0:T(8,128)(2,1)}, bf16[800,1280]{1,0:T(8,128)(2,1)}, u32[]{:S(2)}, u32[]{:S(2)}) collective-permute-start(bf16[800,1280]{1,0:T(8,128)(2,1)} %convolution_convert_fusion.9), channel_id=1, source_target_pairs={{0,4},{4,0},{8,12},{12,8},{16,20},{20,16},{24,28},{28,24},{1,5},{5... | collective-permute-start | bytes 6144008 | tf_op jit(solution)/shard_map/ppermute | solution.py:294
  572.1 70.1 %collective-permute-start.20 = (bf16[800,640]{1,0:T(8,128)(2,1)}, bf16[800,640]{1,0:T(8,128)(2,1)}, u32[]{:S(2)}, u32[]{:S(2)}) collective-permute-start(bf16[800,640]{1,0:T(8,128)(2,1)} %split.777), channel_id=1, source_target_pairs={{0,16},{4,20},{8,24},{12,28},{16,0},{20,4},{24,8},{28,12},{1,17},{... | collective-permute-start | bytes 3072008 | tf_op jit(solution)/shard_map/ppermute | solution.py:294
  588.9 74.6 %collective-permute-start.24 = (bf16[800,640]{1,0:T(8,128)(2,1)}, bf16[800,640]{1,0:T(8,128)(2,1)}, u32[]{:S(2)}, u32[]{:S(2)}) collective-permute-start(bf16[800,640]{1,0:T(8,128)(2,1)} %split.776), channel_id=1, source_target_pairs={{0,16},{4,20},{8,24},{12,28},{16,0},{20,4},{24,8},{28,12},{1,17},{... | collective-permute-start | bytes 3072008 | tf_op jit(solution)/shard_map/ppermute | solution.py:294
  616.1 60.4 %collective-permute-start.21 = (bf16[800,1280]{1,0:T(8,128)(2,1)}, bf16[800,1280]{1,0:T(8,128)(2,1)}, u32[]{:S(2)}, u32[]{:S(2)}) collective-permute-start(bf16[800,1280]{1,0:T(8,128)(2,1)} %convolution_convert_fusion.7), channel_id=1, source_target_pairs={{0,4},{4,0},{8,12},{12,8},{16,20},{20,16},{24,28},{28,24},{1,5},{5... | collective-permute-start | bytes 6144008 | tf_op jit(solution)/shard_map/ppermute | solution.py:294
  635.0 31.3 %collective-permute-start.19 = (bf16[256,2560]{1,0:T(8,128)(2,1)}, bf16[256,2560]{1,0:T(8,128)(2,1)}, u32[]{:S(2)}, u32[]{:S(2)}) collective-permute-start(bf16[256,2560]{1,0:T(8,128)(2,1)} %pad_maximum_fusion.13), channel_id=1, source_target_pairs={{0,2},{1,3},{2,0},{3,1},{4,6},{5,7},{6,4},{7,5},{8,10},{9,11},{10,... | collective-permute-start | bytes 3932168 | tf_op jit(solution)/shard_map/ppermute | solution.py:240
  678.5 46.4 %collective-permute-start.22 = (bf16[128,2560]{1,0:T(8,128)(2,1)S(1)}, bf16[128,2560]{1,0:T(8,128)(2,1)S(1)}, u32[]{:S(2)}, u32[]{:S(2)}) collective-permute-start(bf16[128,2560]{1,0:T(8,128)(2,1)S(1)} %add_convert_fusion), channel_id=1, source_target_pairs={{0,8},{4,12},{8,0},{12,4},{16,24},{20,28},{24,16},{28,20},{1,9},{5... | collective-permute-start | bytes 1966088 | tf_op jit(solution)/shard_map/ppermute | solution.py:294
  703.9 129.6 %collective-permute-start.32 = (bf16[800,640]{1,0:T(8,128)(2,1)}, bf16[800,640]{1,0:T(8,128)(2,1)}, u32[]{:S(2)}, u32[]{:S(2)}) collective-permute-start(bf16[800,640]{1,0:T(8,128)(2,1)} %split.775), channel_id=1, source_target_pairs={{0,16},{4,20},{8,24},{12,28},{16,0},{20,4},{24,8},{28,12},{1,17},{... | collective-permute-start | bytes 3072008 | tf_op jit(solution)/shard_map/ppermute | solution.py:294
  790.5 40.5 %collective-permute-start.25 = (f32[128,640]{1,0:T(8,128)}, f32[128,640]{1,0:T(8,128)}, u32[]{:S(2)}, u32[]{:S(2)}) collective-permute-start(f32[128,640]{1,0:T(8,128)} %get-tuple-element.244), channel_id=1, source_target_pairs={{0,3},{1,2},{2,1},{3,0},{4,7},{5,6},{6,5},{7,4},{8,11},{9,10},{10,... | collective-permute-start | bytes 983048 | tf_op jit(solution)/shard_map/ppermute | solution.py:240
  791.3 39.7 %collective-permute-start.26 = (f32[128,640]{1,0:T(8,128)}, f32[128,640]{1,0:T(8,128)}, u32[]{:S(2)}, u32[]{:S(2)}) collective-permute-start(f32[128,640]{1,0:T(8,128)} %get-tuple-element.198), channel_id=1, source_target_pairs={{0,2},{1,3},{2,0},{3,1},{4,6},{5,7},{6,4},{7,5},{8,10},{9,11},{10,... | collective-permute-start | bytes 983048 | tf_op jit(solution)/shard_map/ppermute | solution.py:240
  796.7 34.3 %collective-permute-start.27 = (f32[128,640]{1,0:T(8,128)}, f32[128,640]{1,0:T(8,128)}, u32[]{:S(2)}, u32[]{:S(2)}) collective-permute-start(f32[128,640]{1,0:T(8,128)} %get-tuple-element.243), channel_id=1, source_target_pairs={{0,1},{1,0},{2,3},{3,2},{4,5},{5,4},{6,7},{7,6},{8,9},{9,8},{10,11... | collective-permute-start | bytes 983048 | tf_op jit(solution)/shard_map/ppermute | solution.py:240
  907.4 31.1 %collective-permute-start.36 = (f32[768]{0:T(1024)S(1)}, f32[768]{0:T(1024)S(1)}, u32[]{:S(2)}, u32[]{:S(2)}) collective-permute-start(f32[768]{0:T(1024)S(1)} %reshape_reshape.7), channel_id=1, source_target_pairs={{0,1},{1,0},{2,3},{3,2},{4,5},{5,4},{6,7},{7,6},{8,9},{9,8},{10,11... | collective-permute-start | bytes 9224 | tf_op jit(solution)/shard_map/ppermute | solution.py:240
  909.0 46.0 %collective-permute-start.33 = (f32[128,640]{1,0:T(8,128)}, f32[128,640]{1,0:T(8,128)}, u32[]{:S(2)}, u32[]{:S(2)}) collective-permute-start(f32[128,640]{1,0:T(8,128)} %get-tuple-element.239), channel_id=1, source_target_pairs={{0,3},{1,2},{2,1},{3,0},{4,7},{5,6},{6,5},{7,4},{8,11},{9,10},{10,... | collective-permute-start | bytes 983048 | tf_op jit(solution)/shard_map/ppermute | solution.py:240
  (113 other events, 1162.4 us)
Sparse Core Ops, SparseCore 0:
  115.9 85.6 all-gather.1
  636.3 130.1 reduce-scatter.1

commit v4 on v3

--- a/solution.py
+++ b/solution.py
@@ -23,6 +23,7 @@
 SCALE = (DN + DR) ** (-0.5)
 VMEM_LIMIT = 56 << 20
 MESH = pl.DeviceIdType.MESH
+PAIR = 2
 bf = jnp.bfloat16
 f32 = jnp.float32
 
@@ -47,17 +48,22 @@
     pl.semaphore_wait(barrier, len(others))
 
 
+def col_peers(column, cols):
+    return [flip(flip(column, 1) if k & 1 else column, 2) if k & 2 else flip(column, 1) for k in range(1, cols)]
+
+
 def ring_gather_kernel(rows, n, *refs):
-    blocks, (tokens_ref, back_ref), refs = refs[:n], refs[n : n + 2], refs[n + 2 :]
-    wholes, (features_ref, own_back_ref), refs = refs[:n], refs[n : n + 2], refs[n + 2 :]
+    blocks, (tokens_ref, back_ref, away_ref), refs = refs[:n], refs[n : n + 3], refs[n + 3 :]
+    wholes, (features_ref, own_back_ref, came_ref), refs = refs[:n], refs[n : n + 3], refs[n + 3 :]
     own_sem, send_sem, recv_sem, col_send, col_recv = refs
     row, column = lax.axis_index("row"), lax.axis_index("col")
     place = ring_place(row, rows)
     ends = (ring_row((place + 1) % rows, rows), ring_row((place + rows - 1) % rows, rows))
     cols = features_ref.shape[1] // tokens_ref.shape[1]
     quarter = back_ref.shape[0] // cols
-    peers = [flip(flip(column, 1) if k & 1 else column, 2) if k & 2 else flip(column, 1) for k in range(1, cols)]
-    ring_barrier([(ends[0], column), (ends[1], column)] + [(row, peer) for peer in peers])
+    peers = col_peers(column, cols)
+    partner = (flip(row, PAIR), column)
+    ring_barrier([(ends[0], column), (ends[1], column), partner] + [(row, peer) for peer in peers])
     lanes = pl.ds(pl.multiple_of(column * tokens_ref.shape[1], 128), tokens_ref.shape[1])
 
     def to_col(k, target):
@@ -77,6 +83,16 @@
                     device_id_type=MESH,
                 )
             )
+    crossing.append(
+        pltpu.make_async_remote_copy(
+            src_ref=away_ref,
+            dst_ref=came_ref,
+            send_sem=col_send.at[2, 0],
+            recv_sem=col_recv.at[2, 0],
+            device_id=partner,
+            device_id_type=MESH,
+        )
+    )
     staying = [
         pltpu.make_async_copy(source, there, own_sem.at[n + which])
         for which, (source, there) in enumerate(to_col(-1, column))
@@ -128,39 +144,74 @@
         copy.wait()
 
 
-def ring_gather(blocks, tokens, back):
+def ring_gather(blocks, tokens, back, away):
     rows, cols, n = lax.axis_size("row"), lax.axis_size("col"), len(blocks)
     halves = [block.reshape(2, block.shape[0] // 2, block.shape[1]) for block in blocks]
     anywhere = pl.BlockSpec(memory_space=pl.ANY)
-    *wholes, features, own_back = pl.pallas_call(
+    *wholes, features, own_back, came = pl.pallas_call(
         functools.partial(ring_gather_kernel, rows, n),
         out_shape=[jax.ShapeDtypeStruct((rows,) + half.shape, half.dtype) for half in halves]
         + [
             jax.ShapeDtypeStruct((tokens.shape[0], cols * tokens.shape[1]), tokens.dtype),
             jax.ShapeDtypeStruct((back.shape[0] // cols, cols * back.shape[1]), back.dtype),
+            jax.ShapeDtypeStruct(away.shape, away.dtype),
         ],
-        in_specs=[anywhere] * (n + 2),
-        out_specs=[anywhere] * (n + 2),
+        in_specs=[anywhere] * (n + 3),
+        out_specs=[anywhere] * (n + 3),
         scratch_shapes=[
             pltpu.SemaphoreType.DMA((n + 2,)),
             pltpu.SemaphoreType.DMA((rows - 1, 2, n)),
             pltpu.SemaphoreType.DMA((rows - 1, 2, n)),
-            pltpu.SemaphoreType.DMA((2, cols - 1)),
-            pltpu.SemaphoreType.DMA((2, cols - 1)),
+            pltpu.SemaphoreType.DMA((3, cols - 1)),
+            pltpu.SemaphoreType.DMA((3, cols - 1)),
         ],
         compiler_params=pltpu.CompilerParams(collective_id=0, has_side_effects=True),
         name="ring_gather",
-    )(*halves, tokens, back)
+    )(*halves, tokens, back, away)
     wholes = [whole.reshape(rows * block.shape[0], block.shape[1]) for whole, block in zip(wholes, blocks)]
-    return wholes, features, own_back
-
-
-def ring_scatter_kernel(rows, n, *refs):
-    terms, sums, slots, (send_sem, recv_sem) = refs[:n], refs[n : 2 * n], refs[2 * n : 3 * n], refs[3 * n :]
+    return wholes, features, own_back, came
+
+
+def ring_scatter_kernel(rows, n, extra, *refs):
+    terms, away_ref, leaving, refs = refs[:n], refs[n], refs[n + 1 : n + 1 + extra], refs[n + 1 + extra :]
+    sums, came_ref, arriving, refs = refs[:n], refs[n], refs[n + 1 : n + 1 + extra], refs[n + 1 + extra :]
+    slots, refs = refs[:n], refs[n:]
+    send_sem, recv_sem, swap_send, swap_recv, own_sem, col_send, col_recv = refs
     row, column = lax.axis_index("row"), lax.axis_index("col")
     place = ring_place(row, rows)
     ends = (ring_row((place + 1) % rows, rows), ring_row((place + rows - 1) % rows, rows))
-    ring_barrier([(ends[0], column), (ends[1], column)])
+    partner = (flip(row, PAIR), column)
+    cols = lax.axis_size("col")
+    peers = col_peers(column, cols)
+    ring_barrier([(ends[0], column), (ends[1], column), partner] + [(row, peer) for peer in peers])
+    crossing = []
+    for e in range(extra):
+        quarter, width = leaving[e].shape[0], leaving[e].shape[1] // cols
+        place_there = arriving[e].at[pl.ds(pl.multiple_of(column * quarter, 128), quarter)]
+
+        def features(target):
+            return leaving[e].at[:, pl.ds(pl.multiple_of(target * width, 128), width)]
+
+        crossing.append(pltpu.make_async_copy(features(column), place_there, own_sem.at[e]))
+        for k, peer in enumerate(peers):
+            crossing.append(
+                pltpu.make_async_remote_copy(
+                    src_ref=features(peer),
+                    dst_ref=place_there,
+                    send_sem=col_send.at[e, k],
+                    recv_sem=col_recv.at[e, k],
+                    device_id=(row, peer),
+                    device_id_type=MESH,
+                )
+            )
+    swap = pltpu.make_async_remote_copy(
+        src_ref=away_ref,
+        dst_ref=came_ref,
+        send_sem=swap_send,
+        recv_sem=swap_recv,
+        device_id=partner,
+        device_id_type=MESH,
+    )
 
     def target(step, side):
         return ring_row((place + (1 + step if side else 2 * rows - 1 - step)) % rows, rows)
@@ -184,6 +235,9 @@
     for k in range(n):
         for side in (0, 1):
             first(side, k).start()
+    swap.start()
+    for copy in crossing:
+        copy.start()
 
     def arrive(step, side, k):
         return hop(step, side, k, slots[k].at[step, side])
@@ -210,24 +264,33 @@
         return carry
 
     lax.fori_loop(0, rows - 1, drain, 0)
-
-
-def ring_scatter(*terms):
+    swap.wait()
+    for copy in crossing:
+        copy.wait()
+
+
+def ring_scatter(terms, away, leaving):
     rows, n = lax.axis_size("row"), len(terms)
     split = [term.reshape(rows, 2, term.shape[0] // rows // 2, term.shape[1]) for term in terms]
-    sums = pl.pallas_call(
-        functools.partial(ring_scatter_kernel, rows, n),
-        out_shape=[jax.ShapeDtypeStruct(term.shape[1:], f32) for term in split],
-        in_specs=[pl.BlockSpec(memory_space=pltpu.VMEM)] * n,
-        out_specs=[pl.BlockSpec(memory_space=pltpu.VMEM)] * n,
+    anywhere = pl.BlockSpec(memory_space=pl.ANY)
+    cols, extra = lax.axis_size("col"), len(leaving)
+    *sums, came, first, second = pl.pallas_call(
+        functools.partial(ring_scatter_kernel, rows, n, extra),
+        out_shape=[jax.ShapeDtypeStruct(term.shape[1:], f32) for term in split]
+        + [jax.ShapeDtypeStruct(away.shape, away.dtype)]
+        + [jax.ShapeDtypeStruct((v.shape[0] * cols, v.shape[1] // cols), v.dtype) for v in leaving],
+        in_specs=[pl.BlockSpec(memory_space=pltpu.VMEM)] * n + [anywhere] * (1 + extra),
+        out_specs=[pl.BlockSpec(memory_space=pltpu.VMEM)] * n + [anywhere] * (1 + extra),
         scratch_shapes=[pltpu.VMEM((rows - 1,) + term.shape[1:], term.dtype) for term in split]
-        + [pltpu.SemaphoreType.DMA((rows - 1, 2, n)), pltpu.SemaphoreType.DMA((rows - 1, 2, n))],
+        + [pltpu.SemaphoreType.DMA((rows - 1, 2, n)), pltpu.SemaphoreType.DMA((rows - 1, 2, n))]
+        + [pltpu.SemaphoreType.DMA, pltpu.SemaphoreType.DMA, pltpu.SemaphoreType.DMA((extra,))]
+        + [pltpu.SemaphoreType.DMA((extra, cols - 1)), pltpu.SemaphoreType.DMA((extra, cols - 1))],
         compiler_params=pltpu.CompilerParams(
             collective_id=1, has_side_effects=True, vmem_limit_bytes=VMEM_LIMIT
         ),
         name="ring_scatter",
-    )(*split)
-    return [total.reshape(total.shape[0] * total.shape[1], total.shape[2]) for total in sums]
+    )(*split, away, *leaving)
+    return [total.reshape(total.shape[0] * total.shape[1], total.shape[2]) for total in sums], came, (first, second)
 
 
 def from_behind(value, steps):
@@ -269,16 +332,8 @@
     return beside + swap_col(across.astype(bf), 2).astype(f32)
 
 
-def col_exchange(pieces):
-    mine = by_owner(pieces)
-    return by_owner([mine[0]] + [swap_col(mine[k], k) for k in range(1, len(mine))])
-
-
 def quarters(value, axis):
     return jnp.split(value, lax.axis_size("col"), axis=axis)
-
-
-PAIR = 2
 
 
 def group_row(group, side):
@@ -365,33 +420,34 @@
 
 
 class HiddenGather:
-    def __init__(self, blocks, late):
-        self.late = late
-        mine, self.away = pair_halves(blocks, 1)
-        self.came = swap_row(self.away, PAIR)
-        self.own = in_pair_order(mine, self.came, 2)
-
-    def near_own(self, mark):
-        self.beside = swap_row(after(self.own, mark), group_masks()[-1][1])
-
-    def far(self, late, mark):
-        n = self.own.shape[0]
-        own = after(self.own[n - self.late :] if late else self.own[: n - self.late], mark)
-        pieces = {0: own}
+    def __init__(self, blocks):
+        self.mine, self.away = pair_halves(blocks, 1)
+        self.pieces = [{} for _ in range(blocks.shape[0])]
+
+    def arrived(self, came):
+        self.own = in_pair_order(self.mine, came, 2)
+        for which, pieces in enumerate(self.pieces):
+            pieces[0] = (self.own, which)
+
+    def near_own(self, first, last, mark):
+        beside = swap_row(after(self.own[first:last], mark), group_masks()[-1][1])
+        for which in range(first, last):
+            self.pieces[which][1] = (beside, which - first)
+        return beside
+
+    def far(self, which, mark):
+        moved = {0: after(self.own[which : which + 1], mark)}
         for bit, mask in group_masks()[:-1]:
-            for k in list(pieces):
-                pieces[k ^ bit] = swap_row(pieces[k], mask)
-        return pieces
-
-    def near(self, pieces, late, mark):
-        n = self.own.shape[0]
-        part = slice(n - self.late, n) if late else slice(0, n - self.late)
-        done = {0: self.own[part], 1: self.beside[part]}
-        for k in pieces:
-            if k:
-                done[k] = pieces[k]
-                done[k ^ 1] = swap_row(after(pieces[k], mark), group_masks()[-1][1])
-        return [done[k] for k in range(len(done))]
+            for k in list(moved):
+                moved[k ^ bit] = swap_row(moved[k], mask)
+        self.pieces[which].update((k, (piece, 0)) for k, piece in moved.items() if k)
+        return [piece for k, piece in moved.items() if k]
+
+    def near(self, which, mark):
+        pieces = self.pieces[which]
+        for k in [k for k in pieces if k > 1]:
+            pieces[k ^ 1] = (swap_row(after(pieces[k][0], mark), group_masks()[-1][1]), 0)
+        return [pieces[k] for k in range(len(pieces))]
 
 
 class HiddenScatter:
@@ -581,6 +637,69 @@
     )(*([own] if cargo is None else [own, cargo]))
     whole = whole if lanes else whole.reshape(count * own.shape[0], own.shape[1])
     return (whole, swapped[0]) if swapped else whole
+
+
+def behind_kernel(reach, key_ref, all_ref, own_sem, send_sem, recv_sem):
+    rows, cols = lax.axis_size("row"), lax.axis_size("col")
+    row, column = lax.axis_index("row"), lax.axis_index("col")
+    count = key_ref.shape[1]
+    quarter = count // cols
+    beside, across = (row, flip(column, 1)), (row, flip(column, 2))
+    ring_barrier([((row + rows - k) % rows, column) for k in range(1, reach + 1)] + [beside, across])
+    own = pltpu.make_async_copy(key_ref, all_ref.at[:, pl.ds(reach * count, count)], own_sem)
+    own.start()
+
+    def view(k, mask):
+        owner = flip(flip(column, 1) if mask & 1 else column, 2) if mask & 2 else (flip(column, 1) if mask else column)
+        return all_ref.at[:, pl.ds(pl.multiple_of((reach - k) * count + owner * quarter, 128), quarter)]
+
+    def hop(k, mask, target, there, source=None):
+        return pltpu.make_async_remote_copy(
+            src_ref=view(k, mask) if source is None else source,
+            dst_ref=view(k, mask),
+            send_sem=send_sem.at[k - 1, there],
+            recv_sem=recv_sem.at[k - 1, there],
+            device_id=target,
+            device_id_type=MESH,
+        )
+
+    mine = key_ref.at[:, pl.ds(pl.multiple_of(column * quarter, 128), quarter)]
+    sent = []
+    for k in range(1, reach + 1):
+        sent.append(hop(k, 0, ((row + k) % rows, column), 0, mine))
+        sent[-1].start()
+    for k in range(1, reach + 1):
+        hop(k, 0, beside, 0).wait_recv()
+        sent += [hop(k, 0, across, 2), hop(k, 0, beside, 1)]
+        sent[-2].start()
+        sent[-1].start()
+    for k in range(1, reach + 1):
+        hop(k, 2, across, 2).wait_recv()
+        sent.append(hop(k, 2, beside, 3))
+        sent[-1].start()
+    for k in range(1, reach + 1):
+        hop(k, 1, beside, 1).wait_recv()
+        hop(k, 3, beside, 3).wait_recv()
+    for copy in sent:
+        copy.wait_send()
+    own.wait()
+
+
+def gather_behind(key, reach):
+    height, count = key.shape
+    return pl.pallas_call(
+        functools.partial(behind_kernel, reach),
+        out_shape=jax.ShapeDtypeStruct((height, (reach + 1) * count), key.dtype),
+        in_specs=[pl.BlockSpec(memory_space=pl.ANY)],
+        out_specs=pl.BlockSpec(memory_space=pl.ANY),
+        scratch_shapes=[
+            pltpu.SemaphoreType.DMA,
+            pltpu.SemaphoreType.DMA((reach, 4)),
+            pltpu.SemaphoreType.DMA((reach, 4)),
+        ],
+        compiler_params=pltpu.CompilerParams(collective_id=2, has_side_effects=True),
+        name="gather_behind",
+    )(key)
 
 
 def fold_kernel(dims, parts, lanes, relative, cargo, *refs):
@@ -737,36 +856,49 @@
     return (plain, turned)
 
 
-def attend_kernel(blocks, first_ref, qn_ref, qr_ref, k_ref, kr_ref, vt_ref, bias_ref, o_ref, lse_ref, s_ref):
+def attend_kernel(
+    blocks, first_ref, qn_ref, qr_ref, k_ref, kr_ref, vt_ref, bias_ref, o_ref, wide_ref, lse_ref, s_ref
+):
     step = pl.program_id(0)
     first = first_ref[0]
     count = qn_ref.shape[1]
-    for side in (0, 1):
+    sides = (0, 1)
+    rights = []
+    for side in sides:
         plain, turned = head_rows(step, side, qn_ref.shape, 0)
-        right = jnp.concatenate([qn_ref[...] * plain, qr_ref[...] * turned], axis=0)
-
-        def score(j, top):
-            rows = pl.ds(pl.multiple_of(j * BLOCK, BLOCK), BLOCK)
-            left = jnp.concatenate([k_ref[rows, :], kr_ref[rows, :]], axis=1)
-            s = multiply(left, right) * (SCALE * LOG2E) + bias_ref[rows, :]
-            s_ref[rows, :] = s
-            return jnp.maximum(top, jnp.max(s, axis=0, keepdims=True))
-
-        top = lax.fori_loop(first, blocks, score, jnp.full((1, count), NEG, f32))
-
-        def gather(j, carry):
-            total, out = carry
-            rows = pl.ds(pl.multiple_of(j * BLOCK, BLOCK), BLOCK)
-            chance = jnp.exp2(s_ref[rows, :] - top)
+        rights.append(jnp.concatenate([qn_ref[...] * plain, qr_ref[...] * turned], axis=0))
+
+    def score(j, tops):
+        rows = pl.ds(pl.multiple_of(j * BLOCK, BLOCK), BLOCK)
+        left = jnp.concatenate([k_ref[rows, :], kr_ref[rows, :]], axis=1)
+        new = []
+        for side in sides:
+            s = multiply(left, rights[side]) * (SCALE * LOG2E) + bias_ref[rows, :]
+            s_ref[side, rows, :] = s
+            new.append(jnp.maximum(tops[side], jnp.max(s, axis=0, keepdims=True)))
+        return tuple(new)
+
+    tops = lax.fori_loop(first, blocks, score, (jnp.full((1, count), NEG, f32),) * 2)
+
+    def gather(j, carry):
+        rows = pl.ds(pl.multiple_of(j * BLOCK, BLOCK), BLOCK)
+        new = []
+        for side in sides:
+            total, out = carry[side]
+            chance = jnp.exp2(s_ref[side, rows, :] - tops[side])
             total = total + jnp.sum(chance, axis=0, keepdims=True)
             out = out + multiply(vt_ref[side * DV : (side + 1) * DV, rows], chance.astype(bf))
-            return (total, out)
-
-        total, out = lax.fori_loop(
-            first, blocks, gather, (jnp.zeros((1, count), f32), jnp.zeros((DV, count), f32))
-        )
-        o_ref[side * DV : (side + 1) * DV, :] = (out / total).astype(bf)
-        lse_ref[0, side : side + 1, :] = top + jnp.log2(total)
+            new.append((total, out))
+        return tuple(new)
+
+    start = (jnp.zeros((1, count), f32), jnp.zeros((DV, count), f32))
+    sums = lax.fori_loop(first, blocks, gather, (start, start))
+    for side in sides:
+        total, out = sums[side]
+        out = out / total
+        o_ref[side * DV : (side + 1) * DV, :] = out.astype(bf)
+        wide_ref[side * DV : (side + 1) * DV, :] = out
+        lse_ref[0, side : side + 1, :] = tops[side] + jnp.log2(total)
 
 
 def attend(first, query, keys, turned_keys, values_t, bias, heads):
@@ -785,15 +917,17 @@
         ],
         out_specs=[
             pl.BlockSpec((128, count), lambda p, s: (p, 0)),
+            pl.BlockSpec((128, count), lambda p, s: (p, 0)),
             pl.BlockSpec((1, 2, count), lambda p, s: (p, 0, 0)),
         ],
-        scratch_shapes=[pltpu.VMEM((kl, count), f32)],
+        scratch_shapes=[pltpu.VMEM((2, kl, count), f32)],
     )
     return pl.pallas_call(
         functools.partial(attend_kernel, kl // BLOCK),
         grid_spec=grid,
         out_shape=[
             jax.ShapeDtypeStruct((heads * DV, count), bf),
+            jax.ShapeDtypeStruct((heads * DV, count), f32),
             jax.ShapeDtypeStruct((pairs, 2, count), f32),
         ],
         compiler_params=pltpu.CompilerParams(vmem_limit_bytes=VMEM_LIMIT),
@@ -802,12 +936,13 @@
 
 
 def attend_back_kernel(
-    blocks, first_ref, qn_ref, qr_ref, qnn_ref, qrn_ref, k_ref, kr_ref, kt_ref, krt_ref, v_ref, dot_ref, do_ref,
-    bias_ref, lse_ref, dqn_ref, dqr_ref, dk_ref, dv_ref, dkr_ref, p_ref, dp_ref,
+    blocks, first_ref, qn_ref, qr_ref, qnn_ref, qrn_ref, k_ref, kr_ref, kt_ref, krt_ref, v_ref, dot_ref, do_ref, o_ref,
+    bias_ref, lse_ref, dqn_ref, dqr_ref, dk_ref, dv_ref, dkr_ref,
 ):
     step = pl.program_id(0)
     first = first_ref[0]
     count = qn_ref.shape[1]
+    sides = (0, 1)
 
     @pl.when(step == 0)
     def _():
@@ -819,46 +954,47 @@
 
     dk_ref[...] = jnp.zeros_like(dk_ref)
     dv_ref[...] = jnp.zeros_like(dv_ref)
-    for side in (0, 1):
+    rights, out_rights, query_rights, value_rights, lses, deltas = [], [], [], [], [], []
+    for side in sides:
         plain, turned = head_rows(step, side, qn_ref.shape, 0)
-        right = jnp.concatenate([qn_ref[...] * plain, qr_ref[...] * turned], axis=0)
-        out_right = dot_ref[...] * plain
-        lse = lse_ref[0, side : side + 1, :]
-
-        def score(j, delta):
-            rows = pl.ds(pl.multiple_of(j * BLOCK, BLOCK), BLOCK)
-            left = jnp.concatenate([k_ref[rows, :], kr_ref[rows, :]], axis=1)
-            s = multiply(left, right) * (SCALE * LOG2E) + bias_ref[rows, :]
-            chance = jnp.exp2(s - lse)
-            p_ref[rows, :] = chance
-            back = multiply(v_ref[rows, :], out_right)
-            dp_ref[rows, :] = back
-            return delta + jnp.sum(chance * back, axis=0, keepdims=True)
-
-        delta = lax.fori_loop(first, blocks, score, jnp.zeros((1, count), f32))
+        rights.append(jnp.concatenate([qn_ref[...] * plain, qr_ref[...] * turned], axis=0))
+        out_rights.append(dot_ref[...] * plain)
         plain_l, turned_l = head_rows(step, side, qnn_ref.shape, 1)
-        query_right = jnp.concatenate([qnn_ref[...] * plain_l, qrn_ref[...] * turned_l], axis=1)
-        value_right = do_ref[...] * plain_l
-
-        def spread(j, dq):
-            rows = pl.ds(pl.multiple_of(j * BLOCK, BLOCK), BLOCK)
-            chance = p_ref[rows, :]
-            ds = (chance * (dp_ref[rows, :] - delta)).astype(bf)
-            left = jnp.concatenate([kt_ref[:, rows], krt_ref[:, rows]], axis=0)
-            dq = dq + multiply(left, ds)
-            dk = multiply(ds, query_right)
-            dk_ref[rows, :] += (dk[:, :128] * SCALE).astype(bf)
-            dkr_ref[rows, :] += dk[:, 128:] * SCALE
-            dv_ref[rows, :] += multiply(chance.astype(bf), value_right).astype(bf)
-            return dq
-
-        dq = lax.fori_loop(first, blocks, spread, jnp.zeros((256, count), f32)) * SCALE
+        query_rights.append(jnp.concatenate([qnn_ref[...] * plain_l, qrn_ref[...] * turned_l], axis=1))
+        value_rights.append(do_ref[...] * plain_l)
+        lses.append(lse_ref[0, side : side + 1, :])
+        rows = slice(side * DV, (side + 1) * DV)
+        deltas.append(jnp.sum(dot_ref[rows, :].astype(f32) * o_ref[rows, :], axis=0, keepdims=True))
+
+    def block(j, dqs):
+        rows = pl.ds(pl.multiple_of(j * BLOCK, BLOCK), BLOCK)
+        left = jnp.concatenate([k_ref[rows, :], kr_ref[rows, :]], axis=1)
+        left_t = jnp.concatenate([kt_ref[:, rows], krt_ref[:, rows]], axis=0)
+        new, dk, dv = [], 0.0, 0.0
+        for side in sides:
+            s = multiply(left, rights[side]) * (SCALE * LOG2E) + bias_ref[rows, :]
+            chance = jnp.exp2(s - lses[side])
+            back = multiply(v_ref[rows, :], out_rights[side])
+            ds = (chance * (back - deltas[side])).astype(bf)
+            new.append(dqs[side] + multiply(left_t, ds))
+            dk = dk + multiply(ds, query_rights[side])
+            dv = dv + multiply(chance.astype(bf), value_rights[side])
+        dk_ref[rows, :] = (dk[:, :128] * SCALE).astype(bf)
+        dkr_ref[rows, :] += dk[:, 128:] * SCALE
+        dv_ref[rows, :] = dv.astype(bf)
+        return tuple(new)
+
+    dqs = lax.fori_loop(first, blocks, block, (jnp.zeros((256, count), f32),) * 2)
+    place = lax.broadcasted_iota(jnp.int32, (128, count), 0)
+    for side in sides:
+        dq = dqs[side] * SCALE
         dqn_ref[side * DN : (side + 1) * DN, :] = dq[side * DN : (side + 1) * DN]
-        place = lax.broadcasted_iota(jnp.int32, (128, count), 0)
         dqr_ref[...] += jnp.where((place % 64) // 16 == 2 * (step % 2) + side, dq[128:], 0.0)
 
 
-def attend_back(first, query, query_n, keys, turned_keys, keys_t, turned_keys_t, values, do_t, do, bias, lse, heads):
+def attend_back(
+    first, query, query_n, keys, turned_keys, keys_t, turned_keys_t, values, do_t, do, out, bias, lse, heads
+):
     count, kl = query.shape[1], keys.shape[0]
     pairs, base, tiles = heads // 2, heads * DN // 128, -(-heads // 4)
     across = lambda p, s: (0, p)
@@ -879,6 +1015,7 @@
             pl.BlockSpec((kl, 128), across),
             pl.BlockSpec((128, count), along),
             pl.BlockSpec((count, 128), across),
+            pl.BlockSpec((128, count), along),
             pl.BlockSpec((kl, count), fixed),
             pl.BlockSpec((1, 2, count), lambda p, s: (p, 0, 0)),
         ],
@@ -889,7 +1026,6 @@
             pl.BlockSpec((kl, 128), across),
             pl.BlockSpec((kl, 128), fixed),
         ],
-        scratch_shapes=[pltpu.VMEM((kl, count), f32), pltpu.VMEM((kl, count), f32)],
     )
     return pl.pallas_call(
         functools.partial(attend_back_kernel, kl // BLOCK),
@@ -903,72 +1039,75 @@
         ],
         compiler_params=pltpu.CompilerParams(vmem_limit_bytes=VMEM_LIMIT),
         name="attend_back",
-    )(first, query, query, query_n, query_n, keys, turned_keys, keys_t, turned_keys_t, values, do_t, do, bias, lse)
+    )(first, query, query, query_n, query_n, keys, turned_keys, keys_t, turned_keys_t, values, do_t, do, out, bias, lse)
 
 
 TOKENS = 256
 
 
-def dot_pieces(left, pieces, which):
+def dot_pieces(left, pieces):
     width = pieces[0].shape[2]
     total = None
     for k, piece in enumerate(pieces):
-        term = against(left[:, k * width : (k + 1) * width], piece[which])
+        term = against(left[:, k * width : (k + 1) * width], piece[0])
         total = term if total is None else total + term
     return total
 
 
 def ffn_kernel(n, x_ref, *refs):
-    pieces, (gate_ref, up_ref, hidden_ref) = refs[:n], refs[n:]
-    gate = dot_pieces(x_ref, pieces, 0)
-    upward = dot_pieces(x_ref, pieces, 1)
+    gate = dot_pieces(x_ref, refs[:n])
+    upward = dot_pieces(x_ref, refs[n : 2 * n])
+    gate_ref, up_ref, hidden_ref = refs[2 * n :]
     gate_ref[...] = gate
     up_ref[...] = upward
     hidden_ref[...] = (gate / (1.0 + jnp.exp(-gate)) * upward).astype(bf)
 
 
-def piece_specs(pieces, count):
-    shape = (count,) + pieces[0].shape[1:]
-    return [pl.BlockSpec(shape, lambda i: (0, 0, 0), pipeline_mode=pl.Buffered(1)) for _ in pieces]
-
-
-def ffn(x, pieces):
-    tokens, hidden = x.shape[0], pieces[0].shape[1]
+def piece_specs(pieces):
+    def spec(array, index):
+        return pl.BlockSpec((1,) + array.shape[1:], lambda i: (index, 0, 0), pipeline_mode=pl.Buffered(1))
+
+    return [spec(array, index) for array, index in pieces]
+
+
+def ffn(x, gate, up):
+    tokens, hidden = x.shape[0], gate[0][0].shape[1]
     tile = lambda width: pl.BlockSpec((TOKENS, width), lambda i: (i, 0))
     return pl.pallas_call(
-        functools.partial(ffn_kernel, len(pieces)),
+        functools.partial(ffn_kernel, len(gate)),
         grid=(tokens // TOKENS,),
         out_shape=[
             jax.ShapeDtypeStruct((tokens, hidden), f32),
             jax.ShapeDtypeStruct((tokens, hidden), f32),
             jax.ShapeDtypeStruct((tokens, hidden), bf),
         ],
-        in_specs=[tile(x.shape[1])] + piece_specs(pieces, 2),
+        in_specs=[tile(x.shape[1])] + piece_specs(gate + up),
         out_specs=[tile(hidden)] * 3,
         compiler_params=pltpu.CompilerParams(vmem_limit_bytes=VMEM_LIMIT),
         name="ffn",
-    )(x, *pieces)
+    )(x, *[array for array, _ in gate + up])
 
 
 def ffn_back_kernel(n, dm_ref, gate_ref, up_ref, hidden_ref, *refs):
-    first, down, (dgate_ref, dup_ref, dx_ref, out_ref) = refs[:n], refs[n : 2 * n], refs[2 * n :]
+    gates, ups, down = refs[:n], refs[n : 2 * n], refs[2 * n : 3 * n]
+    dgate_ref, dup_ref, dx_ref, out_ref = refs[3 * n :]
     width = down[0].shape[2]
-    back_hidden = dot_pieces(dm_ref, down, 0)
+    back_hidden = dot_pieces(dm_ref, down)
     gate, upward = gate_ref[...], up_ref[...]
     sigma = 1.0 / (1.0 + jnp.exp(-gate))
     dgate_ref[...] = (back_hidden * upward * sigma * (1.0 + gate * (1.0 - sigma))).astype(bf)
     dup_ref[...] = (back_hidden * gate * sigma).astype(bf)
     for k in range(n):
         lanes = slice(k * width, (k + 1) * width)
-        dx_ref[:, lanes] = (multiply(dgate_ref[...], first[k][0]) + multiply(dup_ref[...], first[k][1])).astype(bf)
+        dx_ref[:, lanes] = (multiply(dgate_ref[...], gates[k][0]) + multiply(dup_ref[...], ups[k][0])).astype(bf)
         out_ref[:, lanes] = multiply(hidden_ref[...], down[k][0]).astype(bf)
 
 
-def ffn_back(dm, gate, upward, hidden, pieces, down):
+def ffn_back(dm, gate, upward, hidden, pieces, n):
     tokens, units = gate.shape
     tile = lambda width: pl.BlockSpec((TOKENS, width), lambda i: (i, 0))
     return pl.pallas_call(
-        functools.partial(ffn_back_kernel, len(pieces)),
+        functools.partial(ffn_back_kernel, n),
         grid=(tokens // TOKENS,),
         out_shape=[
             jax.ShapeDtypeStruct((tokens, units), bf),
@@ -976,13 +1115,11 @@
             jax.ShapeDtypeStruct(dm.shape, bf),
             jax.ShapeDtypeStruct(dm.shape, bf),
         ],
-        in_specs=[tile(dm.shape[1]), tile(units), tile(units), tile(units)]
-        + piece_specs(pieces, 2)
-        + piece_specs(down, 1),
+        in_specs=[tile(dm.shape[1]), tile(units), tile(units), tile(units)] + piece_specs(pieces),
         out_specs=[tile(units), tile(units), tile(dm.shape[1]), tile(dm.shape[1])],
         compiler_params=pltpu.CompilerParams(vmem_limit_bytes=VMEM_LIMIT),
         name="ffn_back",
-    )(dm, gate, upward, hidden, *pieces, *down)
+    )(dm, gate, upward, hidden, *[array for array, _ in pieces])
 
 
 def shards(
@@ -1013,11 +1150,13 @@
     down_block = jnp.concatenate([down_slice, gains], axis=1)
     down_block = jnp.pad(down_block, ((0, 0), (0, -down_block.shape[1] % 128)))
     ffn_weights = HiddenGather(
-        jnp.stack([gate_weight.astype(bf).T, up_weight.astype(bf).T, down_weight.astype(bf)]), 1
-    )
-    (wide_down, wide_query_up, wide_latent_up), features, own_up = ring_gather(
-        (after(down_block, ffn_weights.away), query_up_low, latent_up_low), tokens, cotangent
-    )
+        jnp.stack([gate_weight.astype(bf).T, up_weight.astype(bf).T, down_weight.astype(bf)])
+    )
+    (wide_down, wide_query_up, wide_latent_up), features, own_up, came = ring_gather(
+        (down_block, query_up_low, latent_up_low), tokens, cotangent, ffn_weights.away
+    )
+    ffn_weights.arrived(came)
+    early = (ffn_weights.near_own(0, 1, wide_down), ffn_weights.far(0, wide_down))
     wide_output = lax.all_gather(after(output_weight, wide_down).astype(bf).T, "row", axis=0, tiled=True)
     gain_one = wide_down[:, slice_width].astype(f32)
     gain_two = wide_down[:, slice_width + 1].astype(f32)
@@ -1039,10 +1178,9 @@
     half = DR // 2
     key_front, key_back = rotate(latents[QR + KR : QR + KR + half], latents[QR + KR + half :], cosine, sine)
     key_part = jnp.concatenate([latent_in, key_front.astype(bf), key_back.astype(bf)], axis=0)
-    key_part = after(key_part, ffn_weights.came)
-    key_parts = jnp.concatenate([from_behind(key_part, step) for step in range(reach, 0, -1)] + [key_part], axis=1)
-    ffn_weights.near_own(key_parts)
-    far_first = ffn_weights.far(False, key_parts)
+    key_parts = gather_behind(after(key_part, early), reach)
+    beside = ffn_weights.near_own(1, 3, key_parts)
+    far_up, far_down = ffn_weights.far(1, key_parts), ffn_weights.far(2, key_parts)
     back_down = group_gather(features_by_group((RES * own_up).astype(bf)), key_parts)
     latent_all = key_parts[:KR]
     turned_t = jnp.concatenate([key_parts[KR : KR + half]] * 4 + [key_parts[KR + half :]] * 4, axis=0)
@@ -1066,24 +1204,26 @@
     up_keys, up_values = wide_latent_up[:, :wide], wide_latent_up[:, wide:]
     keys = over_rows(latent_all, up_keys).astype(bf)
     values_t = over_rows(up_values, latent_all).astype(bf)
-    out_t, lse = attend(first, query, keys, turned, values_t, bias, heads)
-
-    out_t = after(out_t, ffn_weights.beside)
+    out_t, out_wide, lse = attend(first, query, keys, turned, values_t, bias, heads)
+
+    gate_pieces = ffn_weights.near(0, out_t)
+    out_t = after(out_t, beside)
     branch = after(dot(out_t, wide_output, ((0,), (1,))), back_down)
     middle = own_residual + RES * fold(branch, COLS, 4, 4)
-    middle = after(middle, [piece for k, piece in far_first.items() if k])
-    far_down = ffn_weights.far(True, middle)
-    first_pieces = ffn_weights.near(far_first, False, middle)
+    middle = after(middle, far_up)
+    up_pieces = ffn_weights.near(1, middle)
+    middle = after(middle, far_down)
+    down_pieces = ffn_weights.near(2, middle)
     inverse_second = inverse_of(middle, 1)
     second_in = features_by_group((middle * inverse_second * gain_two).astype(bf))
     second_in = spread(second_in, GROUP, 4, 5, relative=True)
 
-    gate, upward, hidden = ffn(second_in, first_pieces)
-    down_pieces = ffn_weights.near(far_down, True, second_in)
+    gate, upward, hidden = ffn(second_in, gate_pieces, up_pieces)
     slope_down = HiddenScatter(hidden, back_down)
     slope_down.near(hidden)
+    gate = after(gate, slope_down.away)
     back_gate, back_upward, back_second, out_part = ffn_back(
-        back_down, gate, upward, hidden, first_pieces, down_pieces
+        back_down, gate, upward, hidden, gate_pieces + up_pieces + down_pieces, len(gate_pieces)
     )
     slope_gate = HiddenScatter(back_gate, second_in)
     slope_gate.near(back_gate)
@@ -1101,17 +1241,13 @@
 
     out = out_t.T
     back_out = multiply(back_branch, wide_output).astype(bf)
-    slope_output = lax.psum_scatter(
-        over_rows(back_branch, out).astype(bf), "row", scatter_dimension=0, tiled=True
-    )
     slope_gate.far(back_out)
     keys_t = over_rows(up_keys, latent_all).astype(bf)
     values = over_rows(latent_all, up_values).astype(bf)
     back_query_n, back_query_r, back_keys, back_values, back_turned = attend_back(
-        first, query, query.T, keys, turned, keys_t, turned_t, values, back_out.T, back_out, bias, lse, heads
-    )
-    back_query_n = after(back_query_n, (slope_down.came, slope_up.came, own_result.came))
-    slope_up.far(back_query_n)
+        first, query, query.T, keys, turned, keys_t, turned_t, values, back_out.T, back_out, out_wide, bias, lse, heads
+    )
+    back_query_n = after(back_query_n, (slope_down.came, own_result.came))
     own_result.partner(back_query_n)
     tiles = back_query_r.reshape(-1, 2, 64, count)
     back_turn = jnp.stack(rotate(tiles[:, 0], tiles[:, 1], cos_tile, -sin_tile), axis=1).reshape(-1, count)
@@ -1123,12 +1259,13 @@
     to_send = jnp.concatenate(
         [query_part] + [far[:, b * count : (b + 1) * count] for b in range(blocks)], axis=0
     )
-    to_send = after(to_send, (slope_gate.came, own_result.came))
+    to_send = after(to_send, slope_up.came)
+    slope_up.far(to_send)
     slope_down, away = slope_down.halves()
     summed, came = fold(to_send, COLS, 3, 8, lanes=True, cargo=away)
     slope_down = in_pair_order(slope_down, came, 0)
-    own_result = after(middle + RES * features_in_order(own_result.result()), summed)
-    result = jnp.concatenate(col_exchange(quarters(own_result, 1)), axis=0)
+    slope_gate.came = after(slope_gate.came, summed)
+    own_result = middle + RES * features_in_order(own_result.result())
     back_query_in = summed[:QR]
     wide_far = KR + DR
     parts = [summed[QR + b * wide_far : QR + (b + 1) * wide_far] for b in range(blocks)]
@@ -1149,11 +1286,9 @@
     back_latents = jnp.concatenate([back_query_latent, back_latent, back_front, back_behind], axis=0).astype(bf)
     back_latents = spread(back_latents, COLS, 3, 9, lanes=True)
     back_slice = lax.dynamic_slice_in_dim(back_latents, column * slice_width, slice_width, 0)
-    slope_gate, away = after(slope_gate.halves(), (result, slope_up.came))
-    back_first, came = fold(dot(back_slice, wide_down, ((0,), (1,))), COLS, 4, 10, cargo=away)
-    slope_gate = in_pair_order(slope_gate, came, 0)
+    back_first = fold(dot(back_slice, wide_down, ((0,), (1,))), COLS, 4, 10)
     back_norm_first, gain_first_part = norm_back(own_residual, inverse_of(own_residual, 1), gain_one, back_first, 1)
-    back_tokens = jnp.concatenate(col_exchange(quarters(back_middle + back_norm_first, 1)), axis=0)
+    own_back = back_middle + back_norm_first
 
     packed = jnp.concatenate(
         [part.reshape(rows, -1) for part in (gain_first_part, gain_second_part, query_gain_part, latent_gain_part)],
@@ -1161,15 +1296,18 @@
     )
     packed = jnp.pad(packed, ((0, 0), (0, -packed.shape[1] % 256))).reshape(-1, 128)
     back_slice_n = jnp.pad(back_slice.T, ((0, 0), (0, -slice_width % 128)))
-    slope_query_up, slope_latent_up, slope_down_slice, packed = ring_scatter(
+    slope_up.came = after(slope_up.came, back_first)
+    halves = [flow.halves() for flow in (slope_gate, slope_up)]
+    away = jnp.stack([gone for _, gone in halves])
+    (slope_output, slope_query_up, slope_latent_up, slope_down_slice, packed), came, (result, back_tokens) = ring_scatter((
+        over_rows(back_branch, out).astype(bf),
         against(query_in, back_raw).astype(bf),
         multiply(latent_all, jnp.concatenate([back_keys, back_values], axis=1)).astype(bf),
         over_rows(first_in, back_slice_n).astype(bf),
         packed,
-    )
-    slope_up, away = slope_up.halves()
-    slope_both, came = spread(slope_down_slice.astype(bf), COLS, 2, 11, lanes=True, cargo=away)
-    slope_up = in_pair_order(slope_up, came, 0)
+    ), away, (own_result, own_back))
+    slope_gate, slope_up = (in_pair_order(mine, got, 0) for (mine, _), got in zip(halves, came))
+    slope_both = spread(slope_down_slice.astype(bf), COLS, 2, 11, lanes=True)
     slope_both = jnp.concatenate([piece[:, :slice_width] for piece in quarters(slope_both, 1)], axis=1).astype(f32)
     packed = packed.reshape(-1)
     bit = 1
@@ -1196,7 +1334,7 @@
         packed[2 * n + m : 2 * n + m + k],
         exact(slope_query_up, query_one.astype(f32)),
         exact(slope_latent_up, latent_one.astype(f32)),
-        slope_output.T.astype(f32),
+        slope_output.T,
         packed[n : 2 * n],
         slope_gate.T.astype(f32),
         slope_up.T.astype(f32),

time: 983 us -> 952 us (0.968); the launches traced: 967 us -> 950 us
  Pallas kernels: 414 us -> 474 us
  starting transfers between devices: 105 us -> 63 us
  waiting for transfers between devices: 136 us -> 108 us
  local copies, waits for them, and re-layouts: 109 us -> 97.4 us
    pallas_call x3 -> x4, Pallas kernels: 101 us -> 183 us  [the longest x1 105 us: ring_scatter(): pl.pallas_call(functools.partial(ring_scatter_kernel, rows, n, extra), ou...]
    ppermute x14 -> x16, waiting for transfers between devices: 119 us -> 83.6 us  [swap_row(): lax.ppermute(value, 'row', [(r, r ^ mask) for r in range(lax.axis_size('r...]
    pallas_call x1, Pallas kernels: 64.1 us -> 98 us  [ring_gather(): pl.pallas_call(functools.partial(ring_gather_kernel, rows, n), out_shape=...]
    pallas_call x4, Pallas kernels: 101 us -> 69.1 us  [spread(): pl.pallas_call(functools.partial(spread_kernel, dims, parts, lanes, relat...]
    pallas_call x4, Pallas kernels: 117 us -> 94.4 us  [fold(): pl.pallas_call(functools.partial(fold_kernel, dims, parts, lanes, relativ...]
    ppermute x14 -> x16, starting transfers between devices: 76.2 us -> 53.9 us  [swap_row(): lax.ppermute(value, 'row', [(r, r ^ mask) for r in range(lax.axis_size('r...]
    ppermute x8 -> x4, starting transfers between devices: 20.9 us -> 5.17 us  [from_behind(): lax.ppermute(value, 'row', [(source, source + steps) for source in range(...]
    ppermute x8 -> x4, waiting for transfers between devices: 16.6 us -> 24 us  [from_behind(): lax.ppermute(value, 'row', [(source, source + steps) for source in range(...]
  transfers between devices with their start and end apart: 40 -> 31, of which waited for: 10 -> 7; matrix products, arithmetic and copies ran while one was open for 27% -> 25% of each run, Pallas kernels for 36% -> 24%
where the time goes in v4:
time: 952 us; the launch traced here: 950 us
  Pallas kernels  474 us (50%)
  waiting for transfers between devices  108 us (11%)
  other arithmetic  99.5 us (10%)
  local copies, waits for them, and re-layouts  97.4 us (10%)
  matrix products  91.9 us (10%)
  starting transfers between devices  63 us (7%)
  between operations  16.9 us (2%)
    pallas_call x1, Pallas kernels, ring_scatter(): pl.pallas_call(functools.partial(ring_scatter_kernel, rows, n, extra), ou...  105 us
    pallas_call x1, Pallas kernels, ring_gather(): pl.pallas_call(functools.partial(ring_gather_kernel, rows, n), out_shape=...  98 us
    pallas_call x4, Pallas kernels, fold(): pl.pallas_call(functools.partial(fold_kernel, dims, parts, lanes, relativ...  94.4 us
    dot_general x24, matrix products, dot(): lax.dot_general(left, right, (dims, ((), ())), preferred_element_type=f32)  85.2 us
    ppermute x16, waiting for transfers between devices, swap_row(): lax.ppermute(value, 'row', [(r, r ^ mask) for r in range(lax.axis_size('r...  83.6 us
    pallas_call x4, Pallas kernels, spread(): pl.pallas_call(functools.partial(spread_kernel, dims, parts, lanes, relat...  69.1 us
    ppermute x16, starting transfers between devices, swap_row(): lax.ppermute(value, 'row', [(r, r ^ mask) for r in range(lax.axis_size('r...  53.9 us
    unnamed x235, local copies, waits for them, and re-layouts  42.5 us
  transfers between devices with their start and end apart: 31, of which 7 were waited for; matrix products, arithmetic and copies ran while one was open for 25% of the time, Pallas kernels for 24%

profile of v4, /device:TPU:0, one launch (start us, length us, event | category | flops | bytes accessed | tf_op | source)
XLA Modules:
  0.0 949.9 jit_solution(1589462937399084286)
XLA Ops:
  27.3 98.0 %ring_gather.1 = (bf16[8,2,160,384]{3,2,1,0:T(8,128)(2,1)}, bf16[8,2,48,1024]{3,2,1,0:T(8,128)(2,1)}, bf16[8,2,16,1280]{3,2,1,0:T(8,128)(2,1)}, bf16[512,2560]{1...) custom-call(bf16[2,160,384]{2,1,0:T(8,128)(2,1)} %bitcast.122, bf16[2,48,1024]{2,1,0:T(8,128)(2,1)} %bitcast.129, ...), custom_call_target="tpu_custom_call" | custom-call | tf_op jit(solution)/shard_map/ring_gather/pallas_call | solution.py:151
  168.8 30.5 %collective-permute-done.6 = bf16[128,2560]{1,0:T(8,128)(2,1)} collective-permute-done((bf16[128,2560]{1,0:T(8,128)(2,1)}, bf16[128,2560]{1,0:T(8,128)(2,1)}, u32[]{:S(2)}, u32[]{:S(2)}) %collective-permute-start.6) | collective-permute-done | bytes 655392 | tf_op jit(solution)/shard_map/ppermute | solution.py:349
  207.9 24.6 %gather_behind.1 = bf16[288,2560]{1,0:T(8,128)(2,1)} custom-call(bf16[288,512]{1,0:T(8,128)(2,1)} %pad_maximum_fusion.25.key_ref), custom_call_target="tpu_custom_call" | custom-call | tf_op jit(solution)/shard_map/gather_behind/pallas_call | solution.py:690
  274.3 10.5 %attend.1 = (bf16[640,512]{1,0:T(8,128)(2,1)}, f32[640,512]{1,0:T(8,128)}, f32[5,2,512]{2,1,0:T(2,128)}) custom-call(s32[1]{0:T(128)} %bitcast.11.first_ref, bf16[1024,512]{1,0:T(8,128)(2,1)} %copy.85.qn_ref.qr_ref, bf16[1024,512]{1,0:T(8,128)(2,1)} %copy.85.qn_ref.qr_ref, bf16[2560,640]{1,0:T(8,128)(2,1)} %convolution_convert_fusion.4.k_ref, ...), custom_call_target="tpu_custom_call" | custom-call | tf_op jit(solution)/shard_map/attend/pallas_call | solution.py:925
  317.1 21.9 %fold4.1 = f32[128,2560]{1,0:T(8,128)} custom-call(bf16[4,128,2560]{2,1,0:T(8,128)(2,1)} %bitcast.111), custom_call_target="tpu_custom_call" | custom-call | tf_op jit(solution)/shard_map/fold4/pallas_call | solution.py:769
  342.1 20.5 %collective-permute-done.11.refs_10_ = bf16[1,800,640]{2,1,0:T(8,128)(2,1)} collective-permute-done((bf16[1,800,640]{2,1,0:T(8,128)(2,1)}, bf16[1,800,640]{2,1,0:T(8,128)(2,1)}, u32[]{:S(2)}, u32[]{:S(2)}) %collective-permute-start.11) | collective-permute-done | bytes 1024032 | tf_op jit(solution)/shard_map/ppermute | solution.py:349
  366.7 26.5 %spread5.1 = bf16[8,128,2560]{2,1,0:T(8,128)(2,1)} custom-call(bf16[128,2560]{1,0:T(8,128)(2,1)} %pad_maximum_fusion.20.refs_0_), custom_call_target="tpu_custom_call" | custom-call | tf_op jit(solution)/shard_map/spread5/pallas_call | solution.py:624
  397.7 10.6 %collective-permute-done.13.refs_7_ = bf16[1,800,640]{2,1,0:T(8,128)(2,1)} collective-permute-done((bf16[1,800,640]{2,1,0:T(8,128)(2,1)}, bf16[1,800,640]{2,1,0:T(8,128)(2,1)}, u32[]{:S(2)}, u32[]{:S(2)}) %collective-permute-start.13) | collective-permute-done | bytes 1024032 | tf_op jit(solution)/shard_map/ppermute | solution.py:349
  408.2 18.8 %ffn.1 = (f32[1024,800]{1,0:T(8,128)}, f32[1024,800]{1,0:T(8,128)}, bf16[1024,800]{1,0:T(8,128)(2,1)}) custom-call(bf16[1024,2560]{1,0:T(8,128)(2,1)} %bitcast.88, bf16[3,800,640]{2,1,0:T(8,128)(2,1)} %pad_maximum_fusion.refs_0_.refs_4_.refs_8_, bf16[1,800,640]{2,1,0:T(8,128)(2,1)} %collective-permute-done.3.refs_1_, ...), custom_call_target="tpu_custom_call" | custom-call | tf_op jit(solution)/shard_map/ffn/pallas_call | solution.py:1076
  432.6 34.0 %ffn_back.1 = (bf16[1024,800]{1,0:T(8,128)(2,1)}, bf16[1024,800]{1,0:T(8,128)(2,1)}, bf16[1024,2560]{1,0:T(8,128)(2,1)}, bf16[1024,2560]{1,0:T(8,128)(2,1)}) custom-call(bf16[1024,2560]{1,0:T(8,128)(2,1)} %slice_dynamic-update-slice_fusion.dm_ref, f32[1024,800]{1,0:T(8,128)} %get-tuple-element.96.gate_ref, f32[1024,800]{1,0:T(8,128)} %get-tuple-element.97.up_ref, ...), custom_call_target="tpu_custom_call" | custom-call | tf_op jit(solution)/shard_map/ffn_back/pallas_call | solution.py:1109
  474.5 31.2 %fold6.1 = f32[128,2560]{1,0:T(8,128)} custom-call(bf16[8,128,2560]{2,1,0:T(8,128)(2,1)} %bitcast.100), custom_call_target="tpu_custom_call" | custom-call | tf_op jit(solution)/shard_map/fold6/pallas_call | solution.py:769
  516.4 6.0 convolution_convert_fusion.7
  524.2 22.8 %spread7.1 = bf16[4,128,2560]{2,1,0:T(8,128)(2,1)} custom-call(bf16[128,2560]{1,0:T(8,128)(2,1)} %get-tuple-element.105.refs_0_), custom_call_target="tpu_custom_call" | custom-call | tf_op jit(solution)/shard_map/spread7/pallas_call | solution.py:624
  563.0 18.9 %attend_back.1 = (f32[640,512]{1,0:T(8,128)}, f32[384,512]{1,0:T(8,128)}, bf16[2560,640]{1,0:T(8,128)(2,1)}, bf16[2560,640]{1,0:T(8,128)(2,1)}, f32[2560,128]{1,0:T(8,128)}) custom-call(s32[1]{0:T(128)} %bitcast.11.first_ref, bf16[1024,512]{1,0:T(8,128)(2,1)} %copy.85.qn_ref.qr_ref, bf16[1024,512]{1,0:T(8,128)(2,1)} %copy.85.qn_ref.qr_ref, ...), custom_call_target="tpu_custom_call" | custom-call | tf_op jit(solution)/shard_map/attend_back/pallas_call | solution.py:1030
  594.6 9.8 %collective-permute-start.25 = (bf16[800,640]{1,0:T(8,128)(2,1)}, bf16[800,640]{1,0:T(8,128)(2,1)}, u32[]{:S(2)}, u32[]{:S(2)}) collective-permute-start(bf16[800,640]{1,0:T(8,128)(2,1)} %split.700), channel_id=1, source_target_pairs={{0,16},{4,20},{8,24},{12,28},{16,0},{20,4},{24,8},{28,12},{1,17},{... | collective-permute-start | bytes 3072008 | tf_op jit(solution)/shard_map/ppermute | solution.py:349
  623.0 9.8 %collective-permute-start.27 = (bf16[128,2560]{1,0:T(8,128)(2,1)S(1)}, bf16[128,2560]{1,0:T(8,128)(2,1)S(1)}, u32[]{:S(2)}, u32[]{:S(2)}) collective-permute-start(bf16[128,2560]{1,0:T(8,128)(2,1)S(1)} %add_convert_fusion), channel_id=1, source_target_pairs={{0,8},{4,12},{8,0},{12,4},{16,24},{20,28},{24,16},{28,20},{1,9},{5... | collective-permute-start | bytes 1966088 | tf_op jit(solution)/shard_map/ppermute | solution.py:349
  640.6 17.4 %collective-permute-done.27 = bf16[128,2560]{1,0:T(8,128)(2,1)S(1)} collective-permute-done((bf16[128,2560]{1,0:T(8,128)(2,1)S(1)}, bf16[128,2560]{1,0:T(8,128)(2,1)S(1)}, u32[]{:S(2)}, u32[]{:S(2)}) %collective-permute-start.27) | collective-permute-done | bytes 655392 | tf_op jit(solution)/shard_map/ppermute | solution.py:349
  665.0 19.7 %fold8.1 = (f32[2208,128]{1,0:T(8,128)}, bf16[800,320]{1,0:T(8,128)(2,1)}) custom-call(bf16[2208,512]{1,0:T(8,128)(2,1)} %fusion.60.refs_0_, bf16[800,320]{1,0:T(8,128)(2,1)} %broadcast_select_fusion.9.refs_1_), custom_call_target="tpu_custom_call" | custom-call | tf_op jit(solution)/shard_map/fold8/pallas_call | solution.py:769
  706.0 10.4 %collective-permute-start.26 = (bf16[800,640]{1,0:T(8,128)(2,1)}, bf16[800,640]{1,0:T(8,128)(2,1)}, u32[]{:S(2)}, u32[]{:S(2)}) collective-permute-start(bf16[800,640]{1,0:T(8,128)(2,1)} %split.699), channel_id=1, source_target_pairs={{0,16},{4,20},{8,24},{12,28},{16,0},{20,4},{24,8},{28,12},{1,17},{... | collective-permute-start | bytes 3072008 | tf_op jit(solution)/shard_map/ppermute | solution.py:349
  717.7 24.0 %collective-permute-done.23 = f32[288,128]{1,0:T(8,128)} collective-permute-done((f32[288,128]{1,0:T(8,128)S(1)}, f32[288,128]{1,0:T(8,128)}, u32[]{:S(2)}, u32[]{:S(2)}) %collective-permute-start.23) | collective-permute-done | bytes 147488 | tf_op jit(solution)/shard_map/ppermute | solution.py:299
  743.9 10.3 %spread9.1 = bf16[1056,512]{1,0:T(8,128)(2,1)} custom-call(bf16[1056,128]{1,0:T(8,128)(2,1)} %pad_maximum_fusion.26.refs_0_), custom_call_target="tpu_custom_call" | custom-call | tf_op jit(solution)/shard_map/spread9/pallas_call | solution.py:624
  759.9 21.7 %fold10.1 = f32[128,2560]{1,0:T(8,128)} custom-call(bf16[4,128,2560]{2,1,0:T(8,128)(2,1)} %bitcast.110), custom_call_target="tpu_custom_call" | custom-call | tf_op jit(solution)/shard_map/fold10/pallas_call | solution.py:769
  795.0 105.3 %ring_scatter.1 = (f32[2,160,640]{2,1,0:T(8,128)}, f32[2,48,1024]{2,1,0:T(8,128)}, f32[2,16,1280]{2,1,0:T(8,128)}, f32[2,160,384]{2,1,0:T(8,128)}, f32[2,3,128]{...) custom-call(bf16[8,2,160,640]{3,2,1,0:T(8,128)(2,1)} %bitcast.105, ...), custom_call_target="tpu_custom_call" | custom-call | tf_op jit(solution)/shard_map/ring_scatter/pallas_call | solution.py:277
  904.1 9.5 %spread11.1 = bf16[320,1536]{1,0:T(8,128)(2,1)} custom-call(bf16[320,384]{1,0:T(8,128)(2,1)} %bitcast.121), custom_call_target="tpu_custom_call" | custom-call | tf_op jit(solution)/shard_map/spread11/pallas_call | solution.py:624
  (484 shorter events, 320.4 us)
Async XLA Ops:
  7.2 304.2 %all-gather.2.cloned.1.call-start = ((), (), s32[]{:S(2)}) async-start(), calls=%async_computation | async-start | bytes 3686400 | tf_op jit(solution)/shard_map/all_gather | solution.py:1160
  131.4 76.5 %collective-permute-start.3 = (bf16[1,800,640]{2,1,0:T(8,128)(2,1)}, bf16[1,800,640]{2,1,0:T(8,128)(2,1)}, u32[]{:S(2)}, u32[]{:S(2)}) collective-permute-start(bf16[1,800,640]{2,1,0:T(8,128)(2,1)} %get-tuple-element.79), channel_id=1, source_target_pairs={{0,4},{4,0},{8,12},{12,8},{16,20},{20,16},{24,28},{28,24},{1,5},{5... | collective-permute-start | bytes 3072008 | tf_op jit(solution)/shard_map/ppermute | solution.py:349
  133.0 74.9 %collective-permute-start.4 = (bf16[1,800,640]{2,1,0:T(8,128)(2,1)}, bf16[1,800,640]{2,1,0:T(8,128)(2,1)}, u32[]{:S(2)}, u32[]{:S(2)}) collective-permute-start(bf16[1,800,640]{2,1,0:T(8,128)(2,1)} %get-tuple-element.79), channel_id=1, source_target_pairs={{0,16},{4,20},{8,24},{12,28},{16,0},{20,4},{24,8},{28,12},{1,17},{... | collective-permute-start | bytes 3072008 | tf_op jit(solution)/shard_map/ppermute | solution.py:349
  144.4 57.2 %collective-permute-start.2 = (f32[264,512]{1,0:T(8,128)}, f32[264,512]{1,0:T(8,128)}, u32[]{:S(2)}, u32[]{:S(2)}) collective-permute-start(f32[264,512]{1,0:T(8,128)} %fusion.33), channel_id=1, source_target_pairs={{0,1},{1,0},{2,3},{3,2},{4,5},{5,4},{6,7},{7,6},{8,9},{9,8},{10,11... | collective-permute-start | bytes 1622024 | tf_op jit(solution)/shard_map/ppermute | solution.py:303
  147.2 52.2 %collective-permute-start.6 = (bf16[128,2560]{1,0:T(8,128)(2,1)}, bf16[128,2560]{1,0:T(8,128)(2,1)}, u32[]{:S(2)}, u32[]{:S(2)}) collective-permute-start(bf16[128,2560]{1,0:T(8,128)(2,1)} %pad_maximum_fusion.19), channel_id=1, source_target_pairs={{0,8},{4,12},{8,0},{12,4},{16,24},{20,28},{24,16},{28,20},{1,9},{5... | collective-permute-start | bytes 1966088 | tf_op jit(solution)/shard_map/ppermute | solution.py:349
  165.2 36.4 %collective-permute-start.1 = (f32[264,512]{1,0:T(8,128)}, f32[264,512]{1,0:T(8,128)S(1)}, u32[]{:S(2)}, u32[]{:S(2)}) collective-permute-start(f32[264,512]{1,0:T(8,128)} %collective-permute-done), channel_id=1, source_target_pairs={{0,1},{1,0},{2,3},{3,2},{4,5},{5,4},{6,7},{7,6},{8,9},{9,8},{10,11... | collective-permute-start | bytes 1622024 | tf_op jit(solution)/shard_map/ppermute | solution.py:303
  243.1 44.5 %collective-permute-start.7 = (bf16[256,2560]{1,0:T(8,128)(2,1)}, bf16[256,2560]{1,0:T(8,128)(2,1)}, u32[]{:S(2)}, u32[]{:S(2)}) collective-permute-start(bf16[256,2560]{1,0:T(8,128)(2,1)} %pad_maximum_fusion.12), channel_id=1, source_target_pairs={{0,1},{1,0},{2,3},{3,2},{4,5},{5,4},{6,7},{7,6},{8,9},{9,8},{10,11... | collective-permute-start | bytes 3932168 | tf_op jit(solution)/shard_map/ppermute | solution.py:303
  243.4 48.0 %collective-permute-start.8 = (bf16[256,2560]{1,0:T(8,128)(2,1)}, bf16[256,2560]{1,0:T(8,128)(2,1)}, u32[]{:S(2)}, u32[]{:S(2)}) collective-permute-start(bf16[256,2560]{1,0:T(8,128)(2,1)} %pad_maximum_fusion.12), channel_id=1, source_target_pairs={{0,2},{1,3},{2,0},{3,1},{4,6},{5,7},{6,4},{7,5},{8,10},{9,11},{10,... | collective-permute-start | bytes 3932168 | tf_op jit(solution)/shard_map/ppermute | solution.py:303
  247.4 51.2 %collective-permute-start.5 = (bf16[2,800,640]{2,1,0:T(8,128)(2,1)}, bf16[2,800,640]{2,1,0:T(8,128)(2,1)S(1)}, u32[]{:S(2)}, u32[]{:S(2)}) collective-permute-start(bf16[2,800,640]{2,1,0:T(8,128)(2,1)} %fusion.23), channel_id=1, source_target_pairs={{0,4},{4,0},{8,12},{12,8},{16,20},{20,16},{24,28},{28,24},{1,5},{5... | collective-permute-start | bytes 6144008 | tf_op jit(solution)/shard_map/ppermute | solution.py:349
  271.4 70.7 %collective-permute-start.10 = (bf16[1,800,640]{2,1,0:T(8,128)(2,1)}, bf16[1,800,640]{2,1,0:T(8,128)(2,1)}, u32[]{:S(2)}, u32[]{:S(2)}) collective-permute-start(bf16[1,800,640]{2,1,0:T(8,128)(2,1)} %get-tuple-element.88), channel_id=1, source_target_pairs={{0,16},{4,20},{8,24},{12,28},{16,0},{20,4},{24,8},{28,12},{1,17},{... | collective-permute-start | bytes 3072008 | tf_op jit(solution)/shard_map/ppermute | solution.py:349
  271.4 91.2 %collective-permute-start.11 = (bf16[1,800,640]{2,1,0:T(8,128)(2,1)}, bf16[1,800,640]{2,1,0:T(8,128)(2,1)}, u32[]{:S(2)}, u32[]{:S(2)}) collective-permute-start(bf16[1,800,640]{2,1,0:T(8,128)(2,1)} %get-tuple-element.90), channel_id=1, source_target_pairs={{0,16},{4,20},{8,24},{12,28},{16,0},{20,4},{24,8},{28,12},{1,17},{... | collective-permute-start | bytes 3072008 | tf_op jit(solution)/shard_map/ppermute | solution.py:349
  287.6 110.1 %collective-permute-start.12 = (bf16[1,800,640]{2,1,0:T(8,128)(2,1)}, bf16[1,800,640]{2,1,0:T(8,128)(2,1)}, u32[]{:S(2)}, u32[]{:S(2)}) collective-permute-start(bf16[1,800,640]{2,1,0:T(8,128)(2,1)} %collective-permute-done.4.refs_2_), channel_id=1, source_target_pairs={{0,4},{4,0},{8,12},{12,8},{16,20},{20,16},{24,28},{28,24},{1,5},{5... | collective-permute-start | bytes 3072008 | tf_op jit(solution)/shard_map/ppermute | solution.py:349
  362.7 69.9 %collective-permute-start.14 = (bf16[1,800,640]{2,1,0:T(8,128)(2,1)}, bf16[1,800,640]{2,1,0:T(8,128)(2,1)}, u32[]{:S(2)}, u32[]{:S(2)}) collective-permute-start(bf16[1,800,640]{2,1,0:T(8,128)(2,1)} %collective-permute-done.11.refs_10_), channel_id=1, source_target_pairs={{0,4},{4,0},{8,12},{12,8},{16,20},{20,16},{24,28},{28,24},{1,5},{5... | collective-permute-start | bytes 3072008 | tf_op jit(solution)/shard_map/ppermute | solution.py:349
  363.1 45.2 %collective-permute-start.13 = (bf16[1,800,640]{2,1,0:T(8,128)(2,1)}, bf16[1,800,640]{2,1,0:T(8,128)(2,1)}, u32[]{:S(2)}, u32[]{:S(2)}) collective-permute-start(bf16[1,800,640]{2,1,0:T(8,128)(2,1)} %collective-permute-done.10.refs_6_), channel_id=1, source_target_pairs={{0,4},{4,0},{8,12},{12,8},{16,20},{20,16},{24,28},{28,24},{1,5},{5... | collective-permute-start | bytes 3072008 | tf_op jit(solution)/shard_map/ppermute | solution.py:349
  470.1 54.1 %collective-permute-start.16 = (bf16[512,2560]{1,0:T(8,128)(2,1)}, bf16[512,2560]{1,0:T(8,128)(2,1)}, u32[]{:S(2)}, u32[]{:S(2)}) collective-permute-start(bf16[512,2560]{1,0:T(8,128)(2,1)} %pad_maximum_fusion.3), channel_id=1, source_target_pairs={{0,1},{1,0},{2,3},{3,2},{4,5},{5,4},{6,7},{7,6},{8,9},{9,8},{10,11... | collective-permute-start | bytes 7864328 | tf_op jit(solution)/shard_map/ppermute | solution.py:303
  470.1 54.1 %collective-permute-start.15 = (bf16[800,1280]{1,0:T(8,128)(2,1)}, bf16[800,1280]{1,0:T(8,128)(2,1)}, u32[]{:S(2)}, u32[]{:S(2)}) collective-permute-start(bf16[800,1280]{1,0:T(8,128)(2,1)} %convolution_convert_fusion.9), channel_id=1, source_target_pairs={{0,4},{4,0},{8,12},{12,8},{16,20},{20,16},{24,28},{28,24},{1,5},{5... | collective-permute-start | bytes 6144008 | tf_op jit(solution)/shard_map/ppermute | solution.py:349
  508.0 81.3 %collective-permute-start.24 = (bf16[800,1280]{1,0:T(8,128)(2,1)}, bf16[800,1280]{1,0:T(8,128)(2,1)}, u32[]{:S(2)}, u32[]{:S(2)}) collective-permute-start(bf16[800,1280]{1,0:T(8,128)(2,1)} %convolution_convert_fusion.8), channel_id=1, source_target_pairs={{0,4},{4,0},{8,12},{12,8},{16,20},{20,16},{24,28},{28,24},{1,5},{5... | collective-permute-start | bytes 6144008 | tf_op jit(solution)/shard_map/ppermute | solution.py:349
  553.3 65.0 %collective-permute-start.17 = (bf16[800,640]{1,0:T(8,128)(2,1)}, bf16[800,640]{1,0:T(8,128)(2,1)}, u32[]{:S(2)}, u32[]{:S(2)}) collective-permute-start(bf16[800,640]{1,0:T(8,128)(2,1)} %split.701), channel_id=1, source_target_pairs={{0,16},{4,20},{8,24},{12,28},{16,0},{20,4},{24,8},{28,12},{1,17},{... | collective-permute-start | bytes 3072008 | tf_op jit(solution)/shard_map/ppermute | solution.py:349
  554.9 110.2 %collective-permute-start.19 = (bf16[800,1280]{1,0:T(8,128)(2,1)}, bf16[800,1280]{1,0:T(8,128)(2,1)}, u32[]{:S(2)}, u32[]{:S(2)}) collective-permute-start(bf16[800,1280]{1,0:T(8,128)(2,1)} %convolution_convert_fusion.7), channel_id=1, source_target_pairs={{0,4},{4,0},{8,12},{12,8},{16,20},{20,16},{24,28},{28,24},{1,5},{5... | collective-permute-start | bytes 6144008 | tf_op jit(solution)/shard_map/ppermute | solution.py:349
  562.2 58.9 %collective-permute-start.18 = (bf16[256,2560]{1,0:T(8,128)(2,1)}, bf16[256,2560]{1,0:T(8,128)(2,1)}, u32[]{:S(2)}, u32[]{:S(2)}) collective-permute-start(bf16[256,2560]{1,0:T(8,128)(2,1)} %pad_maximum_fusion.13), channel_id=1, source_target_pairs={{0,2},{1,3},{2,0},{3,1},{4,6},{5,7},{6,4},{7,5},{8,10},{9,11},{10,... | collective-permute-start | bytes 3932168 | tf_op jit(solution)/shard_map/ppermute | solution.py:303
  594.6 101.7 %collective-permute-start.25 = (bf16[800,640]{1,0:T(8,128)(2,1)}, bf16[800,640]{1,0:T(8,128)(2,1)}, u32[]{:S(2)}, u32[]{:S(2)}) collective-permute-start(bf16[800,640]{1,0:T(8,128)(2,1)} %split.700), channel_id=1, source_target_pairs={{0,16},{4,20},{8,24},{12,28},{16,0},{20,4},{24,8},{28,12},{1,17},{... | collective-permute-start | bytes 3072008 | tf_op jit(solution)/shard_map/ppermute | solution.py:349
  623.0 35.0 %collective-permute-start.27 = (bf16[128,2560]{1,0:T(8,128)(2,1)S(1)}, bf16[128,2560]{1,0:T(8,128)(2,1)S(1)}, u32[]{:S(2)}, u32[]{:S(2)}) collective-permute-start(bf16[128,2560]{1,0:T(8,128)(2,1)S(1)} %add_convert_fusion), channel_id=1, source_target_pairs={{0,8},{4,12},{8,0},{12,4},{16,24},{20,28},{24,16},{28,20},{1,9},{5... | collective-permute-start | bytes 1966088 | tf_op jit(solution)/shard_map/ppermute | solution.py:349
  693.4 48.3 %collective-permute-start.23 = (f32[288,128]{1,0:T(8,128)S(1)}, f32[288,128]{1,0:T(8,128)}, u32[]{:S(2)}, u32[]{:S(2)}) collective-permute-start(f32[288,128]{1,0:T(8,128)S(1)} %get-tuple-element.234), channel_id=1, source_target_pairs={{16,0},{20,4},{24,8},{28,12},{17,1},{21,5},{25,9},{29,13},{18,2},{... | collective-permute-start | bytes 442376 | tf_op jit(solution)/shard_map/ppermute | solution.py:299
  706.0 84.6 %collective-permute-start.26 = (bf16[800,640]{1,0:T(8,128)(2,1)}, bf16[800,640]{1,0:T(8,128)(2,1)}, u32[]{:S(2)}, u32[]{:S(2)}) collective-permute-start(bf16[800,640]{1,0:T(8,128)(2,1)} %split.699), channel_id=1, source_target_pairs={{0,16},{4,20},{8,24},{12,28},{16,0},{20,4},{24,8},{28,12},{1,17},{... | collective-permute-start | bytes 3072008 | tf_op jit(solution)/shard_map/ppermute | solution.py:349
  (112 other events, 1381.2 us)
Sparse Core Ops, SparseCore 0:
  145.4 91.2 all-gather.1

commit v5 on v4

--- a/solution.py
+++ b/solution.py
@@ -377,13 +377,6 @@
     return jnp.concatenate(chunks, axis=1)
 
 
-def group_gather(own, mark):
-    both = after(jnp.concatenate([own, swap_row(own, PAIR)], axis=0), mark)
-    across = swap_col(both, 2)
-    pieces = [both, swap_col(both, 1), across, swap_col(across, 1)]
-    return jnp.concatenate([p for half in zip(*(jnp.split(piece, 2, axis=0) for piece in pieces)) for p in half], axis=0)
-
-
 class GroupScatter:
     def __init__(self, value):
         x = jnp.split(value, 2 * lax.axis_size("col"), axis=0)
@@ -424,19 +417,21 @@
         self.mine, self.away = pair_halves(blocks, 1)
         self.pieces = [{} for _ in range(blocks.shape[0])]
 
-    def arrived(self, came):
-        self.own = in_pair_order(self.mine, came, 2)
-        for which, pieces in enumerate(self.pieces):
-            pieces[0] = (self.own, which)
-
-    def near_own(self, first, last, mark):
-        beside = swap_row(after(self.own[first:last], mark), group_masks()[-1][1])
+    def arrived(self, came, first, last):
+        own = in_pair_order(self.mine[first:last], came, 2)
+        for which in range(first, last):
+            self.pieces[which][0] = (own, which - first)
+        return own
+
+    def near_own(self, own, first, last, mark):
+        beside = swap_row(after(own, mark), group_masks()[-1][1])
         for which in range(first, last):
             self.pieces[which][1] = (beside, which - first)
         return beside
 
     def far(self, which, mark):
-        moved = {0: after(self.own[which : which + 1], mark)}
+        own, index = self.pieces[which][0]
+        moved = {0: after(own[index : index + 1], mark)}
         for bit, mask in group_masks()[:-1]:
             for k in list(moved):
                 moved[k ^ bit] = swap_row(moved[k], mask)
@@ -1153,11 +1148,13 @@
         jnp.stack([gate_weight.astype(bf).T, up_weight.astype(bf).T, down_weight.astype(bf)])
     )
     (wide_down, wide_query_up, wide_latent_up), features, own_up, came = ring_gather(
-        (down_block, query_up_low, latent_up_low), tokens, cotangent, ffn_weights.away
-    )
-    ffn_weights.arrived(came)
-    early = (ffn_weights.near_own(0, 1, wide_down), ffn_weights.far(0, wide_down))
-    wide_output = lax.all_gather(after(output_weight, wide_down).astype(bf).T, "row", axis=0, tiled=True)
+        (down_block, query_up_low, latent_up_low), tokens, cotangent, ffn_weights.away[:1]
+    )
+    first_own = ffn_weights.arrived(came, 0, 1)
+    back_down = spread(features_by_group((RES * own_up).astype(bf)), GROUP, 4, 12, relative=True)
+    others = swap_row(after(ffn_weights.away[1:], back_down), PAIR)
+    early = (ffn_weights.near_own(first_own, 0, 1, back_down), ffn_weights.far(0, back_down), others)
+    wide_output = lax.all_gather(after(output_weight, back_down).astype(bf).T, "row", axis=0, tiled=True)
     gain_one = wide_down[:, slice_width].astype(f32)
     gain_two = wide_down[:, slice_width + 1].astype(f32)
     small_gains = wide_down[:, slice_width + 2].reshape(rows, -1).astype(f32)
@@ -1179,9 +1176,9 @@
     key_front, key_back = rotate(latents[QR + KR : QR + KR + half], latents[QR + KR + half :], cosine, sine)
     key_part = jnp.concatenate([latent_in, key_front.astype(bf), key_back.astype(bf)], axis=0)
     key_parts = gather_behind(after(key_part, early), reach)
-    beside = ffn_weights.near_own(1, 3, key_parts)
+    other_own = ffn_weights.arrived(others, 1, 3)
+    beside = ffn_weights.near_own(other_own, 1, 3, key_parts)
     far_up, far_down = ffn_weights.far(1, key_parts), ffn_weights.far(2, key_parts)
-    back_down = group_gather(features_by_group((RES * own_up).astype(bf)), key_parts)
     latent_all = key_parts[:KR]
     turned_t = jnp.concatenate([key_parts[KR : KR + half]] * 4 + [key_parts[KR + half :]] * 4, axis=0)
     turned = turned_t.T
@@ -1208,15 +1205,15 @@
 
     gate_pieces = ffn_weights.near(0, out_t)
     out_t = after(out_t, beside)
-    branch = after(dot(out_t, wide_output, ((0,), (1,))), back_down)
-    middle = own_residual + RES * fold(branch, COLS, 4, 4)
+    branch = dot(out_t, wide_output, ((0,), (1,)))
+    middle = own_residual + RES * fold(branch, COLS, 8, 4)
     middle = after(middle, far_up)
     up_pieces = ffn_weights.near(1, middle)
     middle = after(middle, far_down)
     down_pieces = ffn_weights.near(2, middle)
     inverse_second = inverse_of(middle, 1)
     second_in = features_by_group((middle * inverse_second * gain_two).astype(bf))
-    second_in = spread(second_in, GROUP, 4, 5, relative=True)
+    second_in = spread(second_in, GROUP, 8, 5, relative=True)
 
     gate, upward, hidden = ffn(second_in, gate_pieces, up_pieces)
     slope_down = HiddenScatter(hidden, back_down)
@@ -1228,7 +1225,7 @@
     slope_gate = HiddenScatter(back_gate, second_in)
     slope_gate.near(back_gate)
     back_second = after(back_second, slope_gate.away)
-    back_second = features_in_order(fold(back_second, GROUP, 4, 6, relative=True))
+    back_second = features_in_order(fold(back_second, GROUP, 8, 6, relative=True))
     slope_up = HiddenScatter(back_upward, second_in)
     own_result = GroupScatter(out_part)
     back_norm, gain_second_part = norm_back(middle, inverse_second, gain_two, back_second, 1)
@@ -1236,7 +1233,7 @@
     back_branch = after((RES * back_middle).astype(bf), (slope_down.came, own_result.came, slope_up.away))
     slope_up.near(back_branch)
     slope_down.far(back_branch)
-    back_branch = spread(back_branch, COLS, 4, 7)
+    back_branch = spread(back_branch, COLS, 8, 7)
     own_result.across(back_branch)
 
     out = out_t.T
@@ -1247,7 +1244,8 @@
     back_query_n, back_query_r, back_keys, back_values, back_turned = attend_back(
         first, query, query.T, keys, turned, keys_t, turned_t, values, back_out.T, back_out, out_wide, bias, lse, heads
     )
-    back_query_n = after(back_query_n, (slope_down.came, own_result.came))
+    back_query_n = after(back_query_n, (slope_down.came, slope_gate.came, slope_up.came, own_result.came))
+    slope_up.far(back_query_n)
     own_result.partner(back_query_n)
     tiles = back_query_r.reshape(-1, 2, 64, count)
     back_turn = jnp.stack(rotate(tiles[:, 0], tiles[:, 1], cos_tile, -sin_tile), axis=1).reshape(-1, count)
@@ -1259,12 +1257,8 @@
     to_send = jnp.concatenate(
         [query_part] + [far[:, b * count : (b + 1) * count] for b in range(blocks)], axis=0
     )
-    to_send = after(to_send, slope_up.came)
-    slope_up.far(to_send)
-    slope_down, away = slope_down.halves()
-    summed, came = fold(to_send, COLS, 3, 8, lanes=True, cargo=away)
-    slope_down = in_pair_order(slope_down, came, 0)
-    slope_gate.came = after(slope_gate.came, summed)
+    summed = after(fold(to_send, COLS, 3, 8, lanes=True), slope_up.came)
+    slope_down.came, slope_gate.came = after((slope_down.came, slope_gate.came), summed)
     own_result = middle + RES * features_in_order(own_result.result())
     back_query_in = summed[:QR]
     wide_far = KR + DR
@@ -1286,7 +1280,10 @@
     back_latents = jnp.concatenate([back_query_latent, back_latent, back_front, back_behind], axis=0).astype(bf)
     back_latents = spread(back_latents, COLS, 3, 9, lanes=True)
     back_slice = lax.dynamic_slice_in_dim(back_latents, column * slice_width, slice_width, 0)
-    back_first = fold(dot(back_slice, wide_down, ((0,), (1,))), COLS, 4, 10)
+    halves = [flow.halves() for flow in (slope_down, slope_gate)]
+    away = jnp.stack([gone for _, gone in halves])
+    back_first, came = fold(dot(back_slice, wide_down, ((0,), (1,))), COLS, 8, 10, cargo=away)
+    slope_down, slope_gate = (in_pair_order(mine, got, 0) for (mine, _), got in zip(halves, came))
     back_norm_first, gain_first_part = norm_back(own_residual, inverse_of(own_residual, 1), gain_one, back_first, 1)
     own_back = back_middle + back_norm_first
 
@@ -1297,8 +1294,7 @@
     packed = jnp.pad(packed, ((0, 0), (0, -packed.shape[1] % 256))).reshape(-1, 128)
     back_slice_n = jnp.pad(back_slice.T, ((0, 0), (0, -slice_width % 128)))
     slope_up.came = after(slope_up.came, back_first)
-    halves = [flow.halves() for flow in (slope_gate, slope_up)]
-    away = jnp.stack([gone for _, gone in halves])
+    slope_up, away = slope_up.halves()
     (slope_output, slope_query_up, slope_latent_up, slope_down_slice, packed), came, (result, back_tokens) = ring_scatter((
         over_rows(back_branch, out).astype(bf),
         against(query_in, back_raw).astype(bf),
@@ -1306,17 +1302,15 @@
         over_rows(first_in, back_slice_n).astype(bf),
         packed,
     ), away, (own_result, own_back))
-    slope_gate, slope_up = (in_pair_order(mine, got, 0) for (mine, _), got in zip(halves, came))
-    slope_both = spread(slope_down_slice.astype(bf), COLS, 2, 11, lanes=True)
-    slope_both = jnp.concatenate([piece[:, :slice_width] for piece in quarters(slope_both, 1)], axis=1).astype(f32)
-    packed = packed.reshape(-1)
-    bit = 1
-    while bit < cols:
-        packed = packed + swap_col(packed, bit)
-        bit *= 2
-    n = gain_first.shape[0]
-    m = query_gain.shape[0]
-    k = latent_gain.shape[0]
+    slope_up = in_pair_order(slope_up, came, 0)
+    n, m, k = gain_first.shape[0], query_gain.shape[0], latent_gain.shape[0]
+    packed = packed.reshape(-1)[: 2 * n + m + k]
+    packed = jnp.pad(packed, (0, n - m - k)).reshape(3, n).T
+    block = jnp.concatenate([slope_down_slice[:, :slice_width], packed], axis=1).astype(bf)
+    block = jnp.pad(block, ((0, 0), (0, -block.shape[1] % 128)))
+    blocks = quarters(spread(block, COLS, 2, 11, lanes=True), 1)
+    slope_both = jnp.concatenate([piece[:, :slice_width] for piece in blocks], axis=1).astype(f32)
+    packed = sum(piece[:, slice_width : slice_width + 3].astype(f32) for piece in blocks).T.reshape(-1)
 
     exact = functools.partial(
         lax.dot_general,

time: 952 us -> 939 us (0.986)
  waiting for transfers between devices: 108 us -> 145 us
  starting transfers between devices: 63 us -> 28.7 us
  other arithmetic: 99.5 us -> 86.2 us
    ppermute x16, waiting for transfers between devices: 83.6 us -> 129 us  [swap_row(): lax.ppermute(value, 'row', [(r, r ^ mask) for r in range(lax.axis_size('r...]
    ppermute x16, starting transfers between devices: 53.9 us -> 21.2 us  [swap_row(): lax.ppermute(value, 'row', [(r, r ^ mask) for r in range(lax.axis_size('r...]
    pallas_call x4 -> x5, Pallas kernels: 69.1 us -> 95.6 us  [spread(): pl.pallas_call(functools.partial(spread_kernel, dims, parts, lanes, relat...]
    pallas_call x1, Pallas kernels: 98 us -> 71.6 us  [ring_gather(): pl.pallas_call(functools.partial(ring_gather_kernel, rows, n), out_shape=...]
    pallas_call x1, Pallas kernels: 105 us -> 92.3 us  [ring_scatter(): pl.pallas_call(functools.partial(ring_scatter_kernel, rows, n, extra), ou...]
    pallas_call x4, Pallas kernels: 94.4 us -> 105 us  [fold(): pl.pallas_call(functools.partial(fold_kernel, dims, parts, lanes, relativ...]
    unnamed x235 -> x220, local copies, waits for them, and re-layouts: 42.5 us -> 34.9 us
  transfers between devices with their start and end apart: 31 -> 26, of which waited for: 7 -> 13; matrix products, arithmetic and copies ran while one was open for 25% -> 18% of each run, Pallas kernels for 24% -> 20%
where the time goes in v5:
time: 939 us; the launch traced here: 928 us
  Pallas kernels  467 us (50%)
  waiting for transfers between devices  145 us (15%)
  local copies, waits for them, and re-layouts  98.3 us (10%)
  matrix products  86.5 us (9%)
  other arithmetic  86.2 us (9%)
  starting transfers between devices  28.7 us (3%)
  between operations  16.8 us (2%)
    ppermute x16, waiting for transfers between devices, swap_row(): lax.ppermute(value, 'row', [(r, r ^ mask) for r in range(lax.axis_size('r...  129 us
    pallas_call x4, Pallas kernels, fold(): pl.pallas_call(functools.partial(fold_kernel, dims, parts, lanes, relativ...  105 us
    pallas_call x5, Pallas kernels, spread(): pl.pallas_call(functools.partial(spread_kernel, dims, parts, lanes, relat...  95.6 us
    pallas_call x1, Pallas kernels, ring_scatter(): pl.pallas_call(functools.partial(ring_scatter_kernel, rows, n, extra), ou...  92.3 us
    dot_general x24, matrix products, dot(): lax.dot_general(left, right, (dims, ((), ())), preferred_element_type=f32)  79.8 us
    pallas_call x1, Pallas kernels, ring_gather(): pl.pallas_call(functools.partial(ring_gather_kernel, rows, n), out_shape=...  71.6 us
    unnamed x220, local copies, waits for them, and re-layouts  34.9 us
    pallas_call x1, Pallas kernels, ffn_back(): pl.pallas_call(functools.partial(ffn_back_kernel, n), grid=(tokens // TOK...  33.8 us
  transfers between devices with their start and end apart: 26, of which 13 were waited for; matrix products, arithmetic and copies ran while one was open for 18% of the time, Pallas kernels for 20%

profile of v5, /device:TPU:0, one launch (start us, length us, event | category | flops | bytes accessed | tf_op | source)
XLA Modules:
  0.0 928.0 jit_solution(17757660858357308567)
XLA Ops:
  27.1 71.6 %ring_gather.1 = (bf16[8,2,160,384]{3,2,1,0:T(8,128)(2,1)}, bf16[8,2,48,1024]{3,2,1,0:T(8,128)(2,1)}, bf16[8,2,16,1280]{3,2,1,0:T(8,128)(2,1)}, bf16[512,2560]{1...) custom-call(bf16[2,160,384]{2,1,0:T(8,128)(2,1)} %bitcast.124, bf16[2,48,1024]{2,1,0:T(8,128)(2,1)} %bitcast.134, ...), custom_call_target="tpu_custom_call" | custom-call | tf_op jit(solution)/shard_map/ring_gather/pallas_call | solution.py:151
  101.9 25.9 %spread12.1 = bf16[8,128,2560]{2,1,0:T(8,128)(2,1)} custom-call(bf16[128,2560]{1,0:T(8,128)(2,1)} %pad_maximum_fusion.19.refs_0_), custom_call_target="tpu_custom_call" | custom-call | tf_op jit(solution)/shard_map/spread12/pallas_call | solution.py:619
  163.9 51.9 %collective-permute-done.5 = bf16[2,800,320]{1,2,0:T(8,128)(2,1)} collective-permute-done((bf16[2,800,320]{1,2,0:T(8,128)(2,1)}, bf16[2,800,320]{1,2,0:T(8,128)(2,1)}, u32[]{:S(2)}, u32[]{:S(2)}) %collective-permute-start.5) | collective-permute-done | bytes 1024032 | tf_op jit(solution)/shard_map/ppermute | solution.py:349
  227.9 19.5 %gather_behind.1 = bf16[288,2560]{1,0:T(8,128)(2,1)} custom-call(bf16[288,512]{1,0:T(8,128)(2,1)} %pad_maximum_fusion.24.key_ref), custom_call_target="tpu_custom_call" | custom-call | tf_op jit(solution)/shard_map/gather_behind/pallas_call | solution.py:685
  275.9 10.8 %attend.1 = (bf16[640,512]{1,0:T(8,128)(2,1)}, f32[640,512]{1,0:T(8,128)}, f32[5,2,512]{2,1,0:T(2,128)}) custom-call(s32[1]{0:T(128)} %bitcast.11.first_ref, bf16[1024,512]{1,0:T(8,128)(2,1)} %copy.116.qn_ref.qr_ref, bf16[1024,512]{1,0:T(8,128)(2,1)} %copy.116.qn_ref.qr_ref, bf16[2560,640]{1,0:T(8,128)(2,1)} %convolution_convert_fusion.4.k_ref, ...), custom_call_target="tpu_custom_call" | custom-call | tf_op jit(solution)/shard_map/attend/pallas_call | solution.py:920
  299.7 5.9 convolution_convert_fusion.6
  305.6 21.9 %fold4.1 = f32[128,2560]{1,0:T(8,128)} custom-call(bf16[4,128,2560]{2,1,0:T(8,128)(2,1)} %bitcast.114), custom_call_target="tpu_custom_call" | custom-call | tf_op jit(solution)/shard_map/fold4/pallas_call | solution.py:764
  328.9 10.8 %collective-permute-done.7.refs_6_ = bf16[1,800,640]{2,1,0:T(8,128)(2,1)} collective-permute-done((bf16[1,800,640]{2,1,0:T(8,128)(2,1)}, bf16[1,800,640]{2,1,0:T(8,128)(2,1)}, u32[]{:S(2)}, u32[]{:S(2)}) %collective-permute-start.7) | collective-permute-done | bytes 1024032 | tf_op jit(solution)/shard_map/ppermute | solution.py:349
  343.9 26.6 %spread5.1 = bf16[8,128,2560]{2,1,0:T(8,128)(2,1)} custom-call(bf16[128,2560]{1,0:T(8,128)(2,1)} %pad_maximum_fusion.20.refs_0_), custom_call_target="tpu_custom_call" | custom-call | tf_op jit(solution)/shard_map/spread5/pallas_call | solution.py:619
  375.1 11.8 %collective-permute-done.10.refs_7_ = bf16[1,800,640]{2,1,0:T(8,128)(2,1)} collective-permute-done((bf16[1,800,640]{2,1,0:T(8,128)(2,1)}, bf16[1,800,640]{2,1,0:T(8,128)(2,1)}, u32[]{:S(2)}, u32[]{:S(2)}) %collective-permute-start.10) | collective-permute-done | bytes 1024032 | tf_op jit(solution)/shard_map/ppermute | solution.py:349
  386.8 19.0 %ffn.1 = (f32[1024,800]{1,0:T(8,128)}, f32[1024,800]{1,0:T(8,128)}, bf16[1024,800]{1,0:T(8,128)(2,1)}) custom-call(bf16[1024,2560]{1,0:T(8,128)(2,1)} %bitcast.93, bf16[1,800,640]{2,1,0:T(8,128)(2,1)} %pad_maximum_fusion.16.refs_0_, bf16[1,800,640]{2,1,0:T(8,128)(2,1)} %collective-permute-done.3.refs_1_, ...), custom_call_target="tpu_custom_call" | custom-call | tf_op jit(solution)/shard_map/ffn/pallas_call | solution.py:1071
  411.0 33.8 %ffn_back.1 = (bf16[1024,800]{1,0:T(8,128)(2,1)}, bf16[1024,800]{1,0:T(8,128)(2,1)}, bf16[1024,2560]{1,0:T(8,128)(2,1)}, bf16[1024,2560]{1,0:T(8,128)(2,1)}) custom-call(bf16[1024,2560]{1,0:T(8,128)(2,1)} %bitcast.95, f32[1024,800]{1,0:T(8,128)} %get-tuple-element.95.gate_ref, f32[1024,800]{1,0:T(8,128)} %get-tuple-element.96.up_ref, ...), custom_call_target="tpu_custom_call" | custom-call | tf_op jit(solution)/shard_map/ffn_back/pallas_call | solution.py:1104
  453.1 30.9 %fold6.1 = f32[128,2560]{1,0:T(8,128)} custom-call(bf16[8,128,2560]{2,1,0:T(8,128)(2,1)} %bitcast.102), custom_call_target="tpu_custom_call" | custom-call | tf_op jit(solution)/shard_map/fold6/pallas_call | solution.py:764
  504.0 22.7 %spread7.1 = bf16[4,128,2560]{2,1,0:T(8,128)(2,1)} custom-call(bf16[128,2560]{1,0:T(8,128)(2,1)} %get-tuple-element.104.refs_0_), custom_call_target="tpu_custom_call" | custom-call | tf_op jit(solution)/shard_map/spread7/pallas_call | solution.py:619
  556.5 18.9 %attend_back.1 = (f32[640,512]{1,0:T(8,128)}, f32[384,512]{1,0:T(8,128)}, bf16[2560,640]{1,0:T(8,128)(2,1)}, bf16[2560,640]{1,0:T(8,128)(2,1)}, f32[2560,128]{1,0:T(8,128)}) custom-call(s32[1]{0:T(128)} %bitcast.11.first_ref, bf16[1024,512]{1,0:T(8,128)(2,1)} %copy.116.qn_ref.qr_ref, bf16[1024,512]{1,0:T(8,128)(2,1)} %copy.116.qn_ref.qr_ref, ...), custom_call_target="tpu_custom_call" | custom-call | tf_op jit(solution)/shard_map/attend_back/pallas_call | solution.py:1025
  598.1 16.0 %collective-permute-done.16 = bf16[800,640]{1,0:T(8,128)(2,1)} collective-permute-done((bf16[800,640]{1,0:T(8,128)(2,1)}, bf16[800,640]{1,0:T(8,128)(2,1)}, u32[]{:S(2)}, u32[]{:S(2)}) %collective-permute-start.16) | collective-permute-done | bytes 1024032 | tf_op jit(solution)/shard_map/ppermute | solution.py:349
  614.1 21.9 %collective-permute-done.14 = bf16[800,640]{1,0:T(8,128)(2,1)} collective-permute-done((bf16[800,640]{1,0:T(8,128)(2,1)}, bf16[800,640]{1,0:T(8,128)(2,1)}, u32[]{:S(2)}, u32[]{:S(2)}) %collective-permute-start.14) | collective-permute-done | bytes 1024032 | tf_op jit(solution)/shard_map/ppermute | solution.py:349
  647.4 19.7 %fold8.1 = f32[2208,128]{1,0:T(8,128)} custom-call(bf16[2208,512]{1,0:T(8,128)(2,1)} %copy-done.46), custom_call_target="tpu_custom_call" | custom-call | tf_op jit(solution)/shard_map/fold8/pallas_call | solution.py:764
  669.3 8.5 collective-permute-done.24
  708.5 10.0 %collective-permute-done.23 = f32[288,128]{1,0:T(8,128)} collective-permute-done((f32[288,128]{1,0:T(8,128)}, f32[288,128]{1,0:T(8,128)}, u32[]{:S(2)}, u32[]{:S(2)}) %collective-permute-start.23) | collective-permute-done | bytes 147488 | tf_op jit(solution)/shard_map/ppermute | solution.py:299
  720.8 10.7 %spread9.1 = bf16[1056,512]{1,0:T(8,128)(2,1)} custom-call(bf16[1056,128]{1,0:T(8,128)(2,1)} %pad_maximum_fusion.25.refs_0_), custom_call_target="tpu_custom_call" | custom-call | tf_op jit(solution)/shard_map/spread9/pallas_call | solution.py:619
  737.2 32.6 %fold10.1 = (f32[128,2560]{1,0:T(8,128)}, bf16[2,800,320]{2,1,0:T(8,128)(2,1)}) custom-call(bf16[4,128,2560]{2,1,0:T(8,128)(2,1)} %bitcast.113, bf16[2,800,320]{2,1,0:T(8,128)(2,1)} %pad_maximum_fusion.13.refs_1_), custom_call_target="tpu_custom_call" | custom-call | tf_op jit(solution)/shard_map/fold10/pallas_call | solution.py:764
  781.4 92.3 %ring_scatter.1 = (f32[2,160,640]{2,1,0:T(8,128)}, f32[2,48,1024]{2,1,0:T(8,128)}, f32[2,16,1280]{2,1,0:T(8,128)}, f32[2,160,384]{2,1,0:T(8,128)}, f32[2,3,128]{...) custom-call(bf16[8,2,160,640]{3,2,1,0:T(8,128)(2,1)} %bitcast.107, ...), custom_call_target="tpu_custom_call" | custom-call | tf_op jit(solution)/shard_map/ring_scatter/pallas_call | solution.py:277
  876.6 9.7 %spread11.1 = bf16[320,1536]{1,0:T(8,128)(2,1)} custom-call(bf16[320,384]{1,0:T(8,128)(2,1)} %fusion.62.refs_0_), custom_call_target="tpu_custom_call" | custom-call | tf_op jit(solution)/shard_map/spread11/pallas_call | solution.py:619
  (468 shorter events, 308.0 us)
Async XLA Ops:
  7.2 292.5 %all-gather.2.cloned.1.call-start = ((), (), s32[]{:S(2)}) async-start(), calls=%async_computation | async-start | bytes 3686400 | tf_op jit(solution)/shard_map/all_gather | solution.py:1157
  129.3 98.7 %collective-permute-start.3 = (bf16[1,800,640]{2,1,0:T(8,128)(2,1)}, bf16[1,800,640]{2,1,0:T(8,128)(2,1)}, u32[]{:S(2)}, u32[]{:S(2)}) collective-permute-start(bf16[1,800,640]{2,1,0:T(8,128)(2,1)} %pad_maximum_fusion.16.refs_0_), channel_id=1, source_target_pairs={{0,4},{4,0},{8,12},{12,8},{16,20},{20,16},{24,28},{28,24},{1,5},{5... | collective-permute-start | bytes 3072008 | tf_op jit(solution)/shard_map/ppermute | solution.py:349
  130.8 97.1 %collective-permute-start.4 = (bf16[1,800,640]{2,1,0:T(8,128)(2,1)}, bf16[1,800,640]{2,1,0:T(8,128)(2,1)}, u32[]{:S(2)}, u32[]{:S(2)}) collective-permute-start(bf16[1,800,640]{2,1,0:T(8,128)(2,1)} %pad_maximum_fusion.16.refs_0_), channel_id=1, source_target_pairs={{0,16},{4,20},{8,24},{12,28},{16,0},{20,4},{24,8},{28,12},{1,17},{... | collective-permute-start | bytes 3072008 | tf_op jit(solution)/shard_map/ppermute | solution.py:349
  139.9 23.7 %collective-permute-start = (f32[264,512]{1,0:T(8,128)}, f32[264,512]{1,0:T(8,128)}, u32[]{:S(2)}, u32[]{:S(2)}) collective-permute-start(f32[264,512]{1,0:T(8,128)} %fusion.32), channel_id=1, source_target_pairs={{0,2},{1,3},{2,0},{3,1},{4,6},{5,7},{6,4},{7,5},{8,10},{9,11},{10,... | collective-permute-start | bytes 1622024 | tf_op jit(solution)/shard_map/ppermute | solution.py:303
  141.1 81.0 %collective-permute-start.2 = (f32[264,512]{1,0:T(8,128)}, f32[264,512]{1,0:T(8,128)}, u32[]{:S(2)}, u32[]{:S(2)}) collective-permute-start(f32[264,512]{1,0:T(8,128)} %fusion.32), channel_id=1, source_target_pairs={{0,1},{1,0},{2,3},{3,2},{4,5},{5,4},{6,7},{7,6},{8,9},{9,8},{10,11... | collective-permute-start | bytes 1622024 | tf_op jit(solution)/shard_map/ppermute | solution.py:303
  144.6 71.1 %collective-permute-start.5 = (bf16[2,800,320]{1,2,0:T(8,128)(2,1)}, bf16[2,800,320]{1,2,0:T(8,128)(2,1)}, u32[]{:S(2)}, u32[]{:S(2)}) collective-permute-start(bf16[2,800,320]{1,2,0:T(8,128)(2,1)} %copy.115), channel_id=1, source_target_pairs={{0,8},{4,12},{8,0},{12,4},{16,24},{20,28},{24,16},{28,20},{1,9},{5... | collective-permute-start | bytes 3072008 | tf_op jit(solution)/shard_map/ppermute | solution.py:349
  163.6 58.5 %collective-permute-start.1 = (f32[264,512]{1,0:T(8,128)}, f32[264,512]{1,0:T(8,128)}, u32[]{:S(2)}, u32[]{:S(2)}) collective-permute-start(f32[264,512]{1,0:T(8,128)} %collective-permute-done), channel_id=1, source_target_pairs={{0,1},{1,0},{2,3},{3,2},{4,5},{5,4},{6,7},{7,6},{8,9},{9,8},{10,11... | collective-permute-start | bytes 1622024 | tf_op jit(solution)/shard_map/ppermute | solution.py:303
  248.5 91.3 %collective-permute-start.8 = (bf16[1,800,640]{2,1,0:T(8,128)(2,1)}, bf16[1,800,640]{2,1,0:T(8,128)(2,1)}, u32[]{:S(2)}, u32[]{:S(2)}) collective-permute-start(bf16[1,800,640]{2,1,0:T(8,128)(2,1)} %get-tuple-element.89), channel_id=1, source_target_pairs={{0,16},{4,20},{8,24},{12,28},{16,0},{20,4},{24,8},{28,12},{1,17},{... | collective-permute-start | bytes 3072008 | tf_op jit(solution)/shard_map/ppermute | solution.py:349
  248.5 91.3 %collective-permute-start.7 = (bf16[1,800,640]{2,1,0:T(8,128)(2,1)}, bf16[1,800,640]{2,1,0:T(8,128)(2,1)}, u32[]{:S(2)}, u32[]{:S(2)}) collective-permute-start(bf16[1,800,640]{2,1,0:T(8,128)(2,1)} %get-tuple-element.87), channel_id=1, source_target_pairs={{0,16},{4,20},{8,24},{12,28},{16,0},{20,4},{24,8},{28,12},{1,17},{... | collective-permute-start | bytes 3072008 | tf_op jit(solution)/shard_map/ppermute | solution.py:349
  251.4 48.3 %collective-permute-start.6 = (bf16[2,800,640]{2,1,0:T(8,128)(2,1)}, bf16[2,800,640]{2,1,0:T(8,128)(2,1)}, u32[]{:S(2)}, u32[]{:S(2)}) collective-permute-start(bf16[2,800,640]{2,1,0:T(8,128)(2,1)} %pad_maximum_fusion.4.refs_4_.refs_8_), channel_id=1, source_target_pairs={{0,4},{4,0},{8,12},{12,8},{16,20},{20,16},{24,28},{28,24},{1,5},{5... | collective-permute-start | bytes 6144008 | tf_op jit(solution)/shard_map/ppermute | solution.py:349
  286.7 88.3 %collective-permute-start.9 = (bf16[1,800,640]{2,1,0:T(8,128)(2,1)}, bf16[1,800,640]{2,1,0:T(8,128)(2,1)}, u32[]{:S(2)}, u32[]{:S(2)}) collective-permute-start(bf16[1,800,640]{2,1,0:T(8,128)(2,1)} %collective-permute-done.4.refs_2_), channel_id=1, source_target_pairs={{0,4},{4,0},{8,12},{12,8},{16,20},{20,16},{24,28},{28,24},{1,5},{5... | collective-permute-start | bytes 3072008 | tf_op jit(solution)/shard_map/ppermute | solution.py:349
  339.9 71.0 %collective-permute-start.11 = (bf16[1,800,640]{2,1,0:T(8,128)(2,1)}, bf16[1,800,640]{2,1,0:T(8,128)(2,1)}, u32[]{:S(2)}, u32[]{:S(2)}) collective-permute-start(bf16[1,800,640]{2,1,0:T(8,128)(2,1)} %collective-permute-done.8.refs_10_), channel_id=1, source_target_pairs={{0,4},{4,0},{8,12},{12,8},{16,20},{20,16},{24,28},{28,24},{1,5},{5... | collective-permute-start | bytes 3072008 | tf_op jit(solution)/shard_map/ppermute | solution.py:349
  341.0 45.8 %collective-permute-start.10 = (bf16[1,800,640]{2,1,0:T(8,128)(2,1)}, bf16[1,800,640]{2,1,0:T(8,128)(2,1)}, u32[]{:S(2)}, u32[]{:S(2)}) collective-permute-start(bf16[1,800,640]{2,1,0:T(8,128)(2,1)} %collective-permute-done.7.refs_6_), channel_id=1, source_target_pairs={{0,4},{4,0},{8,12},{12,8},{16,20},{20,16},{24,28},{28,24},{1,5},{5... | collective-permute-start | bytes 3072008 | tf_op jit(solution)/shard_map/ppermute | solution.py:349
  448.3 55.7 %collective-permute-start.13 = (bf16[512,2560]{1,0:T(8,128)(2,1)}, bf16[512,2560]{1,0:T(8,128)(2,1)}, u32[]{:S(2)}, u32[]{:S(2)}) collective-permute-start(bf16[512,2560]{1,0:T(8,128)(2,1)} %pad_maximum_fusion.2), channel_id=1, source_target_pairs={{0,1},{1,0},{2,3},{3,2},{4,5},{5,4},{6,7},{7,6},{8,9},{9,8},{10,11... | collective-permute-start | bytes 7864328 | tf_op jit(solution)/shard_map/ppermute | solution.py:303
  448.3 55.7 %collective-permute-start.12 = (bf16[800,1280]{1,0:T(8,128)(2,1)}, bf16[800,1280]{1,0:T(8,128)(2,1)}, u32[]{:S(2)}, u32[]{:S(2)}) collective-permute-start(bf16[800,1280]{1,0:T(8,128)(2,1)} %convolution_convert_fusion.10), channel_id=1, source_target_pairs={{0,4},{4,0},{8,12},{12,8},{16,20},{20,16},{24,28},{28,24},{1,5},{5... | collective-permute-start | bytes 6144008 | tf_op jit(solution)/shard_map/ppermute | solution.py:349
  486.2 53.7 %collective-permute-start.15 = (bf16[800,1280]{1,0:T(8,128)(2,1)}, bf16[800,1280]{1,0:T(8,128)(2,1)}, u32[]{:S(2)}, u32[]{:S(2)}) collective-permute-start(bf16[800,1280]{1,0:T(8,128)(2,1)} %convolution_convert_fusion.9), channel_id=1, source_target_pairs={{0,4},{4,0},{8,12},{12,8},{16,20},{20,16},{24,28},{28,24},{1,5},{5... | collective-permute-start | bytes 6144008 | tf_op jit(solution)/shard_map/ppermute | solution.py:349
  530.1 105.9 %collective-permute-start.18 = (bf16[256,2560]{1,0:T(8,128)(2,1)}, bf16[256,2560]{1,0:T(8,128)(2,1)}, u32[]{:S(2)}, u32[]{:S(2)}) collective-permute-start(bf16[256,2560]{1,0:T(8,128)(2,1)} %pad_maximum_fusion.12), channel_id=1, source_target_pairs={{0,2},{1,3},{2,0},{3,1},{4,6},{5,7},{6,4},{7,5},{8,10},{9,11},{10,... | collective-permute-start | bytes 3932168 | tf_op jit(solution)/shard_map/ppermute | solution.py:303
  530.9 105.1 %collective-permute-start.17 = (bf16[800,1280]{1,0:T(8,128)(2,1)}, bf16[800,1280]{1,0:T(8,128)(2,1)}, u32[]{:S(2)}, u32[]{:S(2)}) collective-permute-start(bf16[800,1280]{1,0:T(8,128)(2,1)} %convolution_convert_fusion.8), channel_id=1, source_target_pairs={{0,4},{4,0},{8,12},{12,8},{16,20},{20,16},{24,28},{28,24},{1,5},{5... | collective-permute-start | bytes 6144008 | tf_op jit(solution)/shard_map/ppermute | solution.py:349
  545.1 68.9 %collective-permute-start.16 = (bf16[800,640]{1,0:T(8,128)(2,1)}, bf16[800,640]{1,0:T(8,128)(2,1)}, u32[]{:S(2)}, u32[]{:S(2)}) collective-permute-start(bf16[800,640]{1,0:T(8,128)(2,1)} %split.646), channel_id=1, source_target_pairs={{0,16},{4,20},{8,24},{12,28},{16,0},{20,4},{24,8},{28,12},{1,17},{... | collective-permute-start | bytes 3072008 | tf_op jit(solution)/shard_map/ppermute | solution.py:349
  553.1 82.8 %collective-permute-start.14 = (bf16[800,640]{1,0:T(8,128)(2,1)}, bf16[800,640]{1,0:T(8,128)(2,1)}, u32[]{:S(2)}, u32[]{:S(2)}) collective-permute-start(bf16[800,640]{1,0:T(8,128)(2,1)} %split.647), channel_id=1, source_target_pairs={{0,16},{4,20},{8,24},{12,28},{16,0},{20,4},{24,8},{28,12},{1,17},{... | collective-permute-start | bytes 3072008 | tf_op jit(solution)/shard_map/ppermute | solution.py:349
  641.2 46.4 %collective-permute-start.19 = (bf16[800,640]{1,0:T(8,128)(2,1)}, bf16[800,640]{1,0:T(8,128)(2,1)}, u32[]{:S(2)}, u32[]{:S(2)}) collective-permute-start(bf16[800,640]{1,0:T(8,128)(2,1)} %split.645), channel_id=1, source_target_pairs={{0,16},{4,20},{8,24},{12,28},{16,0},{20,4},{24,8},{28,12},{1,17},{... | collective-permute-start | bytes 3072008 | tf_op jit(solution)/shard_map/ppermute | solution.py:349
  645.5 32.4 %collective-permute-start.24 = (bf16[128,2560]{1,0:T(8,128)(2,1)S(1)}, bf16[128,2560]{1,0:T(8,128)(2,1)S(1)}, u32[]{:S(2)}, u32[]{:S(2)}) collective-permute-start(bf16[128,2560]{1,0:T(8,128)(2,1)S(1)} %add_convert_fusion), channel_id=1, source_target_pairs={{0,8},{4,12},{8,0},{12,4},{16,24},{20,28},{24,16},{28,20},{1,9},{5... | collective-permute-start | bytes 1966088 | tf_op jit(solution)/shard_map/ppermute | solution.py:349
  696.9 11.6 %collective-permute-start.22 = (f32[288,128]{1,0:T(8,128)}, f32[288,128]{1,0:T(8,128)}, u32[]{:S(2)}, u32[]{:S(2)}) collective-permute-start(f32[288,128]{1,0:T(8,128)} %get-tuple-element.254), channel_id=1, source_target_pairs={{12,0},{16,4},{20,8},{24,12},{28,16},{13,1},{17,5},{21,9},{25,13},... | collective-permute-start | bytes 442376 | tf_op jit(solution)/shard_map/ppermute | solution.py:299
  698.2 20.3 %collective-permute-start.23 = (f32[288,128]{1,0:T(8,128)}, f32[288,128]{1,0:T(8,128)}, u32[]{:S(2)}, u32[]{:S(2)}) collective-permute-start(f32[288,128]{1,0:T(8,128)} %get-tuple-element.253), channel_id=1, source_target_pairs={{16,0},{20,4},{24,8},{28,12},{17,1},{21,5},{25,9},{29,13},{18,2},{... | collective-permute-start | bytes 442376 | tf_op jit(solution)/shard_map/ppermute | solution.py:299
  (101 other events, 1108.6 us)
Sparse Core Ops, SparseCore 0:
  147.6 93.6 all-gather.1

commit v6 on v5

--- a/solution.py
+++ b/solution.py
@@ -375,6 +375,13 @@
         for side, chunk in enumerate(jnp.split(group, 2, axis=1)):
             chunks[group_row(g, side)] = chunk
     return jnp.concatenate(chunks, axis=1)
+
+
+def group_gather(own, other):
+    both = jnp.concatenate([own, other], axis=0)
+    across = swap_col(both, 2)
+    pieces = [both, swap_col(both, 1), across, swap_col(across, 1)]
+    return jnp.concatenate([p for half in zip(*(jnp.split(piece, 2, axis=0) for piece in pieces)) for p in half], axis=0)
 
 
 class GroupScatter:
@@ -1151,10 +1158,11 @@
         (down_block, query_up_low, latent_up_low), tokens, cotangent, ffn_weights.away[:1]
     )
     first_own = ffn_weights.arrived(came, 0, 1)
-    back_down = spread(features_by_group((RES * own_up).astype(bf)), GROUP, 4, 12, relative=True)
-    others = swap_row(after(ffn_weights.away[1:], back_down), PAIR)
-    early = (ffn_weights.near_own(first_own, 0, 1, back_down), ffn_weights.far(0, back_down), others)
-    wide_output = lax.all_gather(after(output_weight, back_down).astype(bf).T, "row", axis=0, tiled=True)
+    own_down = features_by_group((RES * own_up).astype(bf))
+    other_down = swap_row(own_down, PAIR)
+    others = swap_row(after(ffn_weights.away[1:], wide_down), PAIR)
+    early = (ffn_weights.near_own(first_own, 0, 1, wide_down), ffn_weights.far(0, wide_down), others, other_down)
+    wide_output = lax.all_gather(after(output_weight, wide_down).astype(bf).T, "row", axis=0, tiled=True)
     gain_one = wide_down[:, slice_width].astype(f32)
     gain_two = wide_down[:, slice_width + 1].astype(f32)
     small_gains = wide_down[:, slice_width + 2].reshape(rows, -1).astype(f32)
@@ -1167,7 +1175,7 @@
     first_in = (residual * inverse_of(residual, 1) * gain_one).astype(bf)
     own_residual = pick(quarters(features, 0)).astype(f32)
 
-    latents = jnp.concatenate(col_gather(dot(wide_down, first_in, ((0,), (1,)))), axis=0)
+    latents = spread(dot(wide_down, first_in, ((0,), (1,))), COLS, 3, 3)
     query_latent, latent_part = latents[:QR], latents[QR : QR + KR]
     inverse_query, inverse_latent = inverse_of(query_latent, 0), inverse_of(latent_part, 0)
     query_in = (query_latent * inverse_query * query_scale).astype(bf)
@@ -1179,6 +1187,7 @@
     other_own = ffn_weights.arrived(others, 1, 3)
     beside = ffn_weights.near_own(other_own, 1, 3, key_parts)
     far_up, far_down = ffn_weights.far(1, key_parts), ffn_weights.far(2, key_parts)
+    back_down = group_gather(*after((own_down, other_down), key_parts))
     latent_all = key_parts[:KR]
     turned_t = jnp.concatenate([key_parts[KR : KR + half]] * 4 + [key_parts[KR + half :]] * 4, axis=0)
     turned = turned_t.T
@@ -1205,7 +1214,7 @@
 
     gate_pieces = ffn_weights.near(0, out_t)
     out_t = after(out_t, beside)
-    branch = dot(out_t, wide_output, ((0,), (1,)))
+    branch = after(dot(out_t, wide_output, ((0,), (1,))), back_down)
     middle = own_residual + RES * fold(branch, COLS, 8, 4)
     middle = after(middle, far_up)
     up_pieces = ffn_weights.near(1, middle)

time: 939 us -> 929 us (0.989)
  Pallas kernels: 467 us -> 451 us
  waiting for transfers between devices: 145 us -> 133 us
    ppermute x16 -> x17, waiting for transfers between devices: 129 us -> 117 us  [swap_row(): lax.ppermute(value, 'row', [(r, r ^ mask) for r in range(lax.axis_size('r...]
    pallas_call x5, Pallas kernels: 95.6 us -> 85.8 us  [spread(): pl.pallas_call(functools.partial(spread_kernel, dims, parts, lanes, relat...]
    unnamed x220 -> x249, local copies, waits for them, and re-layouts: 34.9 us -> 43.2 us
    ppermute x16 -> x17, starting transfers between devices: 21.2 us -> 21.4 us  [swap_row(): lax.ppermute(value, 'row', [(r, r ^ mask) for r in range(lax.axis_size('r...]
  transfers between devices with their start and end apart: 26 -> 27, of which waited for: 13 -> 12; matrix products, arithmetic and copies ran while one was open for 18% -> 20% of each run, Pallas kernels for 20% -> 22%
where the time goes in v6:
time: 929 us; the launch traced here: 921 us
  Pallas kernels  451 us (49%)
  waiting for transfers between devices  133 us (14%)
  local copies, waits for them, and re-layouts  107 us (12%)
  other arithmetic  91.3 us (10%)
  matrix products  90 us (10%)
  starting transfers between devices  31.1 us (3%)
  between operations  16.8 us (2%)
    ppermute x17, waiting for transfers between devices, swap_row(): lax.ppermute(value, 'row', [(r, r ^ mask) for r in range(lax.axis_size('r...  117 us
    pallas_call x4, Pallas kernels, fold(): pl.pallas_call(functools.partial(fold_kernel, dims, parts, lanes, relativ...  103 us
    pallas_call x1, Pallas kernels, ring_scatter(): pl.pallas_call(functools.partial(ring_scatter_kernel, rows, n, extra), ou...  92.7 us
    pallas_call x5, Pallas kernels, spread(): pl.pallas_call(functools.partial(spread_kernel, dims, parts, lanes, relat...  85.8 us
    dot_general x24, matrix products, dot(): lax.dot_general(left, right, (dims, ((), ())), preferred_element_type=f32)  83.3 us
    pallas_call x1, Pallas kernels, ring_gather(): pl.pallas_call(functools.partial(ring_gather_kernel, rows, n), out_shape=...  71.6 us
    unnamed x249, local copies, waits for them, and re-layouts  43.2 us
    pallas_call x1, Pallas kernels, ffn_back(): pl.pallas_call(functools.partial(ffn_back_kernel, n), grid=(tokens // TOK...  33.8 us
  transfers between devices with their start and end apart: 27, of which 12 were waited for; matrix products, arithmetic and copies ran while one was open for 20% of the time, Pallas kernels for 22%

profile of v6, /device:TPU:0, one launch (start us, length us, event | category | flops | bytes accessed | tf_op | source)
XLA Modules:
  0.0 921.0 jit_solution(7006596230492779085)
XLA Ops:
  27.1 71.6 %ring_gather.1 = (bf16[8,2,160,384]{3,2,1,0:T(8,128)(2,1)}, bf16[8,2,48,1024]{3,2,1,0:T(8,128)(2,1)}, bf16[8,2,16,1280]{3,2,1,0:T(8,128)(2,1)}, bf16[512,2560]{1...) custom-call(bf16[2,160,384]{2,1,0:T(8,128)(2,1)} %bitcast.130, bf16[2,48,1024]{2,1,0:T(8,128)(2,1)} %bitcast.140, ...), custom_call_target="tpu_custom_call" | custom-call | tf_op jit(solution)/shard_map/ring_gather/pallas_call | solution.py:151
  120.6 18.3 %spread3.1 = f32[4,264,512]{2,1,0:T(8,128)} custom-call(f32[264,512]{1,0:T(8,128)} %fusion.32.refs_0_), custom_call_target="tpu_custom_call" | custom-call | tf_op jit(solution)/shard_map/spread3/pallas_call | solution.py:626
  184.0 25.1 %collective-permute-done.3 = bf16[128,2560]{1,0:T(8,128)(2,1)} collective-permute-done((bf16[128,2560]{1,0:T(8,128)(2,1)}, bf16[128,2560]{1,0:T(8,128)(2,1)}, u32[]{:S(2)}, u32[]{:S(2)}) %collective-permute-start.3) | collective-permute-done | bytes 655392 | tf_op jit(solution)/shard_map/ppermute | solution.py:349
  209.0 15.8 %gather_behind.1 = bf16[288,2560]{1,0:T(8,128)(2,1)} custom-call(bf16[288,512]{1,0:T(8,128)(2,1)} %pad_maximum_fusion.20.key_ref), custom_call_target="tpu_custom_call" | custom-call | tf_op jit(solution)/shard_map/gather_behind/pallas_call | solution.py:692
  250.3 10.9 %attend.1 = (bf16[640,512]{1,0:T(8,128)(2,1)}, f32[640,512]{1,0:T(8,128)}, f32[5,2,512]{2,1,0:T(2,128)}) custom-call(s32[1]{0:T(128)} %bitcast.11.first_ref, bf16[1024,512]{1,0:T(8,128)(2,1)} %copy.116.qn_ref.qr_ref, bf16[1024,512]{1,0:T(8,128)(2,1)} %copy.116.qn_ref.qr_ref, bf16[2560,640]{1,0:T(8,128)(2,1)} %convolution_convert_fusion.4.k_ref, ...), custom_call_target="tpu_custom_call" | custom-call | tf_op jit(solution)/shard_map/attend/pallas_call | solution.py:927
  274.6 16.8 %collective-permute-done.4.refs_5_.refs_9_ = bf16[2,800,640]{2,1,0:T(8,128)(2,1)} collective-permute-done((bf16[2,800,640]{2,1,0:T(8,128)(2,1)S(1)}, bf16[2,800,640]{2,1,0:T(8,128)(2,1)}, u32[]{:S(2)}, u32[]{:S(2)}) %collective-permute-start.4) | collective-permute-done | bytes 2048032 | tf_op jit(solution)/shard_map/ppermute | solution.py:349
  305.3 20.5 %fold4.1 = f32[128,2560]{1,0:T(8,128)} custom-call(bf16[4,128,2560]{2,1,0:T(8,128)(2,1)} %bitcast.120), custom_call_target="tpu_custom_call" | custom-call | tf_op jit(solution)/shard_map/fold4/pallas_call | solution.py:771
  334.7 26.0 %spread5.1 = bf16[8,128,2560]{2,1,0:T(8,128)(2,1)} custom-call(bf16[128,2560]{1,0:T(8,128)(2,1)} %pad_maximum_fusion.17.refs_0_), custom_call_target="tpu_custom_call" | custom-call | tf_op jit(solution)/shard_map/spread5/pallas_call | solution.py:626
  365.2 12.4 %collective-permute-done.11.refs_7_ = bf16[1,800,640]{2,1,0:T(8,128)(2,1)} collective-permute-done((bf16[1,800,640]{2,1,0:T(8,128)(2,1)}, bf16[1,800,640]{2,1,0:T(8,128)(2,1)}, u32[]{:S(2)}, u32[]{:S(2)}) %collective-permute-start.11) | collective-permute-done | bytes 1024032 | tf_op jit(solution)/shard_map/ppermute | solution.py:349
  377.6 19.0 %ffn.1 = (f32[1024,800]{1,0:T(8,128)}, f32[1024,800]{1,0:T(8,128)}, bf16[1024,800]{1,0:T(8,128)(2,1)}) custom-call(bf16[1024,2560]{1,0:T(8,128)(2,1)} %bitcast.93, bf16[1,800,640]{2,1,0:T(8,128)(2,1)} %pad_maximum_fusion.13.refs_0_, bf16[1,800,640]{2,1,0:T(8,128)(2,1)} %collective-permute-done.refs_1_, bf16[1,800,640]{2,1,0:T(8,128)(2,1)} %collective-permute-done.1.refs_2_, ...), custom_call_target="tpu_custom_call" | custom-call | tf_op jit(solution)/shard_map/ffn/pallas_call | solution.py:1078
  402.1 33.8 %ffn_back.1 = (bf16[1024,800]{1,0:T(8,128)(2,1)}, bf16[1024,800]{1,0:T(8,128)(2,1)}, bf16[1024,2560]{1,0:T(8,128)(2,1)}, bf16[1024,2560]{1,0:T(8,128)(2,1)}) custom-call(bf16[1024,2560]{1,0:T(8,128)(2,1)} %copy-done.2, f32[1024,800]{1,0:T(8,128)} %get-tuple-element.101.gate_ref, f32[1024,800]{1,0:T(8,128)} %get-tuple-element.102.up_ref, ...), custom_call_target="tpu_custom_call" | custom-call | tf_op jit(solution)/shard_map/ffn_back/pallas_call | solution.py:1111
  443.8 30.7 %fold6.1 = f32[128,2560]{1,0:T(8,128)} custom-call(bf16[8,128,2560]{2,1,0:T(8,128)(2,1)} %bitcast.109), custom_call_target="tpu_custom_call" | custom-call | tf_op jit(solution)/shard_map/fold6/pallas_call | solution.py:771
  492.5 21.9 %spread7.1 = bf16[4,128,2560]{2,1,0:T(8,128)(2,1)} custom-call(bf16[128,2560]{1,0:T(8,128)(2,1)} %get-tuple-element.110.refs_0_), custom_call_target="tpu_custom_call" | custom-call | tf_op jit(solution)/shard_map/spread7/pallas_call | solution.py:626
  523.0 8.0 collective-permute-done.16
  547.7 18.9 %attend_back.1 = (f32[640,512]{1,0:T(8,128)}, f32[384,512]{1,0:T(8,128)}, bf16[2560,640]{1,0:T(8,128)(2,1)}, bf16[2560,640]{1,0:T(8,128)(2,1)}, f32[2560,128]{1,0:T(8,128)}) custom-call(s32[1]{0:T(128)} %bitcast.11.first_ref, bf16[1024,512]{1,0:T(8,128)(2,1)} %copy.116.qn_ref.qr_ref, bf16[1024,512]{1,0:T(8,128)(2,1)} %copy.116.qn_ref.qr_ref, ...), custom_call_target="tpu_custom_call" | custom-call | tf_op jit(solution)/shard_map/attend_back/pallas_call | solution.py:1032
  589.2 15.8 %collective-permute-done.17 = bf16[800,640]{1,0:T(8,128)(2,1)} collective-permute-done((bf16[800,640]{1,0:T(8,128)(2,1)}, bf16[800,640]{1,0:T(8,128)(2,1)}, u32[]{:S(2)}, u32[]{:S(2)}) %collective-permute-start.17) | collective-permute-done | bytes 1024032 | tf_op jit(solution)/shard_map/ppermute | solution.py:349
  605.1 21.9 %collective-permute-done.15 = bf16[800,640]{1,0:T(8,128)(2,1)} collective-permute-done((bf16[800,640]{1,0:T(8,128)(2,1)}, bf16[800,640]{1,0:T(8,128)(2,1)}, u32[]{:S(2)}, u32[]{:S(2)}) %collective-permute-start.15) | collective-permute-done | bytes 1024032 | tf_op jit(solution)/shard_map/ppermute | solution.py:349
  639.5 18.6 %fold8.1 = f32[2208,128]{1,0:T(8,128)} custom-call(bf16[2208,512]{1,0:T(8,128)(2,1)} %copy-done.43), custom_call_target="tpu_custom_call" | custom-call | tf_op jit(solution)/shard_map/fold8/pallas_call | solution.py:771
  660.4 8.8 collective-permute-done.25
  701.0 10.4 %collective-permute-done.24 = f32[288,128]{1,0:T(8,128)} collective-permute-done((f32[288,128]{1,0:T(8,128)S(1)}, f32[288,128]{1,0:T(8,128)}, u32[]{:S(2)}, u32[]{:S(2)}) %collective-permute-start.24) | collective-permute-done | bytes 147488 | tf_op jit(solution)/shard_map/ppermute | solution.py:299
  713.7 9.9 %spread9.1 = bf16[1056,512]{1,0:T(8,128)(2,1)} custom-call(bf16[1056,128]{1,0:T(8,128)(2,1)} %pad_maximum_fusion.21.refs_0_), custom_call_target="tpu_custom_call" | custom-call | tf_op jit(solution)/shard_map/spread9/pallas_call | solution.py:626
  730.0 32.9 %fold10.1 = (f32[128,2560]{1,0:T(8,128)}, bf16[2,800,320]{2,1,0:T(8,128)(2,1)}) custom-call(bf16[4,128,2560]{2,1,0:T(8,128)(2,1)} %bitcast.119, bf16[2,800,320]{2,1,0:T(8,128)(2,1)} %pad_maximum_fusion.10.refs_1_), custom_call_target="tpu_custom_call" | custom-call | tf_op jit(solution)/shard_map/fold10/pallas_call | solution.py:771
  774.5 92.7 %ring_scatter.1 = (f32[2,160,640]{2,1,0:T(8,128)}, f32[2,48,1024]{2,1,0:T(8,128)}, f32[2,16,1280]{2,1,0:T(8,128)}, f32[2,160,384]{2,1,0:T(8,128)}, f32[2,3,128]{...) custom-call(bf16[8,2,160,640]{3,2,1,0:T(8,128)(2,1)} %bitcast.114, ...), custom_call_target="tpu_custom_call" | custom-call | tf_op jit(solution)/shard_map/ring_scatter/pallas_call | solution.py:277
  870.0 9.8 %spread11.1 = bf16[320,1536]{1,0:T(8,128)(2,1)} custom-call(bf16[320,384]{1,0:T(8,128)(2,1)} %fusion.62.refs_0_), custom_call_target="tpu_custom_call" | custom-call | tf_op jit(solution)/shard_map/spread11/pallas_call | solution.py:626
  (499 shorter events, 333.8 us)
Async XLA Ops:
  7.2 292.5 %all-gather.2.cloned.1.call-start = ((), (), s32[]{:S(2)}) async-start(), calls=%async_computation | async-start | bytes 3686400 | tf_op jit(solution)/shard_map/all_gather | solution.py:1165
  101.4 107.6 %collective-permute-start = (bf16[1,800,640]{2,1,0:T(8,128)(2,1)}, bf16[1,800,640]{2,1,0:T(8,128)(2,1)}, u32[]{:S(2)}, u32[]{:S(2)}) collective-permute-start(bf16[1,800,640]{2,1,0:T(8,128)(2,1)} %pad_maximum_fusion.13.refs_0_), channel_id=1, source_target_pairs={{0,4},{4,0},{8,12},{12,8},{16,20},{20,16},{24,28},{28,24},{1,5},{5... | collective-permute-start | bytes 3072008 | tf_op jit(solution)/shard_map/ppermute | solution.py:349
  102.9 106.1 %collective-permute-start.1 = (bf16[1,800,640]{2,1,0:T(8,128)(2,1)}, bf16[1,800,640]{2,1,0:T(8,128)(2,1)}, u32[]{:S(2)}, u32[]{:S(2)}) collective-permute-start(bf16[1,800,640]{2,1,0:T(8,128)(2,1)} %pad_maximum_fusion.13.refs_0_), channel_id=1, source_target_pairs={{0,16},{4,20},{8,24},{12,28},{16,0},{20,4},{24,8},{28,12},{1,17},{... | collective-permute-start | bytes 3072008 | tf_op jit(solution)/shard_map/ppermute | solution.py:349
  107.3 71.4 %collective-permute-start.2 = (bf16[2,800,320]{1,2,0:T(8,128)(2,1)}, bf16[2,800,320]{1,2,0:T(8,128)(2,1)}, u32[]{:S(2)}, u32[]{:S(2)}) collective-permute-start(bf16[2,800,320]{1,2,0:T(8,128)(2,1)} %copy.115), channel_id=1, source_target_pairs={{0,8},{4,12},{8,0},{12,4},{16,24},{20,28},{24,16},{28,20},{1,9},{5... | collective-permute-start | bytes 3072008 | tf_op jit(solution)/shard_map/ppermute | solution.py:349
  109.6 99.4 %collective-permute-start.3 = (bf16[128,2560]{1,0:T(8,128)(2,1)}, bf16[128,2560]{1,0:T(8,128)(2,1)}, u32[]{:S(2)}, u32[]{:S(2)}) collective-permute-start(bf16[128,2560]{1,0:T(8,128)(2,1)} %pad_maximum_fusion.16), channel_id=1, source_target_pairs={{0,8},{4,12},{8,0},{12,4},{16,24},{20,28},{24,16},{28,20},{1,9},{5... | collective-permute-start | bytes 1966088 | tf_op jit(solution)/shard_map/ppermute | solution.py:349
  238.0 28.9 %collective-permute-start.5 = (bf16[256,2560]{1,0:T(8,128)(2,1)}, bf16[256,2560]{1,0:T(8,128)(2,1)}, u32[]{:S(2)}, u32[]{:S(2)}) collective-permute-start(bf16[256,2560]{1,0:T(8,128)(2,1)} %constant_dynamic-update-slice_fusion), channel_id=1, source_target_pairs={{0,1},{1,0},{2,3},{3,2},{4,5},{5,4},{6,7},{7,6},{8,9},{9,8},{10,11... | collective-permute-start | bytes 3932168 | tf_op jit(solution)/shard_map/ppermute | solution.py:303
  238.4 33.9 %collective-permute-start.6 = (bf16[256,2560]{1,0:T(8,128)(2,1)}, bf16[256,2560]{1,0:T(8,128)(2,1)}, u32[]{:S(2)}, u32[]{:S(2)}) collective-permute-start(bf16[256,2560]{1,0:T(8,128)(2,1)} %constant_dynamic-update-slice_fusion), channel_id=1, source_target_pairs={{0,2},{1,3},{2,0},{3,1},{4,6},{5,7},{6,4},{7,5},{8,10},{9,11},{10,... | collective-permute-start | bytes 3932168 | tf_op jit(solution)/shard_map/ppermute | solution.py:303
  240.8 89.7 %collective-permute-start.9 = (bf16[1,800,640]{2,1,0:T(8,128)(2,1)}, bf16[1,800,640]{2,1,0:T(8,128)(2,1)}, u32[]{:S(2)}, u32[]{:S(2)}) collective-permute-start(bf16[1,800,640]{2,1,0:T(8,128)(2,1)} %get-tuple-element.95), channel_id=1, source_target_pairs={{0,16},{4,20},{8,24},{12,28},{16,0},{20,4},{24,8},{28,12},{1,17},{... | collective-permute-start | bytes 3072008 | tf_op jit(solution)/shard_map/ppermute | solution.py:349
  240.8 89.7 %collective-permute-start.8 = (bf16[1,800,640]{2,1,0:T(8,128)(2,1)}, bf16[1,800,640]{2,1,0:T(8,128)(2,1)}, u32[]{:S(2)}, u32[]{:S(2)}) collective-permute-start(bf16[1,800,640]{2,1,0:T(8,128)(2,1)} %get-tuple-element.93), channel_id=1, source_target_pairs={{0,16},{4,20},{8,24},{12,28},{16,0},{20,4},{24,8},{28,12},{1,17},{... | collective-permute-start | bytes 3072008 | tf_op jit(solution)/shard_map/ppermute | solution.py:349
  243.7 47.6 %collective-permute-start.4 = (bf16[2,800,640]{2,1,0:T(8,128)(2,1)S(1)}, bf16[2,800,640]{2,1,0:T(8,128)(2,1)}, u32[]{:S(2)}, u32[]{:S(2)}) collective-permute-start(bf16[2,800,640]{2,1,0:T(8,128)(2,1)S(1)} %pad_maximum_fusion.4.refs_4_.refs_8_), channel_id=1, source_target_pairs={{0,4},{4,0},{8,12},{12,8},{16,20},{20,16},{24,28},{28,24},{1,5},{5... | collective-permute-start | bytes 6144008 | tf_op jit(solution)/shard_map/ppermute | solution.py:349
  266.9 98.2 %collective-permute-start.10 = (bf16[1,800,640]{2,1,0:T(8,128)(2,1)}, bf16[1,800,640]{2,1,0:T(8,128)(2,1)}, u32[]{:S(2)}, u32[]{:S(2)}) collective-permute-start(bf16[1,800,640]{2,1,0:T(8,128)(2,1)} %collective-permute-done.1.refs_2_), channel_id=1, source_target_pairs={{0,4},{4,0},{8,12},{12,8},{16,20},{20,16},{24,28},{28,24},{1,5},{5... | collective-permute-start | bytes 3072008 | tf_op jit(solution)/shard_map/ppermute | solution.py:349
  272.3 19.1 %collective-permute-start.7 = (bf16[256,2560]{1,0:T(8,128)(2,1)}, bf16[256,2560]{1,0:T(8,128)(2,1)S(1)}, u32[]{:S(2)}, u32[]{:S(2)}) collective-permute-start(bf16[256,2560]{1,0:T(8,128)(2,1)} %collective-permute-done.6), channel_id=1, source_target_pairs={{0,1},{1,0},{2,3},{3,2},{4,5},{5,4},{6,7},{7,6},{8,9},{9,8},{10,11... | collective-permute-start | bytes 3932168 | tf_op jit(solution)/shard_map/ppermute | solution.py:303
  330.7 71.4 %collective-permute-start.12 = (bf16[1,800,640]{2,1,0:T(8,128)(2,1)}, bf16[1,800,640]{2,1,0:T(8,128)(2,1)}, u32[]{:S(2)}, u32[]{:S(2)}) collective-permute-start(bf16[1,800,640]{2,1,0:T(8,128)(2,1)} %collective-permute-done.9.refs_10_), channel_id=1, source_target_pairs={{0,4},{4,0},{8,12},{12,8},{16,20},{20,16},{24,28},{28,24},{1,5},{5... | collective-permute-start | bytes 3072008 | tf_op jit(solution)/shard_map/ppermute | solution.py:349
  331.3 46.3 %collective-permute-start.11 = (bf16[1,800,640]{2,1,0:T(8,128)(2,1)}, bf16[1,800,640]{2,1,0:T(8,128)(2,1)}, u32[]{:S(2)}, u32[]{:S(2)}) collective-permute-start(bf16[1,800,640]{2,1,0:T(8,128)(2,1)} %collective-permute-done.8.refs_6_), channel_id=1, source_target_pairs={{0,4},{4,0},{8,12},{12,8},{16,20},{20,16},{24,28},{28,24},{1,5},{5... | collective-permute-start | bytes 3072008 | tf_op jit(solution)/shard_map/ppermute | solution.py:349
  439.4 53.1 %collective-permute-start.14 = (bf16[512,2560]{1,0:T(8,128)(2,1)}, bf16[512,2560]{1,0:T(8,128)(2,1)}, u32[]{:S(2)}, u32[]{:S(2)}) collective-permute-start(bf16[512,2560]{1,0:T(8,128)(2,1)} %pad_maximum_fusion.2), channel_id=1, source_target_pairs={{0,1},{1,0},{2,3},{3,2},{4,5},{5,4},{6,7},{7,6},{8,9},{9,8},{10,11... | collective-permute-start | bytes 7864328 | tf_op jit(solution)/shard_map/ppermute | solution.py:303
  439.4 53.1 %collective-permute-start.13 = (bf16[800,1280]{1,0:T(8,128)(2,1)}, bf16[800,1280]{1,0:T(8,128)(2,1)}, u32[]{:S(2)}, u32[]{:S(2)}) collective-permute-start(bf16[800,1280]{1,0:T(8,128)(2,1)} %convolution_convert_fusion.9), channel_id=1, source_target_pairs={{0,4},{4,0},{8,12},{12,8},{16,20},{20,16},{24,28},{28,24},{1,5},{5... | collective-permute-start | bytes 6144008 | tf_op jit(solution)/shard_map/ppermute | solution.py:349
  476.8 54.2 %collective-permute-start.16 = (bf16[800,1280]{1,0:T(8,128)(2,1)}, bf16[800,1280]{1,0:T(8,128)(2,1)}, u32[]{:S(2)}, u32[]{:S(2)}) collective-permute-start(bf16[800,1280]{1,0:T(8,128)(2,1)} %convolution_convert_fusion.8), channel_id=1, source_target_pairs={{0,4},{4,0},{8,12},{12,8},{16,20},{20,16},{24,28},{28,24},{1,5},{5... | collective-permute-start | bytes 6144008 | tf_op jit(solution)/shard_map/ppermute | solution.py:349
  517.7 109.3 %collective-permute-start.19 = (bf16[256,2560]{1,0:T(8,128)(2,1)}, bf16[256,2560]{1,0:T(8,128)(2,1)}, u32[]{:S(2)}, u32[]{:S(2)}) collective-permute-start(bf16[256,2560]{1,0:T(8,128)(2,1)} %pad_maximum_fusion.9), channel_id=1, source_target_pairs={{0,2},{1,3},{2,0},{3,1},{4,6},{5,7},{6,4},{7,5},{8,10},{9,11},{10,... | collective-permute-start | bytes 3932168 | tf_op jit(solution)/shard_map/ppermute | solution.py:303
  519.4 107.6 %collective-permute-start.18 = (bf16[800,1280]{1,0:T(8,128)(2,1)}, bf16[800,1280]{1,0:T(8,128)(2,1)}, u32[]{:S(2)}, u32[]{:S(2)}) collective-permute-start(bf16[800,1280]{1,0:T(8,128)(2,1)} %convolution_convert_fusion.7), channel_id=1, source_target_pairs={{0,4},{4,0},{8,12},{12,8},{16,20},{20,16},{24,28},{28,24},{1,5},{5... | collective-permute-start | bytes 6144008 | tf_op jit(solution)/shard_map/ppermute | solution.py:349
  536.3 68.8 %collective-permute-start.17 = (bf16[800,640]{1,0:T(8,128)(2,1)}, bf16[800,640]{1,0:T(8,128)(2,1)}, u32[]{:S(2)}, u32[]{:S(2)}) collective-permute-start(bf16[800,640]{1,0:T(8,128)(2,1)} %split.682), channel_id=1, source_target_pairs={{0,16},{4,20},{8,24},{12,28},{16,0},{20,4},{24,8},{28,12},{1,17},{... | collective-permute-start | bytes 3072008 | tf_op jit(solution)/shard_map/ppermute | solution.py:349
  544.3 82.7 %collective-permute-start.15 = (bf16[800,640]{1,0:T(8,128)(2,1)}, bf16[800,640]{1,0:T(8,128)(2,1)}, u32[]{:S(2)}, u32[]{:S(2)}) collective-permute-start(bf16[800,640]{1,0:T(8,128)(2,1)} %split.683), channel_id=1, source_target_pairs={{0,16},{4,20},{8,24},{12,28},{16,0},{20,4},{24,8},{28,12},{1,17},{... | collective-permute-start | bytes 3072008 | tf_op jit(solution)/shard_map/ppermute | solution.py:349
  632.4 47.4 %collective-permute-start.20 = (bf16[800,640]{1,0:T(8,128)(2,1)}, bf16[800,640]{1,0:T(8,128)(2,1)}, u32[]{:S(2)}, u32[]{:S(2)}) collective-permute-start(bf16[800,640]{1,0:T(8,128)(2,1)} %split.681), channel_id=1, source_target_pairs={{0,16},{4,20},{8,24},{12,28},{16,0},{20,4},{24,8},{28,12},{1,17},{... | collective-permute-start | bytes 3072008 | tf_op jit(solution)/shard_map/ppermute | solution.py:349
  637.6 31.6 %collective-permute-start.25 = (bf16[128,2560]{1,0:T(8,128)(2,1)}, bf16[128,2560]{1,0:T(8,128)(2,1)}, u32[]{:S(2)}, u32[]{:S(2)}) collective-permute-start(bf16[128,2560]{1,0:T(8,128)(2,1)} %add_convert_fusion), channel_id=1, source_target_pairs={{0,8},{4,12},{8,0},{12,4},{16,24},{20,28},{24,16},{28,20},{1,9},{5... | collective-permute-start | bytes 1966088 | tf_op jit(solution)/shard_map/ppermute | solution.py:349
  690.1 21.2 %collective-permute-start.24 = (f32[288,128]{1,0:T(8,128)S(1)}, f32[288,128]{1,0:T(8,128)}, u32[]{:S(2)}, u32[]{:S(2)}) collective-permute-start(f32[288,128]{1,0:T(8,128)S(1)} %get-tuple-element.257), channel_id=1, source_target_pairs={{16,0},{20,4},{24,8},{28,12},{17,1},{21,5},{25,9},{29,13},{18,2},{... | collective-permute-start | bytes 442376 | tf_op jit(solution)/shard_map/ppermute | solution.py:299
  (112 other events, 1248.4 us)
Sparse Core Ops, SparseCore 0:
  112.2 95.4 all-gather.1

commit v7 on v6

--- a/solution.py
+++ b/solution.py
@@ -1287,12 +1287,13 @@
     own_cosine, own_sine = pick(quarters(cosine, 1)), pick(quarters(sine, 1))
     back_front, back_behind = rotate(back_key[KR : KR + half], back_key[KR + half :], own_cosine, -own_sine)
     back_latents = jnp.concatenate([back_query_latent, back_latent, back_front, back_behind], axis=0).astype(bf)
-    back_latents = spread(back_latents, COLS, 3, 9, lanes=True)
+    slope_down, away = slope_down.halves()
+    back_latents, came = spread(back_latents, COLS, 3, 9, lanes=True, cargo=away)
+    slope_down = in_pair_order(slope_down, came, 0)
     back_slice = lax.dynamic_slice_in_dim(back_latents, column * slice_width, slice_width, 0)
-    halves = [flow.halves() for flow in (slope_down, slope_gate)]
-    away = jnp.stack([gone for _, gone in halves])
+    slope_gate, away = slope_gate.halves()
     back_first, came = fold(dot(back_slice, wide_down, ((0,), (1,))), COLS, 8, 10, cargo=away)
-    slope_down, slope_gate = (in_pair_order(mine, got, 0) for (mine, _), got in zip(halves, came))
+    slope_gate = in_pair_order(slope_gate, came, 0)
     back_norm_first, gain_first_part = norm_back(own_residual, inverse_of(own_residual, 1), gain_one, back_first, 1)
     own_back = back_middle + back_norm_first
 
@@ -1324,7 +1325,7 @@
     exact = functools.partial(
         lax.dot_general,
         dimension_numbers=(((1,), (1,)), ((), ())),
-        precision=lax.Precision.HIGHEST,
+        precision=lax.Precision.HIGH,
         preferred_element_type=f32,
     )
     return (

time: 929 us -> 921 us (level)
    pallas_call x4, Pallas kernels: 103 us -> 90.9 us  [fold(): pl.pallas_call(functools.partial(fold_kernel, dims, parts, lanes, relativ...]
    unnamed x249 -> x241, local copies, waits for them, and re-layouts: 43.2 us -> 43.2 us
  transfers between devices with their start and end apart: 27 -> 27, of which waited for: 12 -> 13; matrix products, arithmetic and copies ran while one was open for 20% -> 20% of each run, Pallas kernels for 22% -> 22%
where the time goes in v7:
time: 921 us; the launch traced here: 914 us
  Pallas kernels  445 us (48%)
  waiting for transfers between devices  136 us (15%)
  local copies, waits for them, and re-layouts  107 us (12%)
  other arithmetic  89.5 us (10%)
  matrix products  88.4 us (10%)
  starting transfers between devices  31.1 us (3%)
  between operations  16.6 us (2%)
    ppermute x17, waiting for transfers between devices, swap_row(): lax.ppermute(value, 'row', [(r, r ^ mask) for r in range(lax.axis_size('r...  117 us
    pallas_call x1, Pallas kernels, ring_scatter(): pl.pallas_call(functools.partial(ring_scatter_kernel, rows, n, extra), ou...  93.7 us
    pallas_call x4, Pallas kernels, fold(): pl.pallas_call(functools.partial(fold_kernel, dims, parts, lanes, relativ...  90.9 us
    pallas_call x5, Pallas kernels, spread(): pl.pallas_call(functools.partial(spread_kernel, dims, parts, lanes, relat...  90.7 us
    dot_general x24, matrix products, dot(): lax.dot_general(left, right, (dims, ((), ())), preferred_element_type=f32)  83.3 us
    pallas_call x1, Pallas kernels, ring_gather(): pl.pallas_call(functools.partial(ring_gather_kernel, rows, n), out_shape=...  71.6 us
    unnamed x241, local copies, waits for them, and re-layouts  43.2 us
    pallas_call x1, Pallas kernels, ffn_back(): pl.pallas_call(functools.partial(ffn_back_kernel, n), grid=(tokens // TOK...  33.8 us
  transfers between devices with their start and end apart: 27, of which 13 were waited for; matrix products, arithmetic and copies ran while one was open for 20% of the time, Pallas kernels for 22%

profile of v7, /device:TPU:0, one launch (start us, length us, event | category | flops | bytes accessed | tf_op | source)
XLA Modules:
  0.0 913.7 jit_solution(1615036582056847852)
XLA Ops:
  27.1 71.6 %ring_gather.1 = (bf16[8,2,160,384]{3,2,1,0:T(8,128)(2,1)}, bf16[8,2,48,1024]{3,2,1,0:T(8,128)(2,1)}, bf16[8,2,16,1280]{3,2,1,0:T(8,128)(2,1)}, bf16[512,2560]{1...) custom-call(bf16[2,160,384]{2,1,0:T(8,128)(2,1)} %bitcast.120, bf16[2,48,1024]{2,1,0:T(8,128)(2,1)} %bitcast.130, ...), custom_call_target="tpu_custom_call" | custom-call | tf_op jit(solution)/shard_map/ring_gather/pallas_call | solution.py:151
  120.6 18.2 %spread3.1 = f32[4,264,512]{2,1,0:T(8,128)} custom-call(f32[264,512]{1,0:T(8,128)} %fusion.32.refs_0_), custom_call_target="tpu_custom_call" | custom-call | tf_op jit(solution)/shard_map/spread3/pallas_call | solution.py:626
  183.8 25.1 %collective-permute-done.3 = bf16[128,2560]{1,0:T(8,128)(2,1)} collective-permute-done((bf16[128,2560]{1,0:T(8,128)(2,1)}, bf16[128,2560]{1,0:T(8,128)(2,1)}, u32[]{:S(2)}, u32[]{:S(2)}) %collective-permute-start.3) | collective-permute-done | bytes 655392 | tf_op jit(solution)/shard_map/ppermute | solution.py:349
  209.0 15.8 %gather_behind.1 = bf16[288,2560]{1,0:T(8,128)(2,1)} custom-call(bf16[288,512]{1,0:T(8,128)(2,1)} %pad_maximum_fusion.19.key_ref), custom_call_target="tpu_custom_call" | custom-call | tf_op jit(solution)/shard_map/gather_behind/pallas_call | solution.py:692
  250.2 10.8 %attend.1 = (bf16[640,512]{1,0:T(8,128)(2,1)}, f32[640,512]{1,0:T(8,128)}, f32[5,2,512]{2,1,0:T(2,128)}) custom-call(s32[1]{0:T(128)} %bitcast.11.first_ref, bf16[1024,512]{1,0:T(8,128)(2,1)} %copy.116.qn_ref.qr_ref, bf16[1024,512]{1,0:T(8,128)(2,1)} %copy.116.qn_ref.qr_ref, bf16[2560,640]{1,0:T(8,128)(2,1)} %convolution_convert_fusion.4.k_ref, ...), custom_call_target="tpu_custom_call" | custom-call | tf_op jit(solution)/shard_map/attend/pallas_call | solution.py:927
  274.4 16.8 %collective-permute-done.4.refs_5_.refs_9_ = bf16[2,800,640]{2,1,0:T(8,128)(2,1)} collective-permute-done((bf16[2,800,640]{2,1,0:T(8,128)(2,1)S(1)}, bf16[2,800,640]{2,1,0:T(8,128)(2,1)}, u32[]{:S(2)}, u32[]{:S(2)}) %collective-permute-start.4) | collective-permute-done | bytes 2048032 | tf_op jit(solution)/shard_map/ppermute | solution.py:349
  305.2 20.5 %fold4.1 = f32[128,2560]{1,0:T(8,128)} custom-call(bf16[4,128,2560]{2,1,0:T(8,128)(2,1)} %bitcast.110), custom_call_target="tpu_custom_call" | custom-call | tf_op jit(solution)/shard_map/fold4/pallas_call | solution.py:771
  334.6 26.0 %spread5.1 = bf16[8,128,2560]{2,1,0:T(8,128)(2,1)} custom-call(bf16[128,2560]{1,0:T(8,128)(2,1)} %pad_maximum_fusion.16.refs_0_), custom_call_target="tpu_custom_call" | custom-call | tf_op jit(solution)/shard_map/spread5/pallas_call | solution.py:626
  365.1 12.4 %collective-permute-done.11.refs_7_ = bf16[1,800,640]{2,1,0:T(8,128)(2,1)} collective-permute-done((bf16[1,800,640]{2,1,0:T(8,128)(2,1)}, bf16[1,800,640]{2,1,0:T(8,128)(2,1)}, u32[]{:S(2)}, u32[]{:S(2)}) %collective-permute-start.11) | collective-permute-done | bytes 1024032 | tf_op jit(solution)/shard_map/ppermute | solution.py:349
  377.5 19.0 %ffn.1 = (f32[1024,800]{1,0:T(8,128)}, f32[1024,800]{1,0:T(8,128)}, bf16[1024,800]{1,0:T(8,128)(2,1)}) custom-call(bf16[1024,2560]{1,0:T(8,128)(2,1)} %bitcast.83, bf16[1,800,640]{2,1,0:T(8,128)(2,1)} %pad_maximum_fusion.12.refs_0_, bf16[1,800,640]{2,1,0:T(8,128)(2,1)} %collective-permute-done.refs_1_, bf16[1,800,640]{2,1,0:T(8,128)(2,1)} %collective-permute-done.1.refs_2_, ...), custom_call_target="tpu_custom_call" | custom-call | tf_op jit(solution)/shard_map/ffn/pallas_call | solution.py:1078
  402.0 33.8 %ffn_back.1 = (bf16[1024,800]{1,0:T(8,128)(2,1)}, bf16[1024,800]{1,0:T(8,128)(2,1)}, bf16[1024,2560]{1,0:T(8,128)(2,1)}, bf16[1024,2560]{1,0:T(8,128)(2,1)}) custom-call(bf16[1024,2560]{1,0:T(8,128)(2,1)} %copy-done.2, f32[1024,800]{1,0:T(8,128)} %get-tuple-element.103.gate_ref, f32[1024,800]{1,0:T(8,128)} %get-tuple-element.104.up_ref, ...), custom_call_target="tpu_custom_call" | custom-call | tf_op jit(solution)/shard_map/ffn_back/pallas_call | solution.py:1111
  443.7 30.7 %fold6.1 = f32[128,2560]{1,0:T(8,128)} custom-call(bf16[8,128,2560]{2,1,0:T(8,128)(2,1)} %bitcast.99), custom_call_target="tpu_custom_call" | custom-call | tf_op jit(solution)/shard_map/fold6/pallas_call | solution.py:771
  492.4 21.9 %spread7.1 = bf16[4,128,2560]{2,1,0:T(8,128)(2,1)} custom-call(bf16[128,2560]{1,0:T(8,128)(2,1)} %get-tuple-element.112.refs_0_), custom_call_target="tpu_custom_call" | custom-call | tf_op jit(solution)/shard_map/spread7/pallas_call | solution.py:626
  522.9 8.0 collective-permute-done.16
  547.5 18.9 %attend_back.1 = (f32[640,512]{1,0:T(8,128)}, f32[384,512]{1,0:T(8,128)}, bf16[2560,640]{1,0:T(8,128)(2,1)}, bf16[2560,640]{1,0:T(8,128)(2,1)}, f32[2560,128]{1,0:T(8,128)}) custom-call(s32[1]{0:T(128)} %bitcast.11.first_ref, bf16[1024,512]{1,0:T(8,128)(2,1)} %copy.116.qn_ref.qr_ref, bf16[1024,512]{1,0:T(8,128)(2,1)} %copy.116.qn_ref.qr_ref, ...), custom_call_target="tpu_custom_call" | custom-call | tf_op jit(solution)/shard_map/attend_back/pallas_call | solution.py:1032
  589.1 15.9 %collective-permute-done.17 = bf16[800,640]{1,0:T(8,128)(2,1)} collective-permute-done((bf16[800,640]{1,0:T(8,128)(2,1)}, bf16[800,640]{1,0:T(8,128)(2,1)}, u32[]{:S(2)}, u32[]{:S(2)}) %collective-permute-start.17) | collective-permute-done | bytes 1024032 | tf_op jit(solution)/shard_map/ppermute | solution.py:349
  605.0 21.9 %collective-permute-done.15 = bf16[800,640]{1,0:T(8,128)(2,1)} collective-permute-done((bf16[800,640]{1,0:T(8,128)(2,1)}, bf16[800,640]{1,0:T(8,128)(2,1)}, u32[]{:S(2)}, u32[]{:S(2)}) %collective-permute-start.15) | collective-permute-done | bytes 1024032 | tf_op jit(solution)/shard_map/ppermute | solution.py:349
  639.4 18.6 %fold8.1 = f32[2208,128]{1,0:T(8,128)} custom-call(bf16[2208,512]{1,0:T(8,128)(2,1)} %copy-done.40), custom_call_target="tpu_custom_call" | custom-call | tf_op jit(solution)/shard_map/fold8/pallas_call | solution.py:771
  660.3 8.8 collective-permute-done.25
  701.8 10.4 %collective-permute-done.24 = f32[288,128]{1,0:T(8,128)} collective-permute-done((f32[288,128]{1,0:T(8,128)S(1)}, f32[288,128]{1,0:T(8,128)}, u32[]{:S(2)}, u32[]{:S(2)}) %collective-permute-start.24) | collective-permute-done | bytes 147488 | tf_op jit(solution)/shard_map/ppermute | solution.py:299
  714.6 15.1 %spread9.1 = (bf16[1056,512]{1,0:T(8,128)(2,1)}, bf16[800,320]{1,0:T(8,128)(2,1)}) custom-call(bf16[1056,128]{1,0:T(8,128)(2,1)} %pad_maximum_fusion.20.refs_0_, bf16[800,320]{1,0:T(8,128)(2,1)} %broadcast_select_fusion.15.refs_1_), custom_call_target="tpu_custom_call" | custom-call | tf_op jit(solution)/shard_map/spread9/pallas_call | solution.py:626
  736.1 21.0 %fold10.1 = (f32[128,2560]{1,0:T(8,128)}, bf16[800,320]{1,0:T(8,128)(2,1)}) custom-call(bf16[4,128,2560]{2,1,0:T(8,128)(2,1)} %bitcast.109, bf16[800,320]{1,0:T(8,128)(2,1)} %broadcast_select_fusion.14.refs_1_), custom_call_target="tpu_custom_call" | custom-call | tf_op jit(solution)/shard_map/fold10/pallas_call | solution.py:771
  768.7 93.7 %ring_scatter.1 = (f32[2,160,640]{2,1,0:T(8,128)}, f32[2,48,1024]{2,1,0:T(8,128)}, f32[2,16,1280]{2,1,0:T(8,128)}, f32[2,160,384]{2,1,0:T(8,128)}, f32[2,3,128]{...) custom-call(bf16[8,2,160,640]{3,2,1,0:T(8,128)(2,1)} %bitcast.104, ...), custom_call_target="tpu_custom_call" | custom-call | tf_op jit(solution)/shard_map/ring_scatter/pallas_call | solution.py:277
  865.2 9.5 %spread11.1 = bf16[320,1536]{1,0:T(8,128)(2,1)} custom-call(bf16[320,384]{1,0:T(8,128)(2,1)} %fusion.62.refs_0_), custom_call_target="tpu_custom_call" | custom-call | tf_op jit(solution)/shard_map/spread11/pallas_call | solution.py:626
  (491 shorter events, 332.7 us)
Async XLA Ops:
  7.2 292.4 %all-gather.2.cloned.1.call-start = ((), (), s32[]{:S(2)}) async-start(), calls=%async_computation | async-start | bytes 3686400 | tf_op jit(solution)/shard_map/all_gather | solution.py:1165
  101.4 107.6 %collective-permute-start = (bf16[1,800,640]{2,1,0:T(8,128)(2,1)}, bf16[1,800,640]{2,1,0:T(8,128)(2,1)}, u32[]{:S(2)}, u32[]{:S(2)}) collective-permute-start(bf16[1,800,640]{2,1,0:T(8,128)(2,1)} %pad_maximum_fusion.12.refs_0_), channel_id=1, source_target_pairs={{0,4},{4,0},{8,12},{12,8},{16,20},{20,16},{24,28},{28,24},{1,5},{5... | collective-permute-start | bytes 3072008 | tf_op jit(solution)/shard_map/ppermute | solution.py:349
  102.9 106.1 %collective-permute-start.1 = (bf16[1,800,640]{2,1,0:T(8,128)(2,1)}, bf16[1,800,640]{2,1,0:T(8,128)(2,1)}, u32[]{:S(2)}, u32[]{:S(2)}) collective-permute-start(bf16[1,800,640]{2,1,0:T(8,128)(2,1)} %pad_maximum_fusion.12.refs_0_), channel_id=1, source_target_pairs={{0,16},{4,20},{8,24},{12,28},{16,0},{20,4},{24,8},{28,12},{1,17},{... | collective-permute-start | bytes 3072008 | tf_op jit(solution)/shard_map/ppermute | solution.py:349
  107.3 71.4 %collective-permute-start.2 = (bf16[2,800,320]{1,2,0:T(8,128)(2,1)}, bf16[2,800,320]{1,2,0:T(8,128)(2,1)}, u32[]{:S(2)}, u32[]{:S(2)}) collective-permute-start(bf16[2,800,320]{1,2,0:T(8,128)(2,1)} %copy.115), channel_id=1, source_target_pairs={{0,8},{4,12},{8,0},{12,4},{16,24},{20,28},{24,16},{28,20},{1,9},{5... | collective-permute-start | bytes 3072008 | tf_op jit(solution)/shard_map/ppermute | solution.py:349
  109.6 99.4 %collective-permute-start.3 = (bf16[128,2560]{1,0:T(8,128)(2,1)}, bf16[128,2560]{1,0:T(8,128)(2,1)}, u32[]{:S(2)}, u32[]{:S(2)}) collective-permute-start(bf16[128,2560]{1,0:T(8,128)(2,1)} %pad_maximum_fusion.15), channel_id=1, source_target_pairs={{0,8},{4,12},{8,0},{12,4},{16,24},{20,28},{24,16},{28,20},{1,9},{5... | collective-permute-start | bytes 1966088 | tf_op jit(solution)/shard_map/ppermute | solution.py:349
  237.9 28.9 %collective-permute-start.5 = (bf16[256,2560]{1,0:T(8,128)(2,1)}, bf16[256,2560]{1,0:T(8,128)(2,1)}, u32[]{:S(2)}, u32[]{:S(2)}) collective-permute-start(bf16[256,2560]{1,0:T(8,128)(2,1)} %constant_dynamic-update-slice_fusion), channel_id=1, source_target_pairs={{0,1},{1,0},{2,3},{3,2},{4,5},{5,4},{6,7},{7,6},{8,9},{9,8},{10,11... | collective-permute-start | bytes 3932168 | tf_op jit(solution)/shard_map/ppermute | solution.py:303
  238.3 33.8 %collective-permute-start.6 = (bf16[256,2560]{1,0:T(8,128)(2,1)}, bf16[256,2560]{1,0:T(8,128)(2,1)}, u32[]{:S(2)}, u32[]{:S(2)}) collective-permute-start(bf16[256,2560]{1,0:T(8,128)(2,1)} %constant_dynamic-update-slice_fusion), channel_id=1, source_target_pairs={{0,2},{1,3},{2,0},{3,1},{4,6},{5,7},{6,4},{7,5},{8,10},{9,11},{10,... | collective-permute-start | bytes 3932168 | tf_op jit(solution)/shard_map/ppermute | solution.py:303
  240.7 89.7 %collective-permute-start.9 = (bf16[1,800,640]{2,1,0:T(8,128)(2,1)}, bf16[1,800,640]{2,1,0:T(8,128)(2,1)}, u32[]{:S(2)}, u32[]{:S(2)}) collective-permute-start(bf16[1,800,640]{2,1,0:T(8,128)(2,1)} %get-tuple-element.97), channel_id=1, source_target_pairs={{0,16},{4,20},{8,24},{12,28},{16,0},{20,4},{24,8},{28,12},{1,17},{... | collective-permute-start | bytes 3072008 | tf_op jit(solution)/shard_map/ppermute | solution.py:349
  240.7 89.7 %collective-permute-start.8 = (bf16[1,800,640]{2,1,0:T(8,128)(2,1)}, bf16[1,800,640]{2,1,0:T(8,128)(2,1)}, u32[]{:S(2)}, u32[]{:S(2)}) collective-permute-start(bf16[1,800,640]{2,1,0:T(8,128)(2,1)} %get-tuple-element.95), channel_id=1, source_target_pairs={{0,16},{4,20},{8,24},{12,28},{16,0},{20,4},{24,8},{28,12},{1,17},{... | collective-permute-start | bytes 3072008 | tf_op jit(solution)/shard_map/ppermute | solution.py:349
  243.6 47.6 %collective-permute-start.4 = (bf16[2,800,640]{2,1,0:T(8,128)(2,1)S(1)}, bf16[2,800,640]{2,1,0:T(8,128)(2,1)}, u32[]{:S(2)}, u32[]{:S(2)}) collective-permute-start(bf16[2,800,640]{2,1,0:T(8,128)(2,1)S(1)} %pad_maximum_fusion.4.refs_4_.refs_8_), channel_id=1, source_target_pairs={{0,4},{4,0},{8,12},{12,8},{16,20},{20,16},{24,28},{28,24},{1,5},{5... | collective-permute-start | bytes 6144008 | tf_op jit(solution)/shard_map/ppermute | solution.py:349
  266.8 98.3 %collective-permute-start.10 = (bf16[1,800,640]{2,1,0:T(8,128)(2,1)}, bf16[1,800,640]{2,1,0:T(8,128)(2,1)}, u32[]{:S(2)}, u32[]{:S(2)}) collective-permute-start(bf16[1,800,640]{2,1,0:T(8,128)(2,1)} %collective-permute-done.1.refs_2_), channel_id=1, source_target_pairs={{0,4},{4,0},{8,12},{12,8},{16,20},{20,16},{24,28},{28,24},{1,5},{5... | collective-permute-start | bytes 3072008 | tf_op jit(solution)/shard_map/ppermute | solution.py:349
  272.1 19.1 %collective-permute-start.7 = (bf16[256,2560]{1,0:T(8,128)(2,1)}, bf16[256,2560]{1,0:T(8,128)(2,1)S(1)}, u32[]{:S(2)}, u32[]{:S(2)}) collective-permute-start(bf16[256,2560]{1,0:T(8,128)(2,1)} %collective-permute-done.6), channel_id=1, source_target_pairs={{0,1},{1,0},{2,3},{3,2},{4,5},{5,4},{6,7},{7,6},{8,9},{9,8},{10,11... | collective-permute-start | bytes 3932168 | tf_op jit(solution)/shard_map/ppermute | solution.py:303
  330.6 71.4 %collective-permute-start.12 = (bf16[1,800,640]{2,1,0:T(8,128)(2,1)}, bf16[1,800,640]{2,1,0:T(8,128)(2,1)}, u32[]{:S(2)}, u32[]{:S(2)}) collective-permute-start(bf16[1,800,640]{2,1,0:T(8,128)(2,1)} %collective-permute-done.9.refs_10_), channel_id=1, source_target_pairs={{0,4},{4,0},{8,12},{12,8},{16,20},{20,16},{24,28},{28,24},{1,5},{5... | collective-permute-start | bytes 3072008 | tf_op jit(solution)/shard_map/ppermute | solution.py:349
  331.3 46.2 %collective-permute-start.11 = (bf16[1,800,640]{2,1,0:T(8,128)(2,1)}, bf16[1,800,640]{2,1,0:T(8,128)(2,1)}, u32[]{:S(2)}, u32[]{:S(2)}) collective-permute-start(bf16[1,800,640]{2,1,0:T(8,128)(2,1)} %collective-permute-done.8.refs_6_), channel_id=1, source_target_pairs={{0,4},{4,0},{8,12},{12,8},{16,20},{20,16},{24,28},{28,24},{1,5},{5... | collective-permute-start | bytes 3072008 | tf_op jit(solution)/shard_map/ppermute | solution.py:349
  439.3 53.1 %collective-permute-start.14 = (bf16[512,2560]{1,0:T(8,128)(2,1)}, bf16[512,2560]{1,0:T(8,128)(2,1)}, u32[]{:S(2)}, u32[]{:S(2)}) collective-permute-start(bf16[512,2560]{1,0:T(8,128)(2,1)} %pad_maximum_fusion.2), channel_id=1, source_target_pairs={{0,1},{1,0},{2,3},{3,2},{4,5},{5,4},{6,7},{7,6},{8,9},{9,8},{10,11... | collective-permute-start | bytes 7864328 | tf_op jit(solution)/shard_map/ppermute | solution.py:303
  439.3 53.1 %collective-permute-start.13 = (bf16[800,1280]{1,0:T(8,128)(2,1)}, bf16[800,1280]{1,0:T(8,128)(2,1)}, u32[]{:S(2)}, u32[]{:S(2)}) collective-permute-start(bf16[800,1280]{1,0:T(8,128)(2,1)} %convolution_convert_fusion.9), channel_id=1, source_target_pairs={{0,4},{4,0},{8,12},{12,8},{16,20},{20,16},{24,28},{28,24},{1,5},{5... | collective-permute-start | bytes 6144008 | tf_op jit(solution)/shard_map/ppermute | solution.py:349
  476.6 54.2 %collective-permute-start.16 = (bf16[800,1280]{1,0:T(8,128)(2,1)}, bf16[800,1280]{1,0:T(8,128)(2,1)}, u32[]{:S(2)}, u32[]{:S(2)}) collective-permute-start(bf16[800,1280]{1,0:T(8,128)(2,1)} %convolution_convert_fusion.8), channel_id=1, source_target_pairs={{0,4},{4,0},{8,12},{12,8},{16,20},{20,16},{24,28},{28,24},{1,5},{5... | collective-permute-start | bytes 6144008 | tf_op jit(solution)/shard_map/ppermute | solution.py:349
  517.6 109.2 %collective-permute-start.19 = (bf16[256,2560]{1,0:T(8,128)(2,1)}, bf16[256,2560]{1,0:T(8,128)(2,1)}, u32[]{:S(2)}, u32[]{:S(2)}) collective-permute-start(bf16[256,2560]{1,0:T(8,128)(2,1)} %pad_maximum_fusion.9), channel_id=1, source_target_pairs={{0,2},{1,3},{2,0},{3,1},{4,6},{5,7},{6,4},{7,5},{8,10},{9,11},{10,... | collective-permute-start | bytes 3932168 | tf_op jit(solution)/shard_map/ppermute | solution.py:303
  519.3 107.5 %collective-permute-start.18 = (bf16[800,1280]{1,0:T(8,128)(2,1)}, bf16[800,1280]{1,0:T(8,128)(2,1)}, u32[]{:S(2)}, u32[]{:S(2)}) collective-permute-start(bf16[800,1280]{1,0:T(8,128)(2,1)} %convolution_convert_fusion.7), channel_id=1, source_target_pairs={{0,4},{4,0},{8,12},{12,8},{16,20},{20,16},{24,28},{28,24},{1,5},{5... | collective-permute-start | bytes 6144008 | tf_op jit(solution)/shard_map/ppermute | solution.py:349
  536.1 68.8 %collective-permute-start.17 = (bf16[800,640]{1,0:T(8,128)(2,1)}, bf16[800,640]{1,0:T(8,128)(2,1)}, u32[]{:S(2)}, u32[]{:S(2)}) collective-permute-start(bf16[800,640]{1,0:T(8,128)(2,1)} %split.682), channel_id=1, source_target_pairs={{0,16},{4,20},{8,24},{12,28},{16,0},{20,4},{24,8},{28,12},{1,17},{... | collective-permute-start | bytes 3072008 | tf_op jit(solution)/shard_map/ppermute | solution.py:349
  544.1 82.7 %collective-permute-start.15 = (bf16[800,640]{1,0:T(8,128)(2,1)}, bf16[800,640]{1,0:T(8,128)(2,1)}, u32[]{:S(2)}, u32[]{:S(2)}) collective-permute-start(bf16[800,640]{1,0:T(8,128)(2,1)} %split.683), channel_id=1, source_target_pairs={{0,16},{4,20},{8,24},{12,28},{16,0},{20,4},{24,8},{28,12},{1,17},{... | collective-permute-start | bytes 3072008 | tf_op jit(solution)/shard_map/ppermute | solution.py:349
  632.3 47.4 %collective-permute-start.20 = (bf16[800,640]{1,0:T(8,128)(2,1)}, bf16[800,640]{1,0:T(8,128)(2,1)}, u32[]{:S(2)}, u32[]{:S(2)}) collective-permute-start(bf16[800,640]{1,0:T(8,128)(2,1)} %split.681), channel_id=1, source_target_pairs={{0,16},{4,20},{8,24},{12,28},{16,0},{20,4},{24,8},{28,12},{1,17},{... | collective-permute-start | bytes 3072008 | tf_op jit(solution)/shard_map/ppermute | solution.py:349
  637.4 31.6 %collective-permute-start.25 = (bf16[128,2560]{1,0:T(8,128)(2,1)}, bf16[128,2560]{1,0:T(8,128)(2,1)}, u32[]{:S(2)}, u32[]{:S(2)}) collective-permute-start(bf16[128,2560]{1,0:T(8,128)(2,1)} %add_convert_fusion), channel_id=1, source_target_pairs={{0,8},{4,12},{8,0},{12,4},{16,24},{20,28},{24,16},{28,20},{1,9},{5... | collective-permute-start | bytes 1966088 | tf_op jit(solution)/shard_map/ppermute | solution.py:349
  690.9 21.3 %collective-permute-start.24 = (f32[288,128]{1,0:T(8,128)S(1)}, f32[288,128]{1,0:T(8,128)}, u32[]{:S(2)}, u32[]{:S(2)}) collective-permute-start(f32[288,128]{1,0:T(8,128)S(1)} %get-tuple-element.259), channel_id=1, source_target_pairs={{16,0},{20,4},{24,8},{28,12},{17,1},{21,5},{25,9},{29,13},{18,2},{... | collective-permute-start | bytes 442376 | tf_op jit(solution)/shard_map/ppermute | solution.py:299
  (108 other events, 1206.7 us)
Sparse Core Ops, SparseCore 0:
  112.1 95.4 all-gather.1
